TPU v7x, 128 devices: a whole 4x4x4 slice. The times are simulated.
128 devices in a mesh: rows: 8 (over y, x_hi), cols: 16 (over x_lo, z, core).
Axes of the slice: x: 4 (x_hi: 2, x_lo: 2; x = x_hi * 2 + x_lo), y: 4, z: 4, core: 2. Of those that a mesh axis runs over, the one named last changes fastest.
Arguments:
- object_field: float32 [2, 2048, 4096], P(None, 'rows', 'cols'), may hold values from -6 to 6
- probe: float32 [2, 256, 256], replicated, may hold values from -6 to 6
- positions: int32 [8, 16, 6, 2], P('rows', 'cols'), may hold values from 0 to 256
- counts: int32 [8, 16], P('rows', 'cols'), may hold values from 2 to 6
- intensity: int32 [8, 16, 6, 256, 256], P('rows', 'cols'), may hold values from 0 to 4000
Outputs:
- updated_field: float32 [2, 2048, 4096], P(None, 'rows', 'cols')
Inputs may be any that keep to these rules, and one draw needn't show every extreme that they name: Only the first counts[a, b] entries of tile (a, b) in positions and intensity are used.
All inputs are finite; a program needn't handle non-finite values.
Results may differ from a plain program's by a relative error of at most 0.00029.
Values sent between devices are 32-bit elements; how exact they have to be, the bound alone decides.
No kernel may reach another device: no remote copies, remote signals or barrier semaphores. Data moves between devices by JAX's collectives and lax.ppermute only.
A program may use at most 64 MiB of HBM per device.

v0:
```python
import functools

import jax
import jax.numpy as jnp
import numpy as np
from jax import lax
from jax.experimental import pallas as pl
from jax.experimental.pallas import tpu as pltpu
from jax.sharding import PartitionSpec as P

MARGIN = 128
HALF = 128
GROUP = 2


step_rate = 0.02
photon_unit = 0.001


def rotation_tables(length):
    half = length // 2
    index = np.arange(half, dtype=np.int64)
    angle = (index[:, None] * index[None, :] % half) * (2.0 * np.pi / half)
    norm = 1.0 / np.sqrt(length)
    cosine = np.cos(angle) * norm
    sine = np.sin(angle) * norm
    mixed = np.block([[cosine, -sine], [sine, cosine]]).astype(np.float32)
    turn = index * (2.0 * np.pi / length)
    twiddle = np.stack([np.cos(turn), -np.sin(turn)]).astype(np.float32)
    return mixed, twiddle


def split_order(length):
    half = length // 2
    order = np.concatenate([np.arange(half) * 2, np.arange(half) * 2 + 1])
    return (np.arange(length)[:, None] == order[None, :]).astype(np.float32)


VMEM = pl.BlockSpec(memory_space=pltpu.VMEM)
SMEM = pl.BlockSpec(memory_space=pltpu.SMEM)
ANY = pl.BlockSpec(memory_space=pl.ANY)


def shaped(*dims):
    return jax.ShapeDtypeStruct(dims, jnp.float32)


def whole(body, outs, scalars, arrays, scratch=(), limit=40 << 20, flops=1 << 20, unread=()):
    return pl.pallas_call(
        body,
        out_shape=outs,
        in_specs=[SMEM] * len(scalars) + [VMEM] * len(arrays) + [ANY] * len(unread),
        out_specs=tuple(VMEM for _ in outs),
        scratch_shapes=scratch,
        compiler_params=pltpu.CompilerParams(vmem_limit_bytes=limit),
        cost_estimate=pl.CostEstimate(flops=flops, bytes_accessed=8 << 20, transcendentals=0),
    )(*scalars, *arrays, *unread)


def cut_body(info, tile, edge_a, edge_b, side_a, side_b):
    last = tile.shape[1] - MARGIN
    edge_a[...] = tile[:, pl.ds(pl.multiple_of((1 - info[0]) * last, 8), MARGIN), :]
    edge_b[...] = tile[:, pl.ds(pl.multiple_of(info[0] * last, 8), MARGIN), :]
    left, right = slice(0, MARGIN), slice(last, last + MARGIN)

    @pl.when(info[1] == 1)
    def _():
        side_a[...] = tile[:, :, left]
        side_b[...] = tile[:, :, right]

    @pl.when(info[1] == 0)
    def _():
        side_a[...] = tile[:, :, right]
        side_b[...] = tile[:, :, left]


def prepare_body(positions, intensity, probe, order, earlier, measured, rolled, held, arrived):
    slots, size = intensity.shape[0], probe.shape[1]
    half = size // 2
    moves = [order[:half], order[half:]]
    copies = [
        pltpu.make_async_copy(intensity.at[:, :, pl.ds(half * block, half)], held.at[block], arrived.at[block])
        for block in range(2)
    ]
    for copy in copies:
        copy.start()

    def turn(slot, carry):
        shift = lax.rem(positions[slot, 1], size)
        for part in range(2):
            rolled[slot, part] = pltpu.roll(probe[part], shift, 1)
        return carry

    lax.fori_loop(0, slots, turn, 0)
    for copy in copies:
        copy.wait()

    def reorder(slot, carry):
        for parity in range(2):
            moved = jnp.zeros((half, size), jnp.float32)
            for block in range(2):
                counts = held[block, slot, pl.ds(parity, half, stride=2), :]
                upper = lax.shift_right_logical(counts, 8).astype(jnp.float32).astype(jnp.bfloat16)
                lower = lax.bitwise_and(counts, 255).astype(jnp.float32).astype(jnp.bfloat16)
                high = jnp.dot(upper, moves[block], preferred_element_type=jnp.float32)
                low = jnp.dot(lower, moves[block], preferred_element_type=jnp.float32)
                moved = moved + (256.0 * high + low)
            measured[slot, parity] = moved * photon_unit
        return carry

    lax.fori_loop(0, slots, reorder, 0)


def prepare(positions, intensity, probe, order, earlier):
    slots, size = intensity.shape[0], probe.shape[1]
    half = size // 2
    return pl.pallas_call(
        prepare_body,
        out_shape=(shaped(slots, 2, half, size), shaped(slots, 2, size, size)),
        in_specs=[SMEM, ANY, VMEM, VMEM, ANY],
        out_specs=(VMEM, VMEM),
        scratch_shapes=[pltpu.VMEM((2, slots, size, half), jnp.int32), pltpu.SemaphoreType.DMA((2,))],
        compiler_params=pltpu.CompilerParams(vmem_limit_bytes=24 << 20),
        cost_estimate=pl.CostEstimate(flops=slots * 2**27, bytes_accessed=8 << 20, transcendentals=0),
    )(positions, intensity, probe, order, earlier)


def halves(value):
    upper = value.astype(jnp.bfloat16)
    lower = (value - upper.astype(jnp.float32)).astype(jnp.bfloat16)
    return upper, lower


def times_table(value, table):
    upper, lower = halves(value)
    packed = jnp.concatenate([upper, lower, upper], axis=1)
    return jnp.dot(packed, table, preferred_element_type=jnp.float32)


def table_times(table, value):
    upper, lower = halves(value)
    packed = jnp.concatenate([upper, lower, upper], axis=0)
    return jnp.dot(table, packed, preferred_element_type=jnp.float32)


def wide(left, right):
    return jnp.concatenate([left, right], axis=1)


def tall(upper, lower):
    return jnp.concatenate([upper, lower], axis=0)


def places(odd_col):
    return 3 - 3 * odd_col, 2 - odd_col, 1 + odd_col, 3 * odd_col


def gradient_body(
    first, info, positions, counts, ext_r, ext_i, ext_b, *refs
):
    if first:
        near_edge, near_corner, far_edge, far_corner, *refs = refs
    else:
        near_r, near_i, far_strip, *refs = refs
    measured, rolled, fore_lane, fore_row, back_row, back_lane, twist_lane, twist_row, *refs = refs
    out_r, out_i, out_b, in_a, in_b, field, sums = refs
    size = rolled.shape[2]
    half = size // 2
    extent = field.shape[2]
    odd_col = info[1]
    other = 1 - odd_col
    near_at, a_at, b_at, far_at = places(odd_col)
    lanes = lax.broadcasted_iota(jnp.int32, (1, half), 1)
    sums[...] = jnp.zeros_like(sums)
    field[a_at, 0] = ext_r[...]
    field[a_at, 1] = ext_i[...]
    field[b_at] = ext_b[...]
    if first:
        upper, middle, lower = slice(0, MARGIN), slice(MARGIN, extent - MARGIN), slice(extent - MARGIN, extent)
        field[near_at, :, middle] = near_edge[other]
        field[near_at, :, upper] = near_corner[other, 0]
        field[near_at, :, lower] = near_corner[other, 1]
        field[far_at, :, middle] = jnp.where(info[4] == 1, 0.0, far_edge[odd_col])
        field[far_at, :, upper] = far_corner[0]
        field[far_at, :, lower] = far_corner[1]
    else:
        field[near_at, 0] = near_r[other]
        field[near_at, 1] = near_i[other]
        field[far_at] = far_strip[...]
    lane_r, lane_i = twist_lane[0], twist_lane[1]
    row_r, row_i = twist_row[0], twist_row[1]

    def enter(slot):
        rows = pl.ds(positions[slot, 0], size)
        waves = []
        for block in range(2):
            near = lanes + half * block >= positions[slot, 1]
            cut = slice(half * block, half * (block + 1))
            p_r, p_i = rolled[slot, 0, :, cut], rolled[slot, 1, :, cut]
            o_r = jnp.where(near, field[block, 0, rows, :], field[block + 2, 0, rows, :])
            o_i = jnp.where(near, field[block, 1, rows, :], field[block + 2, 1, rows, :])
            waves.append((p_r * o_r - p_i * o_i, p_r * o_i + p_i * o_r))
        (r0, i0), (r1, i1) = waves
        d_r, d_i = r0 - r1, i0 - i1
        return [
            wide(r0 + r1, i0 + i1),
            wide(d_r * lane_r - d_i * lane_i, d_r * lane_i + d_i * lane_r),
        ]

    def cross(pair):
        even, odd = pair
        r_all = wide(even[:, :half], odd[:, :half])
        i_all = wide(even[:, half:], odd[:, half:])
        r0, r1 = r_all[:half], r_all[half:]
        i0, i1 = i_all[:half], i_all[half:]
        d_r, d_i = r0 - r1, i0 - i1
        return [
            tall(r0 + r1, i0 + i1),
            tall(d_r * row_r - d_i * row_i, d_r * row_i + d_i * row_r),
        ]

    def scale(slot, pair):
        scaled = []
        for parity, spectrum in enumerate(pair):
            s_r, s_i = spectrum[:half], spectrum[half:]
            misfit = s_r * s_r + s_i * s_i - measured[slot, parity]
            scaled.append(tall(misfit * s_r, misfit * s_i))
        return scaled

    def cross_back(pair):
        even, odd = pair
        e_r, e_i = even[:half], even[half:]
        o_r, o_i = odd[:half], odd[half:]
        t_r = o_r * row_r + o_i * row_i
        t_i = o_i * row_r - o_r * row_i
        full_r = tall(e_r + t_r, e_r - t_r)
        full_i = tall(e_i + t_i, e_i - t_i)
        return [
            wide(full_r[:, :half], full_i[:, :half]),
            wide(full_r[:, half:], full_i[:, half:]),
        ]

    def leave(slot, pair, keep):
        rows = pl.ds(positions[slot, 0], size)
        even, odd = pair
        e_r, e_i = even[:, :half], even[:, half:]
        o_r, o_i = odd[:, :half], odd[:, half:]
        t_r = o_r * lane_r + o_i * lane_i
        t_i = o_i * lane_r - o_r * lane_i
        outs = [(e_r + t_r, e_i + t_i), (e_r - t_r, e_i - t_i)]
        for block, (b_r, b_i) in enumerate(outs):
            place = lanes + half * block
            near = place >= positions[slot, 1]
            far = place < positions[slot, 1]
            if keep is not None:
                near, far = near & keep, far & keep
            cut = slice(half * block, half * (block + 1))
            p_r, p_i = rolled[slot, 0, :, cut], rolled[slot, 1, :, cut]
            terms = (p_r * b_r + p_i * b_i, p_r * b_i - p_i * b_r)
            for part, term in enumerate(terms):
                sums[block, part, rows, :] += jnp.where(near, term, 0.0)
                sums[block + 2, part, rows, :] += jnp.where(far, term, 0.0)

    def one_group(group, carry):
        slots = [GROUP * group + i for i in range(GROUP)]
        live = [None] + [slot < counts[0, 0] for slot in slots[1:]]
        pairs = [enter(slot) for slot in slots]
        pairs = [[times_table(half_, fore_lane[...]) for half_ in pair] for pair in pairs]
        pairs = [cross(pair) for pair in pairs]
        pairs = [[table_times(fore_row[...], half_) for half_ in pair] for pair in pairs]
        pairs = [scale(slot, pair) for slot, pair in zip(slots, pairs)]
        pairs = [[table_times(back_row[...], half_) for half_ in pair] for pair in pairs]
        pairs = [cross_back(pair) for pair in pairs]
        pairs = [[times_table(half_, back_lane[...]) for half_ in pair] for pair in pairs]
        for slot, pair, keep in zip(slots, pairs, live):
            leave(slot, pair, keep)
        return carry

    lax.fori_loop(0, (counts[0, 0] + GROUP - 1) // GROUP, one_group, 0)
    out_r[...] = sums[near_at, 0]
    out_i[...] = sums[near_at, 1]
    out_b[...] = sums[far_at]
    in_a[...] = sums[a_at]
    in_b[...] = sums[b_at]


def gradient(first, info, positions, counts, ext, sides, measured, rolled, tables):
    extent = ext[0].shape[0]
    plane, strip = shaped(extent, HALF), shaped(2, extent, HALF)
    return whole(
        functools.partial(gradient_body, first),
        (plane, plane, strip, strip, strip),
        (info, positions, counts),
        (*ext, *sides, measured, rolled, *tables),
        [pltpu.VMEM((4, 2, extent, HALF), jnp.float32)] * 2,
        flops=6 * 8 * 3 * 2**25,
    )


def extend_body(info, tile, halo_a, halo_b, near, far, ext_r, ext_i, ext_b, corner_a, corner_b):
    size = tile.shape[1]
    odd_row, odd_col = info[0], info[1]

    def fill(cut_a, cut_b):
        above = [jnp.where(odd_row == 1, halo_a[part], halo_b[part]) for part in range(2)]
        below = [jnp.where(odd_row == 1, halo_b[part], halo_a[part]) for part in range(2)]
        targets = [ext_r, ext_i]
        for part in range(2):
            corner_a[0, part] = above[part][:, cut_a]
            corner_a[1, part] = below[part][:, cut_a]
            corner_b[0, part] = above[part][:, cut_b]
            corner_b[1, part] = below[part][:, cut_b]
            targets[part][:MARGIN, :] = above[part][:, cut_a]
            targets[part][MARGIN : MARGIN + size, :] = tile[part, :, cut_a]
            targets[part][MARGIN + size :, :] = below[part][:, cut_a]
            ext_b[part, :MARGIN] = above[part][:, cut_b]
            ext_b[part, MARGIN : MARGIN + size] = tile[part, :, cut_b]
            ext_b[part, MARGIN + size :] = below[part][:, cut_b]

    left, right = slice(0, HALF), slice(HALF, 2 * HALF)

    @pl.when(odd_col == 1)
    def _():
        fill(left, right)

    @pl.when(odd_col == 0)
    def _():
        fill(right, left)


def outgoing(odd_row, total, width, out_a, out_b):
    extent = total.shape[1]
    out_a[...] = total[:, pl.ds(pl.multiple_of((1 - odd_row) * (extent - width), 8), width), :]
    out_b[...] = total[:, pl.ds(pl.multiple_of(odd_row * (extent - width), 8), width), :]


def join_near_body(width, info, inner, near_r, near_i, total, out_a, out_b):
    other = 1 - info[1]
    total[0] = inner[0] + near_r[other]
    total[1] = inner[1] + near_i[other]
    outgoing(info[0], total, width, out_a, out_b)


def join_far_body(width, info, inner, strip, total, out_a, out_b):
    total[...] = inner[...] + strip[...]
    outgoing(info[0], total, width, out_a, out_b)


def updated(info, part, ext, total, halo_a, halo_b):
    middle = total.shape[1] // 2
    above = total[part, :middle] + jnp.where(info[0] == 1, halo_a[part], halo_b[part])
    below = total[part, middle:] + jnp.where(info[0] == 1, halo_b[part], halo_a[part])
    row = lax.broadcasted_iota(jnp.int32, (middle, HALF), 0)
    above = jnp.where((info[2] == 1) & (row < MARGIN), 0.0, above)
    below = jnp.where((info[3] == 1) & (row >= middle - MARGIN), 0.0, below)
    return tall(ext[:middle] - step_rate * above, ext[middle:] - step_rate * below)


def update_near_body(info, ext_r, ext_i, total, halo_a, halo_b, out_r, out_i):
    out_r[...] = updated(info, 0, ext_r, total, halo_a, halo_b)
    out_i[...] = updated(info, 1, ext_i, total, halo_a, halo_b)


def update_far_body(info, ext_b, total, halo_a, halo_b, out):
    for part in range(2):
        out[part] = updated(info, part, ext_b.at[part], total, halo_a, halo_b)


def finish_body(info, ext_r, ext_i, ext_b, total_a, total_b, near_a, near_b, far_a, far_b, out):
    size = out.shape[1]
    half = size // 2
    upper, lower = slice(MARGIN, MARGIN + half), slice(MARGIN + half, MARGIN + size)

    def settle(cut, ext, total, halo_a, halo_b):
        for part in range(2):
            above = total[part, upper] + jnp.where(info[0] == 1, halo_a[part], halo_b[part])
            below = total[part, lower] + jnp.where(info[0] == 1, halo_b[part], halo_a[part])
            out[part, :half, cut] = ext[part][upper] - step_rate * above
            out[part, half:, cut] = ext[part][lower] - step_rate * below

    def place(cut_a, cut_b):
        settle(cut_a, [ext_r, ext_i], total_a, near_a, near_b)
        settle(cut_b, [ext_b.at[0], ext_b.at[1]], total_b, far_a, far_b)

    left, right = slice(0, HALF), slice(HALF, 2 * HALF)

    @pl.when(info[1] == 1)
    def _():
        place(left, right)

    @pl.when(info[1] == 0)
    def _():
        place(right, left)


def constants(size):
    half = size // 2
    mixed, twiddle = rotation_tables(size)
    upper = mixed.astype(jnp.bfloat16)
    lower = (mixed - upper.astype(np.float32)).astype(jnp.bfloat16)
    fore_lane = jnp.asarray(np.concatenate([upper, upper, lower], axis=0))
    back_row = jnp.asarray(np.concatenate([upper, upper, lower], axis=1))
    fore_row = jnp.asarray(np.concatenate([upper.T, upper.T, lower.T], axis=1))
    back_lane = jnp.asarray(np.concatenate([upper.T, upper.T, lower.T], axis=0))
    twist_lane = jnp.asarray(twiddle.reshape(2, 1, half))
    twist_row = jnp.asarray(np.ascontiguousarray(np.broadcast_to(twiddle[:, :, None], (2, half, size))))
    return fore_lane, fore_row, back_row, back_lane, twist_lane, twist_row


def swapped(value, axis, first):
    count = lax.axis_size(axis)
    route = []
    for i in range(first, count - 1, 2):
        route += [(i, i + 1), (i + 1, i)]
    return lax.ppermute(value, axis, route)


def paired(value, first=0):
    count = lax.axis_size("cols")
    groups = [[i, (i + 1) % count] for i in range(first, count, 2)]
    return lax.all_gather(value, "cols", axis_index_groups=groups)


def both_rows(edge_a, edge_b):
    return swapped(edge_a, "rows", 0), swapped(edge_b, "rows", 1)


def summed(info, width, out_r, out_i, out_b, in_a, in_b):
    extent = in_a.shape[1]
    strip, piece = shaped(2, extent, HALF), shaped(2, width, HALF)
    far = swapped(out_b, "cols", 1)
    near = paired(out_r), paired(out_i)
    total_a, *edges = whole(functools.partial(join_near_body, width), (strip, piece, piece), (info,), (in_a, *near))
    halos_a = both_rows(*edges)
    total_b, *edges = whole(functools.partial(join_far_body, width), (strip, piece, piece), (info,), (in_b, far))
    halos_b = both_rows(*edges)
    return total_a, halos_a, total_b, halos_b


def on_device(object_field, probe, positions, counts, intensity):
    size = probe.shape[1]
    tile = object_field.shape[1]
    extent = tile + 2 * MARGIN
    row, col = lax.axis_index("rows"), lax.axis_index("cols")
    last, end = lax.axis_size("rows") - 1, lax.axis_size("cols") - 1
    info = jnp.stack(
        [row % 2, col % 2, row == 0, row == last, (col == 0) | (col == end)]
    ).astype(jnp.int32)
    tables = constants(size)
    order = jnp.asarray(split_order(size)).astype(jnp.bfloat16)
    positions, intensity = positions[0, 0], intensity[0, 0]
    plane, strip = shaped(extent, HALF), shaped(2, extent, HALF)
    corner = shaped(2, 2, MARGIN, HALF)

    edge, side = shaped(2, MARGIN, tile), shaped(2, tile, MARGIN)
    edge_a, edge_b, side_a, side_b = whole(cut_body, (edge, edge, side, side), (info,), (object_field,))
    halos = both_rows(edge_a, edge_b)
    far_edge, near_edge = paired(side_b, 1), paired(side_a)
    *ext, corner_a, corner_b = whole(
        extend_body,
        (plane, plane, strip, corner, corner),
        (info,),
        (object_field, *halos),
        unread=(near_edge, far_edge),
    )
    measured, rolled = prepare(positions, intensity, probe, order, corner_a)
    far_corner = swapped(corner_b, "cols", 1)
    sides = near_edge, paired(corner_a), far_edge, far_corner
    parts = gradient(True, info, positions, counts, ext, sides, measured, rolled, tables)
    total_a, halos_a, total_b, halos_b = summed(info, extent // 2, *parts)
    near_ext = whole(update_near_body, (plane, plane), (info,), (*ext[:2], total_a, *halos_a))
    far_ext = whole(update_far_body, (strip,), (info,), (ext[2], total_b, *halos_b))
    ext = (*near_ext, *far_ext)
    sides = paired(ext[0]), paired(ext[1]), swapped(ext[2], "cols", 1)
    parts = gradient(False, info, positions, counts, ext, sides, measured, rolled, tables)
    total_a, halos_a, total_b, halos_b = summed(info, MARGIN, *parts)
    return whole(
        finish_body, (shaped(2, tile, tile),), (info,), (*ext, total_a, total_b, *halos_a, *halos_b)
    )[0]


def solution(mesh):
    placed = (
        P(None, "rows", "cols"),
        P(),
        P("rows", "cols", None, None),
        P("rows", "cols"),
        P("rows", "cols", None, None, None),
    )
    return jax.shard_map(
        on_device, mesh=mesh, in_specs=placed, out_specs=P(None, "rows", "cols"), check_vma=False
    )
```

profile of v0, /device:TPU:10, one launch (start us, length us, event | category | flops | bytes accessed | tf_op | source)
XLA Modules:
  0.0 125.5 jit_solution(2147377170716973558)
XLA Ops:
  1.8 2.2 %collective-permute-start = (f32[2,128,256]{2,1,0:T(8,128)S(1)}, f32[2,128,256]{2,1,0:T(8,128)S(1)}, u32[]{:S(2)}, u32[]{:S(2)}) collective-permute-start(f32[2,128,256]{2,1,0:T(8,128)S(1)} %get-tuple-element.40), channel_id=1, source_target_pairs={{0,16},{16,0},{32,48},{48,32},{64,80},{80,64},{96,112},{112,96},{1... | collective-permute-start | bytes 786440 | tf_op jit(solution)/shard_map/ppermute | solution.py:415
  4.0 3.2 %collective-permute-start.1 = (f32[2,128,256]{2,1,0:T(8,128)S(1)}, f32[2,128,256]{2,1,0:T(8,128)S(1)}, u32[]{:S(2)}, u32[]{:S(2)}) collective-permute-start(f32[2,128,256]{2,1,0:T(8,128)S(1)} %get-tuple-element.41), channel_id=1, source_target_pairs={{16,32},{32,16},{48,64},{64,48},{80,96},{96,80},{17,33},{33,17},{4... | collective-permute-start | bytes 786440 | tf_op jit(solution)/shard_map/ppermute | solution.py:415
  7.2 2.2 %all-gather = f32[4,256,128]{2,1,0:T(8,128)S(1)} all-gather(f32[2,256,128]{2,1,0:T(8,128)S(1)} %get-tuple-element.42), channel_id=2, replica_groups={{0,1},{2,3},{4,5},{6,7},{8,9},{10,11},{12,13},{14,15},{16,17},{18,19},{..., dimensions={0}, use_global_device_ids=true | all-gather | bytes 786432 | tf_op jit(solution)/shard_map/all_gather | solution.py:421
  9.3 14.0 %all-gather.1 = f32[4,256,128]{2,1,0:T(8,128)S(1)} all-gather(f32[2,256,128]{2,1,0:T(8,128)S(1)} %get-tuple-element.43), channel_id=3, replica_groups={{1,2},{3,4},{5,6},{7,8},{9,10},{11,12},{13,14},{15,0},{17,18},{19,20},{..., dimensions={0}, use_global_device_ids=true | all-gather | bytes 786432 | tf_op jit(solution)/shard_map/all_gather | solution.py:421
  24.0 1.9 %collective-permute-start.2 = (f32[2,2,128,128]{3,2,1,0:T(8,128)S(1)}, f32[2,2,128,128]{3,2,1,0:T(8,128)S(1)}, u32[]{:S(2)}, u32[]{:S(2)}) collective-permute-start(f32[2,2,128,128]{3,2,1,0:T(8,128)S(1)} %get-tuple-element.48), channel_id=1, source_target_pairs={{1,2},{2,1},{3,4},{4,3},{5,6},{6,5},{7,8},{8,7},{9,10},{10,9},{11,... | collective-permute-start | bytes 786440 | tf_op jit(solution)/shard_map/ppermute | solution.py:415
  28.1 3.7 %shard_map.120 = (f32[6,2,128,256]{3,2,1,0:T(8,128)S(1)}, f32[6,2,256,256]{3,2,1,0:T(8,128)S(1)}) custom-call(s32[6,2]{1,0:T(8,128)S(1)} %copy.17.positions, s32[6,256,256]{2,1,0:T(8,128)S(1)} %bitcast.27, f32[2,256,256]{2,1,0:T(8,128)S(1)} %copy-done.2, bf16[256,256]{1,0:T(8,128)(2,1)S(1)} %copy-done.8, f32[2,2,128,128]{3,2,1,0:T(8,128)S(1)} %get-tuple-element.47.earlier), custom_call_target="tpu_custom_call" | custom-call | flops 805306368 | bytes 8388608 | tf_op jit(solution)/shard_map/pallas_call | solution.py:117
  31.9 2.2 %all-gather.2 = f32[4,2,128,128]{3,2,1,0:T(8,128)S(1)} all-gather(f32[2,2,128,128]{3,2,1,0:T(8,128)S(1)} %get-tuple-element.47.earlier), channel_id=4, replica_groups={{0,1},{2,3},{4,5},{6,7},{8,9},{10,11},{12,13},{14,15},{16,17},{18,19},{..., dimensions={0}, use_global_device_ids=true | all-gather | bytes 786432 | tf_op jit(solution)/shard_map/all_gather | solution.py:421
  34.1 8.2 %shard_map.121 = (f32[512,128]{1,0:T(8,128)S(1)}, f32[512,128]{1,0:T(8,128)S(1)}, f32[2,512,128]{2,1,0:T(8,128)S(1)}, f32[2,512,128]{2,1,0:T(8,128)S(1)}, f32[2,512,128]{2,1,0:T(8,128)S(1)}) custom-call(s32[5]{0:T(128)S(1)} %stack.35.info, s32[6,2]{1,0:T(8,128)S(1)} %copy.17.positions, s32[1,1]{1,0:T(1,128)S(6)} %copy.19.counts, ...), custom_call_target="tpu_custom_call" | custom-call | flops 4831838208 | bytes 8388608 | tf_op jit(solution)/shard_map/pallas_call | solution.py:49
  42.4 3.4 %collective-permute-start.5 = (f32[2,512,128]{2,1,0:T(8,128)S(1)}, f32[2,512,128]{2,1,0:T(8,128)S(1)}, u32[]{:S(2)}, u32[]{:S(2)}) collective-permute-start(f32[2,512,128]{2,1,0:T(8,128)S(1)} %get-tuple-element.60), channel_id=1, source_target_pairs={{1,2},{2,1},{3,4},{4,3},{5,6},{6,5},{7,8},{8,7},{9,10},{10,9},{11,... | collective-permute-start | bytes 1572872 | tf_op jit(solution)/shard_map/ppermute | solution.py:415
  45.7 9.2 %collective-permute-done.5.strip = f32[2,512,128]{2,1,0:T(8,128)S(1)} collective-permute-done((f32[2,512,128]{2,1,0:T(8,128)S(1)}, f32[2,512,128]{2,1,0:T(8,128)S(1)}, u32[]{:S(2)}, u32[]{:S(2)}) %collective-permute-start.5) | collective-permute-done | bytes 524320 | tf_op jit(solution)/shard_map/ppermute | solution.py:415
  55.7 3.9 %collective-permute-start.7 = (f32[2,256,128]{2,1,0:T(8,128)S(1)}, f32[2,256,128]{2,1,0:T(8,128)S(1)}, u32[]{:S(2)}, u32[]{:S(2)}) collective-permute-start(f32[2,256,128]{2,1,0:T(8,128)S(1)} %get-tuple-element.63), channel_id=1, source_target_pairs={{16,32},{32,16},{48,64},{64,48},{80,96},{96,80},{17,33},{33,17},{4... | collective-permute-start | bytes 786440 | tf_op jit(solution)/shard_map/ppermute | solution.py:415
  59.6 2.2 %all-gather.3 = f32[1024,128]{1,0:T(8,128)S(1)} all-gather(f32[512,128]{1,0:T(8,128)S(1)} %get-tuple-element.52), channel_id=5, replica_groups={{0,1},{2,3},{4,5},{6,7},{8,9},{10,11},{12,13},{14,15},{16,17},{18,19},{..., dimensions={0}, use_global_device_ids=true | all-gather | bytes 786432 | tf_op jit(solution)/shard_map/all_gather | solution.py:421
  61.7 2.2 %all-gather.4 = f32[1024,128]{1,0:T(8,128)S(1)} all-gather(f32[512,128]{1,0:T(8,128)S(1)} %get-tuple-element.53), channel_id=6, replica_groups={{0,1},{2,3},{4,5},{6,7},{8,9},{10,11},{12,13},{14,15},{16,17},{18,19},{..., dimensions={0}, use_global_device_ids=true | all-gather | bytes 786432 | tf_op jit(solution)/shard_map/all_gather | solution.py:421
  64.5 3.2 %collective-permute-start.3 = (f32[2,256,128]{2,1,0:T(8,128)S(1)}, f32[2,256,128]{2,1,0:T(8,128)S(1)}, u32[]{:S(2)}, u32[]{:S(2)}) collective-permute-start(f32[2,256,128]{2,1,0:T(8,128)S(1)} %get-tuple-element.55), channel_id=1, source_target_pairs={{0,16},{16,0},{32,48},{48,32},{64,80},{80,64},{96,112},{112,96},{1... | collective-permute-start | bytes 786440 | tf_op jit(solution)/shard_map/ppermute | solution.py:415
  67.8 1.9 %collective-permute-start.4 = (f32[2,256,128]{2,1,0:T(8,128)S(1)}, f32[2,256,128]{2,1,0:T(8,128)S(1)}, u32[]{:S(2)}, u32[]{:S(2)}) collective-permute-start(f32[2,256,128]{2,1,0:T(8,128)S(1)} %get-tuple-element.56), channel_id=1, source_target_pairs={{16,32},{32,16},{48,64},{64,48},{80,96},{96,80},{17,33},{33,17},{4... | collective-permute-start | bytes 786440 | tf_op jit(solution)/shard_map/ppermute | solution.py:415
  70.4 5.7 %collective-permute-start.8 = (f32[2,512,128]{2,1,0:T(8,128)S(1)}, f32[2,512,128]{2,1,0:T(8,128)S(1)}, u32[]{:S(2)}, u32[]{:S(2)}) collective-permute-start(f32[2,512,128]{2,1,0:T(8,128)S(1)} %shard_map.125.ext_b), channel_id=1, source_target_pairs={{1,2},{2,1},{3,4},{4,3},{5,6},{6,5},{7,8},{8,7},{9,10},{10,9},{11,... | collective-permute-start | bytes 1572872 | tf_op jit(solution)/shard_map/ppermute | solution.py:415
  76.1 4.0 %collective-permute-done.4.halo_b = f32[2,256,128]{2,1,0:T(8,128)S(1)} collective-permute-done((f32[2,256,128]{2,1,0:T(8,128)S(1)}, f32[2,256,128]{2,1,0:T(8,128)S(1)}, u32[]{:S(2)}, u32[]{:S(2)}) %collective-permute-start.4) | collective-permute-done | bytes 262176 | tf_op jit(solution)/shard_map/ppermute | solution.py:415
  80.8 2.2 %all-gather.5 = f32[1024,128]{1,0:T(8,128)S(1)} all-gather(f32[512,128]{1,0:T(8,128)S(1)} %get-tuple-element.57.ext_r), channel_id=7, replica_groups={{0,1},{2,3},{4,5},{6,7},{8,9},{10,11},{12,13},{14,15},{16,17},{18,19},{..., dimensions={0}, use_global_device_ids=true | all-gather | bytes 786432 | tf_op jit(solution)/shard_map/all_gather | solution.py:421
  83.0 2.2 %all-gather.6 = f32[1024,128]{1,0:T(8,128)S(1)} all-gather(f32[512,128]{1,0:T(8,128)S(1)} %get-tuple-element.58.ext_i), channel_id=8, replica_groups={{0,1},{2,3},{4,5},{6,7},{8,9},{10,11},{12,13},{14,15},{16,17},{18,19},{..., dimensions={0}, use_global_device_ids=true | all-gather | bytes 786432 | tf_op jit(solution)/shard_map/all_gather | solution.py:421
  85.2 4.5 %collective-permute-done.8.refs_2_ = f32[2,512,128]{2,1,0:T(8,128)S(1)} collective-permute-done((f32[2,512,128]{2,1,0:T(8,128)S(1)}, f32[2,512,128]{2,1,0:T(8,128)S(1)}, u32[]{:S(2)}, u32[]{:S(2)}) %collective-permute-start.8) | collective-permute-done | bytes 524320 | tf_op jit(solution)/shard_map/ppermute | solution.py:415
  89.6 8.2 %shard_map.126 = (f32[512,128]{1,0:T(8,128)S(1)}, f32[512,128]{1,0:T(8,128)S(1)}, f32[2,512,128]{2,1,0:T(8,128)S(1)}, f32[2,512,128]{2,1,0:T(8,128)S(1)}, f32[2,512,128]{2,1,0:T(8,128)S(1)}) custom-call(s32[5]{0:T(128)S(1)} %stack.35.info, s32[6,2]{1,0:T(8,128)S(1)} %copy.17.positions, s32[1,1]{1,0:T(1,128)S(6)} %copy.19.counts, ...), custom_call_target="tpu_custom_call" | custom-call | flops 4831838208 | bytes 8388608 | tf_op jit(solution)/shard_map/pallas_call | solution.py:49
  97.9 1.9 %collective-permute-start.9 = (f32[2,512,128]{2,1,0:T(8,128)S(1)}, f32[2,512,128]{2,1,0:T(8,128)S(1)}, u32[]{:S(2)}, u32[]{:S(2)}) collective-permute-start(f32[2,512,128]{2,1,0:T(8,128)S(1)} %get-tuple-element.69), channel_id=1, source_target_pairs={{1,2},{2,1},{3,4},{4,3},{5,6},{6,5},{7,8},{8,7},{9,10},{10,9},{11,... | collective-permute-start | bytes 1572872 | tf_op jit(solution)/shard_map/ppermute | solution.py:415
  99.8 2.2 %all-gather.7 = f32[1024,128]{1,0:T(8,128)S(1)} all-gather(f32[512,128]{1,0:T(8,128)S(1)} %get-tuple-element.65), channel_id=9, replica_groups={{0,1},{2,3},{4,5},{6,7},{8,9},{10,11},{12,13},{14,15},{16,17},{18,19},{..., dimensions={0}, use_global_device_ids=true | all-gather | bytes 786432 | tf_op jit(solution)/shard_map/all_gather | solution.py:421
  102.0 2.2 %all-gather.8 = f32[1024,128]{1,0:T(8,128)S(1)} all-gather(f32[512,128]{1,0:T(8,128)S(1)} %get-tuple-element.66), channel_id=10, replica_groups={{0,1},{2,3},{4,5},{6,7},{8,9},{10,11},{12,13},{14,15},{16,17},{18,19},{..., dimensions={0}, use_global_device_ids=true | all-gather | bytes 786432 | tf_op jit(solution)/shard_map/all_gather | solution.py:421
  104.8 2.8 %collective-permute-start.10 = (f32[2,128,128]{2,1,0:T(8,128)S(1)}, f32[2,128,128]{2,1,0:T(8,128)S(1)}, u32[]{:S(2)}, u32[]{:S(2)}) collective-permute-start(f32[2,128,128]{2,1,0:T(8,128)S(1)} %get-tuple-element.71), channel_id=1, source_target_pairs={{0,16},{16,0},{32,48},{48,32},{64,80},{80,64},{96,112},{112,96},{1... | collective-permute-start | bytes 393224 | tf_op jit(solution)/shard_map/ppermute | solution.py:415
  107.6 1.9 %collective-permute-start.11 = (f32[2,128,128]{2,1,0:T(8,128)S(1)}, f32[2,128,128]{2,1,0:T(8,128)S(1)}, u32[]{:S(2)}, u32[]{:S(2)}) collective-permute-start(f32[2,128,128]{2,1,0:T(8,128)S(1)} %get-tuple-element.72), channel_id=1, source_target_pairs={{16,32},{32,16},{48,64},{64,48},{80,96},{96,80},{17,33},{33,17},{4... | collective-permute-start | bytes 393224 | tf_op jit(solution)/shard_map/ppermute | solution.py:415
  111.3 3.6 %collective-permute-start.12 = (f32[2,128,128]{2,1,0:T(8,128)S(1)}, f32[2,128,128]{2,1,0:T(8,128)S(1)}, u32[]{:S(2)}, u32[]{:S(2)}) collective-permute-start(f32[2,128,128]{2,1,0:T(8,128)S(1)} %get-tuple-element.73), channel_id=1, source_target_pairs={{0,16},{16,0},{32,48},{48,32},{64,80},{80,64},{96,112},{112,96},{1... | collective-permute-start | bytes 393224 | tf_op jit(solution)/shard_map/ppermute | solution.py:415
  114.8 1.9 %collective-permute-start.13 = (f32[2,128,128]{2,1,0:T(8,128)S(1)}, f32[2,128,128]{2,1,0:T(8,128)S(1)}, u32[]{:S(2)}, u32[]{:S(2)}) collective-permute-start(f32[2,128,128]{2,1,0:T(8,128)S(1)} %get-tuple-element.74), channel_id=1, source_target_pairs={{16,32},{32,16},{48,64},{64,48},{80,96},{96,80},{17,33},{33,17},{4... | collective-permute-start | bytes 393224 | tf_op jit(solution)/shard_map/ppermute | solution.py:415
  116.7 1.5 %collective-permute-done.11.near_b = f32[2,128,128]{2,1,0:T(8,128)S(1)} collective-permute-done((f32[2,128,128]{2,1,0:T(8,128)S(1)}, f32[2,128,128]{2,1,0:T(8,128)S(1)}, u32[]{:S(2)}, u32[]{:S(2)}) %collective-permute-start.11) | collective-permute-done | bytes 131104 | tf_op jit(solution)/shard_map/ppermute | solution.py:415
  118.2 2.2 %collective-permute-done.12.far_a = f32[2,128,128]{2,1,0:T(8,128)S(1)} collective-permute-done((f32[2,128,128]{2,1,0:T(8,128)S(1)}, f32[2,128,128]{2,1,0:T(8,128)S(1)}, u32[]{:S(2)}, u32[]{:S(2)}) %collective-permute-start.12) | collective-permute-done | bytes 131104 | tf_op jit(solution)/shard_map/ppermute | solution.py:415
  120.4 3.6 %collective-permute-done.13.far_b = f32[2,128,128]{2,1,0:T(8,128)S(1)} collective-permute-done((f32[2,128,128]{2,1,0:T(8,128)S(1)}, f32[2,128,128]{2,1,0:T(8,128)S(1)}, u32[]{:S(2)}, u32[]{:S(2)}) %collective-permute-start.13) | collective-permute-done | bytes 131104 | tf_op jit(solution)/shard_map/ppermute | solution.py:415
  124.1 1.5 %shard_map.129 = f32[2,256,256]{2,1,0:T(8,128)} custom-call(s32[5]{0:T(128)S(1)} %stack.35.info, f32[512,128]{1,0:T(8,128)S(1)} %get-tuple-element.57.ext_r, f32[512,128]{1,0:T(8,128)S(1)} %get-tuple-element.58.ext_i, f32[2,512,128]{2,1,0:T(8,128)S(1)} %shard_map.125.ext_b, f32[2,512,128]{2,1,0:T(8,128)S(1)} %get-tuple-element.67.total_a, ...), custom_call_target="tpu_custom_call" | custom-call | flops 1048576 | bytes 8388608 | tf_op jit(solution)/shard_map/pallas_call | solution.py:49
  (41 shorter events, 9.0 us)
Async XLA Ops:
  0.1 1.0 copy-start
  1.8 21.6 %collective-permute-start = (f32[2,128,256]{2,1,0:T(8,128)S(1)}, f32[2,128,256]{2,1,0:T(8,128)S(1)}, u32[]{:S(2)}, u32[]{:S(2)}) collective-permute-start(f32[2,128,256]{2,1,0:T(8,128)S(1)} %get-tuple-element.40), channel_id=1, source_target_pairs={{0,16},{16,0},{32,48},{48,32},{64,80},{80,64},{96,112},{112,96},{1... | collective-permute-start | bytes 786440 | tf_op jit(solution)/shard_map/ppermute | solution.py:415
  4.0 19.4 %collective-permute-start.1 = (f32[2,128,256]{2,1,0:T(8,128)S(1)}, f32[2,128,256]{2,1,0:T(8,128)S(1)}, u32[]{:S(2)}, u32[]{:S(2)}) collective-permute-start(f32[2,128,256]{2,1,0:T(8,128)S(1)} %get-tuple-element.41), channel_id=1, source_target_pairs={{16,32},{32,16},{48,64},{64,48},{80,96},{96,80},{17,33},{33,17},{4... | collective-permute-start | bytes 786440 | tf_op jit(solution)/shard_map/ppermute | solution.py:415
  9.3 17.2 %copy-start.10 = (s32[1,1,6,2]{2,3,1,0:T(2,128)S(1)}, s32[1,1,6,2]{2,3,1,0:T(2,128)}, u32[]{:S(2)}) copy-start(s32[1,1,6,2]{2,3,1,0:T(2,128)} %param.14) | copy-start | bytes 148
  9.3 17.3 %copy-start.2 = (f32[2,256,256]{2,1,0:T(8,128)S(1)}, f32[2,256,256]{2,1,0:T(8,128)}, u32[]{:S(2)}) copy-start(f32[2,256,256]{2,1,0:T(8,128)} %probe.1) | copy-start | bytes 1572868
  9.3 17.3 %copy-start.8 = (bf16[256,256]{1,0:T(8,128)(2,1)S(1)}, bf16[256,256]{1,0:T(8,128)(2,1)}, u32[]{:S(2)}) copy-start(bf16[256,256]{1,0:T(8,128)(2,1)} %constant.55.order) | copy-start | bytes 393220
  24.0 10.1 %collective-permute-start.2 = (f32[2,2,128,128]{3,2,1,0:T(8,128)S(1)}, f32[2,2,128,128]{3,2,1,0:T(8,128)S(1)}, u32[]{:S(2)}, u32[]{:S(2)}) collective-permute-start(f32[2,2,128,128]{3,2,1,0:T(8,128)S(1)} %get-tuple-element.48), channel_id=1, source_target_pairs={{1,2},{2,1},{3,4},{4,3},{5,6},{6,5},{7,8},{8,7},{9,10},{10,9},{11,... | collective-permute-start | bytes 786440 | tf_op jit(solution)/shard_map/ppermute | solution.py:415
  26.7 1.4 %copy-start.1 = (s32[1,1,6,256,256]{4,3,2,1,0:T(8,128)S(1)}, s32[1,1,6,256,256]{4,3,2,1,0:T(8,128)}, u32[]{:S(2)}) copy-start(s32[1,1,6,256,256]{4,3,2,1,0:T(8,128)} %param.16) | copy-start | bytes 4718596
  28.1 6.0 %copy-start.3 = (bf16[768,256]{1,0:T(8,128)(2,1)S(1)}, bf16[768,256]{1,0:T(8,128)(2,1)}, u32[]{:S(2)}) copy-start(bf16[768,256]{1,0:T(8,128)(2,1)} %constant.48.clone.refs_9_.refs_8_) | copy-start | bytes 1179652
  28.1 6.0 %copy-start.4 = (bf16[256,768]{1,0:T(8,128)(2,1)S(1)}, bf16[256,768]{1,0:T(8,128)(2,1)}, u32[]{:S(2)}) copy-start(bf16[256,768]{1,0:T(8,128)(2,1)} %constant.47.clone.refs_7_.refs_6_) | copy-start | bytes 1179652
  28.1 6.0 %copy-start.5 = (bf16[256,768]{1,0:T(8,128)(2,1)S(1)}, bf16[256,768]{1,0:T(8,128)(2,1)}, u32[]{:S(2)}) copy-start(bf16[256,768]{1,0:T(8,128)(2,1)} %constant.46.clone.refs_8_.refs_7_) | copy-start | bytes 1179652
  28.1 6.0 %copy-start.6 = (bf16[768,256]{1,0:T(8,128)(2,1)S(1)}, bf16[768,256]{1,0:T(8,128)(2,1)}, u32[]{:S(2)}) copy-start(bf16[768,256]{1,0:T(8,128)(2,1)} %constant.45.clone.refs_6_.refs_5_) | copy-start | bytes 1179652
  28.1 6.0 %copy-start.7 = (f32[2,128,256]{2,1,0:T(8,128)S(1)}, f32[2,128,256]{2,1,0:T(8,128)}, u32[]{:S(2)}) copy-start(f32[2,128,256]{2,1,0:T(8,128)} %constant.50.clone.refs_11_.refs_10_) | copy-start | bytes 786436
  28.1 6.0 %copy-start.9 = (f32[2,1,128]{2,1,0:T(1,128)S(1)}, f32[2,1,128]{2,1,0:T(1,128)}, u32[]{:S(2)}) copy-start(f32[2,1,128]{2,1,0:T(1,128)} %constant.49.clone.refs_10_.refs_9_) | copy-start | bytes 3076
  42.4 12.6 %collective-permute-start.5 = (f32[2,512,128]{2,1,0:T(8,128)S(1)}, f32[2,512,128]{2,1,0:T(8,128)S(1)}, u32[]{:S(2)}, u32[]{:S(2)}) collective-permute-start(f32[2,512,128]{2,1,0:T(8,128)S(1)} %get-tuple-element.60), channel_id=1, source_target_pairs={{1,2},{2,1},{3,4},{4,3},{5,6},{6,5},{7,8},{8,7},{9,10},{10,9},{11,... | collective-permute-start | bytes 1572872 | tf_op jit(solution)/shard_map/ppermute | solution.py:415
  55.6 14.1 %collective-permute-start.6 = (f32[2,256,128]{2,1,0:T(8,128)S(1)}, f32[2,256,128]{2,1,0:T(8,128)S(1)}, u32[]{:S(2)}, u32[]{:S(2)}) collective-permute-start(f32[2,256,128]{2,1,0:T(8,128)S(1)} %get-tuple-element.62), channel_id=1, source_target_pairs={{0,16},{16,0},{32,48},{48,32},{64,80},{80,64},{96,112},{112,96},{1... | collective-permute-start | bytes 786440 | tf_op jit(solution)/shard_map/ppermute | solution.py:415
  55.7 14.0 %collective-permute-start.7 = (f32[2,256,128]{2,1,0:T(8,128)S(1)}, f32[2,256,128]{2,1,0:T(8,128)S(1)}, u32[]{:S(2)}, u32[]{:S(2)}) collective-permute-start(f32[2,256,128]{2,1,0:T(8,128)S(1)} %get-tuple-element.63), channel_id=1, source_target_pairs={{16,32},{32,16},{48,64},{64,48},{80,96},{96,80},{17,33},{33,17},{4... | collective-permute-start | bytes 786440 | tf_op jit(solution)/shard_map/ppermute | solution.py:415
  64.5 11.5 %collective-permute-start.3 = (f32[2,256,128]{2,1,0:T(8,128)S(1)}, f32[2,256,128]{2,1,0:T(8,128)S(1)}, u32[]{:S(2)}, u32[]{:S(2)}) collective-permute-start(f32[2,256,128]{2,1,0:T(8,128)S(1)} %get-tuple-element.55), channel_id=1, source_target_pairs={{0,16},{16,0},{32,48},{48,32},{64,80},{80,64},{96,112},{112,96},{1... | collective-permute-start | bytes 786440 | tf_op jit(solution)/shard_map/ppermute | solution.py:415
  67.8 12.4 %collective-permute-start.4 = (f32[2,256,128]{2,1,0:T(8,128)S(1)}, f32[2,256,128]{2,1,0:T(8,128)S(1)}, u32[]{:S(2)}, u32[]{:S(2)}) collective-permute-start(f32[2,256,128]{2,1,0:T(8,128)S(1)} %get-tuple-element.56), channel_id=1, source_target_pairs={{16,32},{32,16},{48,64},{64,48},{80,96},{96,80},{17,33},{33,17},{4... | collective-permute-start | bytes 786440 | tf_op jit(solution)/shard_map/ppermute | solution.py:415
  70.4 19.3 %collective-permute-start.8 = (f32[2,512,128]{2,1,0:T(8,128)S(1)}, f32[2,512,128]{2,1,0:T(8,128)S(1)}, u32[]{:S(2)}, u32[]{:S(2)}) collective-permute-start(f32[2,512,128]{2,1,0:T(8,128)S(1)} %shard_map.125.ext_b), channel_id=1, source_target_pairs={{1,2},{2,1},{3,4},{4,3},{5,6},{6,5},{7,8},{8,7},{9,10},{10,9},{11,... | collective-permute-start | bytes 1572872 | tf_op jit(solution)/shard_map/ppermute | solution.py:415
  97.9 12.8 %collective-permute-start.9 = (f32[2,512,128]{2,1,0:T(8,128)S(1)}, f32[2,512,128]{2,1,0:T(8,128)S(1)}, u32[]{:S(2)}, u32[]{:S(2)}) collective-permute-start(f32[2,512,128]{2,1,0:T(8,128)S(1)} %get-tuple-element.69), channel_id=1, source_target_pairs={{1,2},{2,1},{3,4},{4,3},{5,6},{6,5},{7,8},{8,7},{9,10},{10,9},{11,... | collective-permute-start | bytes 1572872 | tf_op jit(solution)/shard_map/ppermute | solution.py:415
  104.8 12.0 %collective-permute-start.10 = (f32[2,128,128]{2,1,0:T(8,128)S(1)}, f32[2,128,128]{2,1,0:T(8,128)S(1)}, u32[]{:S(2)}, u32[]{:S(2)}) collective-permute-start(f32[2,128,128]{2,1,0:T(8,128)S(1)} %get-tuple-element.71), channel_id=1, source_target_pairs={{0,16},{16,0},{32,48},{48,32},{64,80},{80,64},{96,112},{112,96},{1... | collective-permute-start | bytes 393224 | tf_op jit(solution)/shard_map/ppermute | solution.py:415
  107.6 10.7 %collective-permute-start.11 = (f32[2,128,128]{2,1,0:T(8,128)S(1)}, f32[2,128,128]{2,1,0:T(8,128)S(1)}, u32[]{:S(2)}, u32[]{:S(2)}) collective-permute-start(f32[2,128,128]{2,1,0:T(8,128)S(1)} %get-tuple-element.72), channel_id=1, source_target_pairs={{16,32},{32,16},{48,64},{64,48},{80,96},{96,80},{17,33},{33,17},{4... | collective-permute-start | bytes 393224 | tf_op jit(solution)/shard_map/ppermute | solution.py:415
  111.3 9.2 %collective-permute-start.12 = (f32[2,128,128]{2,1,0:T(8,128)S(1)}, f32[2,128,128]{2,1,0:T(8,128)S(1)}, u32[]{:S(2)}, u32[]{:S(2)}) collective-permute-start(f32[2,128,128]{2,1,0:T(8,128)S(1)} %get-tuple-element.73), channel_id=1, source_target_pairs={{0,16},{16,0},{32,48},{48,32},{64,80},{80,64},{96,112},{112,96},{1... | collective-permute-start | bytes 393224 | tf_op jit(solution)/shard_map/ppermute | solution.py:415
  114.8 9.3 %collective-permute-start.13 = (f32[2,128,128]{2,1,0:T(8,128)S(1)}, f32[2,128,128]{2,1,0:T(8,128)S(1)}, u32[]{:S(2)}, u32[]{:S(2)}) collective-permute-start(f32[2,128,128]{2,1,0:T(8,128)S(1)} %get-tuple-element.74), channel_id=1, source_target_pairs={{16,32},{32,16},{48,64},{64,48},{80,96},{96,80},{17,33},{33,17},{4... | collective-permute-start | bytes 393224 | tf_op jit(solution)/shard_map/ppermute | solution.py:415
where the time goes:
time: 124 us; the launch traced here: 126 us
  starting transfers between devices  37.6 us (30%)
  blocking collectives  31.4 us (25%)
  Pallas kernels  26.8 us (22%)
  waiting for transfers between devices  26.2 us (21%)
  local copies, waits for them, and re-layouts  2.67 us (2%)
    ppermute x14, starting transfers between devices, swapped(): return lax.ppermute(value, axis, route)  37.6 us
    all_gather x9, blocking collectives, paired(): return lax.all_gather(value, 'cols', axis_index_groups=groups)  31.4 us
    ppermute x14, waiting for transfers between devices, swapped(): return lax.ppermute(value, axis, route)  26.2 us
    pallas_call x11, Pallas kernels, whole(): pl.pallas_call(body, out_shape=outs, in_specs=[SMEM] * len(scalars) + [VM...  23.1 us
    pallas_call x1, Pallas kernels, prepare(): pl.pallas_call(prepare_body, out_shape=(shaped(slots, 2, half, size), sha...  3.74 us
    unnamed x22, local copies, waits for them, and re-layouts  2.49 us
  transfers between devices with their start and end apart: 14, of which 7 were waited for; matrix products, arithmetic and copies ran while one was open for 0% of the time, Pallas kernels for 6%

commit v1 on v0

--- a/solution.py
+++ b/solution.py
@@ -163,7 +163,7 @@
     else:
         near_r, near_i, far_strip, *refs = refs
     measured, rolled, fore_lane, fore_row, back_row, back_lane, twist_lane, twist_row, *refs = refs
-    out_r, out_i, out_b, in_a, in_b, field, sums = refs
+    out_r, out_i, out_b, sums, field = refs
     size = rolled.shape[2]
     half = size // 2
     extent = field.shape[2]
@@ -180,7 +180,7 @@
         field[near_at, :, middle] = near_edge[other]
         field[near_at, :, upper] = near_corner[other, 0]
         field[near_at, :, lower] = near_corner[other, 1]
-        field[far_at, :, middle] = jnp.where(info[4] == 1, 0.0, far_edge[odd_col])
+        field[far_at, :, middle] = far_edge[...]
         field[far_at, :, upper] = far_corner[0]
         field[far_at, :, lower] = far_corner[1]
     else:
@@ -280,8 +280,6 @@
     out_r[...] = sums[near_at, 0]
     out_i[...] = sums[near_at, 1]
     out_b[...] = sums[far_at]
-    in_a[...] = sums[a_at]
-    in_b[...] = sums[b_at]
 
 
 def gradient(first, info, positions, counts, ext, sides, measured, rolled, tables):
@@ -289,15 +287,15 @@
     plane, strip = shaped(extent, HALF), shaped(2, extent, HALF)
     return whole(
         functools.partial(gradient_body, first),
-        (plane, plane, strip, strip, strip),
+        (plane, plane, strip, shaped(4, 2, extent, HALF)),
         (info, positions, counts),
         (*ext, *sides, measured, rolled, *tables),
-        [pltpu.VMEM((4, 2, extent, HALF), jnp.float32)] * 2,
+        [pltpu.VMEM((4, 2, extent, HALF), jnp.float32)],
         flops=6 * 8 * 3 * 2**25,
     )
 
 
-def extend_body(info, tile, halo_a, halo_b, near, far, ext_r, ext_i, ext_b, corner_a, corner_b):
+def extend_body(info, tile, halo_a, halo_b, near, ext_r, ext_i, ext_b, corner_a, corner_b):
     size = tile.shape[1]
     odd_row, odd_col = info[0], info[1]
 
@@ -334,15 +332,16 @@
     out_b[...] = total[:, pl.ds(pl.multiple_of(odd_row * (extent - width), 8), width), :]
 
 
-def join_near_body(width, info, inner, near_r, near_i, total, out_a, out_b):
+def join_near_body(width, info, sums, near_r, near_i, total, out_a, out_b):
     other = 1 - info[1]
-    total[0] = inner[0] + near_r[other]
-    total[1] = inner[1] + near_i[other]
+    block = places(info[1])[1]
+    total[0] = sums[block, 0] + near_r[other]
+    total[1] = sums[block, 1] + near_i[other]
     outgoing(info[0], total, width, out_a, out_b)
 
 
-def join_far_body(width, info, inner, strip, total, out_a, out_b):
-    total[...] = inner[...] + strip[...]
+def join_far_body(width, info, sums, strip, total, out_a, out_b):
+    total[...] = sums[places(info[1])[2]] + strip[...]
     outgoing(info[0], total, width, out_a, out_b)
 
 
@@ -415,9 +414,8 @@
     return lax.ppermute(value, axis, route)
 
 
-def paired(value, first=0):
-    count = lax.axis_size("cols")
-    groups = [[i, (i + 1) % count] for i in range(first, count, 2)]
+def paired(value):
+    groups = [[i, i + 1] for i in range(0, lax.axis_size("cols"), 2)]
     return lax.all_gather(value, "cols", axis_index_groups=groups)
 
 
@@ -425,14 +423,14 @@
     return swapped(edge_a, "rows", 0), swapped(edge_b, "rows", 1)
 
 
-def summed(info, width, out_r, out_i, out_b, in_a, in_b):
-    extent = in_a.shape[1]
+def summed(info, width, out_r, out_i, out_b, sums):
+    extent = sums.shape[2]
     strip, piece = shaped(2, extent, HALF), shaped(2, width, HALF)
     far = swapped(out_b, "cols", 1)
     near = paired(out_r), paired(out_i)
-    total_a, *edges = whole(functools.partial(join_near_body, width), (strip, piece, piece), (info,), (in_a, *near))
+    total_a, *edges = whole(functools.partial(join_near_body, width), (strip, piece, piece), (info,), (sums, *near))
     halos_a = both_rows(*edges)
-    total_b, *edges = whole(functools.partial(join_far_body, width), (strip, piece, piece), (info,), (in_b, far))
+    total_b, *edges = whole(functools.partial(join_far_body, width), (strip, piece, piece), (info,), (sums, far))
     halos_b = both_rows(*edges)
     return total_a, halos_a, total_b, halos_b
 
@@ -442,10 +440,8 @@
     tile = object_field.shape[1]
     extent = tile + 2 * MARGIN
     row, col = lax.axis_index("rows"), lax.axis_index("cols")
-    last, end = lax.axis_size("rows") - 1, lax.axis_size("cols") - 1
-    info = jnp.stack(
-        [row % 2, col % 2, row == 0, row == last, (col == 0) | (col == end)]
-    ).astype(jnp.int32)
+    last = lax.axis_size("rows") - 1
+    info = jnp.stack([row % 2, col % 2, row == 0, row == last]).astype(jnp.int32)
     tables = constants(size)
     order = jnp.asarray(split_order(size)).astype(jnp.bfloat16)
     positions, intensity = positions[0, 0], intensity[0, 0]
@@ -455,13 +451,13 @@
     edge, side = shaped(2, MARGIN, tile), shaped(2, tile, MARGIN)
     edge_a, edge_b, side_a, side_b = whole(cut_body, (edge, edge, side, side), (info,), (object_field,))
     halos = both_rows(edge_a, edge_b)
-    far_edge, near_edge = paired(side_b, 1), paired(side_a)
+    far_edge, near_edge = swapped(side_b, "cols", 1), paired(side_a)
     *ext, corner_a, corner_b = whole(
         extend_body,
         (plane, plane, strip, corner, corner),
         (info,),
         (object_field, *halos),
-        unread=(near_edge, far_edge),
+        unread=(near_edge,),
     )
     measured, rolled = prepare(positions, intensity, probe, order, corner_a)
     far_corner = swapped(corner_b, "cols", 1)

time: 124 us -> 122 us (0.984); the launches traced: 126 us -> 121 us
  starting transfers between devices: 37.6 us -> 51.9 us
  blocking collectives: 31.4 us -> 17.4 us
  Pallas kernels: 26.8 us -> 23.7 us
  waiting for transfers between devices: 26.2 us -> 24.6 us
    ppermute x14 -> x15, starting transfers between devices: 37.6 us -> 51.9 us  [swapped(): return lax.ppermute(value, axis, route)]
    all_gather x9 -> x8, blocking collectives: 31.4 us -> 17.4 us  [paired(): return lax.all_gather(value, 'cols', axis_index_groups=groups)]
    pallas_call x11, Pallas kernels: 23.1 us -> 20 us  [whole(): pl.pallas_call(body, out_shape=outs, in_specs=[SMEM] * len(scalars) + [VM...]
    ppermute x14 -> x15, waiting for transfers between devices: 26.2 us -> 24.6 us  [swapped(): return lax.ppermute(value, axis, route)]
  transfers between devices with their start and end apart: 14 -> 15, of which waited for: 7 -> 8; matrix products, arithmetic and copies ran while one was open for 0% -> 0% of each run, Pallas kernels for 6% -> 7%
where the time goes in v1:
time: 122 us; the launch traced here: 121 us
  starting transfers between devices  51.9 us (43%)
  waiting for transfers between devices  24.6 us (20%)
  Pallas kernels  23.7 us (19%)
  blocking collectives  17.4 us (14%)
  local copies, waits for them, and re-layouts  2.21 us (2%)
    ppermute x15, starting transfers between devices, swapped(): return lax.ppermute(value, axis, route)  51.9 us
    ppermute x15, waiting for transfers between devices, swapped(): return lax.ppermute(value, axis, route)  24.6 us
    pallas_call x11, Pallas kernels, whole(): pl.pallas_call(body, out_shape=outs, in_specs=[SMEM] * len(scalars) + [VM...  20 us
    all_gather x8, blocking collectives, paired(): return lax.all_gather(value, 'cols', axis_index_groups=groups)  17.4 us
    pallas_call x1, Pallas kernels, prepare(): pl.pallas_call(prepare_body, out_shape=(shaped(slots, 2, half, size), sha...  3.75 us
  transfers between devices with their start and end apart: 15, of which 8 were waited for; matrix products, arithmetic and copies ran while one was open for 0% of the time, Pallas kernels for 7%

profile of v1, /device:TPU:10, one launch (start us, length us, event | category | flops | bytes accessed | tf_op | source)
XLA Modules:
  0.0 120.8 jit_solution(8100264432179878893)
XLA Ops:
  2.4 2.1 %collective-permute-start = (f32[2,128,256]{2,1,0:T(8,128)S(1)}, f32[2,128,256]{2,1,0:T(8,128)S(1)}, u32[]{:S(2)}, u32[]{:S(2)}) collective-permute-start(f32[2,128,256]{2,1,0:T(8,128)S(1)} %get-tuple-element.38), channel_id=1, source_target_pairs={{0,16},{16,0},{32,48},{48,32},{64,80},{80,64},{96,112},{112,96},{1... | collective-permute-start | bytes 786440 | tf_op jit(solution)/shard_map/ppermute | solution.py:414
  4.6 3.2 %collective-permute-start.1 = (f32[2,128,256]{2,1,0:T(8,128)S(1)}, f32[2,128,256]{2,1,0:T(8,128)S(1)}, u32[]{:S(2)}, u32[]{:S(2)}) collective-permute-start(f32[2,128,256]{2,1,0:T(8,128)S(1)} %get-tuple-element.39), channel_id=1, source_target_pairs={{16,32},{32,16},{48,64},{64,48},{80,96},{96,80},{17,33},{33,17},{4... | collective-permute-start | bytes 786440 | tf_op jit(solution)/shard_map/ppermute | solution.py:414
  7.8 4.8 %collective-permute-start.2 = (f32[2,256,128]{2,1,0:T(8,128)}, f32[2,256,128]{2,1,0:T(8,128)}, u32[]{:S(2)}, u32[]{:S(2)}) collective-permute-start(f32[2,256,128]{2,1,0:T(8,128)} %get-tuple-element.45), channel_id=1, source_target_pairs={{1,2},{2,1},{3,4},{4,3},{5,6},{6,5},{7,8},{8,7},{9,10},{10,9},{11,... | collective-permute-start | bytes 786440 | tf_op jit(solution)/shard_map/ppermute | solution.py:414
  12.6 2.2 %all-gather = f32[4,256,128]{2,1,0:T(8,128)S(1)} all-gather(f32[2,256,128]{2,1,0:T(8,128)S(1)} %get-tuple-element.40), channel_id=2, replica_groups={{0,1},{2,3},{4,5},{6,7},{8,9},{10,11},{12,13},{14,15},{16,17},{18,19},{..., dimensions={0}, use_global_device_ids=true | all-gather | bytes 786432 | tf_op jit(solution)/shard_map/all_gather | solution.py:419
  14.8 2.7 %collective-permute-done.1.halo_b = f32[2,128,256]{2,1,0:T(8,128)S(1)} collective-permute-done((f32[2,128,256]{2,1,0:T(8,128)S(1)}, f32[2,128,256]{2,1,0:T(8,128)S(1)}, u32[]{:S(2)}, u32[]{:S(2)}) %collective-permute-start.1) | collective-permute-done | bytes 262176 | tf_op jit(solution)/shard_map/ppermute | solution.py:414
  18.9 4.3 %collective-permute-start.3 = (f32[2,2,128,128]{3,2,1,0:T(8,128)}, f32[2,2,128,128]{3,2,1,0:T(8,128)}, u32[]{:S(2)}, u32[]{:S(2)}) collective-permute-start(f32[2,2,128,128]{3,2,1,0:T(8,128)} %get-tuple-element.46), channel_id=1, source_target_pairs={{1,2},{2,1},{3,4},{4,3},{5,6},{6,5},{7,8},{8,7},{9,10},{10,9},{11,... | collective-permute-start | bytes 786440 | tf_op jit(solution)/shard_map/ppermute | solution.py:414
  25.0 3.7 %shard_map.120 = (f32[6,2,128,256]{3,2,1,0:T(8,128)S(1)}, f32[6,2,256,256]{3,2,1,0:T(8,128)S(1)}) custom-call(s32[6,2]{1,0:T(8,128)S(1)} %copy.17.positions, s32[6,256,256]{2,1,0:T(8,128)S(1)} %bitcast.23, f32[2,256,256]{2,1,0:T(8,128)S(1)} %copy-done.2, bf16[256,256]{1,0:T(8,128)(2,1)S(1)} %copy-done.8, f32[2,2,128,128]{3,2,1,0:T(8,128)S(1)} %get-tuple-element.44.earlier), custom_call_target="tpu_custom_call" | custom-call | flops 805306368 | bytes 8388608 | tf_op jit(solution)/shard_map/pallas_call | solution.py:117
  28.8 2.2 %all-gather.1 = f32[4,2,128,128]{3,2,1,0:T(8,128)S(1)} all-gather(f32[2,2,128,128]{3,2,1,0:T(8,128)S(1)} %get-tuple-element.44.earlier), channel_id=3, replica_groups={{0,1},{2,3},{4,5},{6,7},{8,9},{10,11},{12,13},{14,15},{16,17},{18,19},{..., dimensions={0}, use_global_device_ids=true | all-gather | bytes 786432 | tf_op jit(solution)/shard_map/all_gather | solution.py:419
  31.0 6.2 %shard_map.121 = (f32[512,128]{1,0:T(8,128)S(1)}, f32[512,128]{1,0:T(8,128)S(1)}, f32[2,512,128]{2,1,0:T(8,128)S(1)}, f32[4,2,512,128]{3,2,1,0:T(8,128)S(1)}) custom-call(s32[4]{0:T(128)S(1)} %pad_add_fusion.info, s32[6,2]{1,0:T(8,128)S(1)} %copy.17.positions, s32[1,1]{1,0:T(1,128)S(6)} %copy.19.counts, f32[512,128]{1,0:T(8,128)S(1)} %get-tuple-element.41.ext_r, ...), custom_call_target="tpu_custom_call" | custom-call | flops 4831838208 | bytes 8388608 | tf_op jit(solution)/shard_map/pallas_call | solution.py:49
  37.2 7.3 %collective-permute-start.6 = (f32[2,512,128]{2,1,0:T(8,128)S(1)}, f32[2,512,128]{2,1,0:T(8,128)S(1)}, u32[]{:S(2)}, u32[]{:S(2)}) collective-permute-start(f32[2,512,128]{2,1,0:T(8,128)S(1)} %get-tuple-element.57), channel_id=1, source_target_pairs={{1,2},{2,1},{3,4},{4,3},{5,6},{6,5},{7,8},{8,7},{9,10},{10,9},{11,... | collective-permute-start | bytes 1572872 | tf_op jit(solution)/shard_map/ppermute | solution.py:414
  44.5 6.8 %collective-permute-done.6.strip = f32[2,512,128]{2,1,0:T(8,128)S(1)} collective-permute-done((f32[2,512,128]{2,1,0:T(8,128)S(1)}, f32[2,512,128]{2,1,0:T(8,128)S(1)}, u32[]{:S(2)}, u32[]{:S(2)}) %collective-permute-start.6) | collective-permute-done | bytes 524320 | tf_op jit(solution)/shard_map/ppermute | solution.py:414
  52.0 3.3 %collective-permute-start.7 = (f32[2,256,128]{2,1,0:T(8,128)S(1)}, f32[2,256,128]{2,1,0:T(8,128)S(1)}, u32[]{:S(2)}, u32[]{:S(2)}) collective-permute-start(f32[2,256,128]{2,1,0:T(8,128)S(1)} %get-tuple-element.59), channel_id=1, source_target_pairs={{0,16},{16,0},{32,48},{48,32},{64,80},{80,64},{96,112},{112,96},{1... | collective-permute-start | bytes 786440 | tf_op jit(solution)/shard_map/ppermute | solution.py:414
  55.3 3.3 %collective-permute-start.8 = (f32[2,256,128]{2,1,0:T(8,128)S(1)}, f32[2,256,128]{2,1,0:T(8,128)S(1)}, u32[]{:S(2)}, u32[]{:S(2)}) collective-permute-start(f32[2,256,128]{2,1,0:T(8,128)S(1)} %get-tuple-element.60), channel_id=1, source_target_pairs={{16,32},{32,16},{48,64},{64,48},{80,96},{96,80},{17,33},{33,17},{4... | collective-permute-start | bytes 786440 | tf_op jit(solution)/shard_map/ppermute | solution.py:414
  58.6 2.2 %all-gather.2 = f32[1024,128]{1,0:T(8,128)S(1)} all-gather(f32[512,128]{1,0:T(8,128)S(1)} %get-tuple-element.50), channel_id=4, replica_groups={{0,1},{2,3},{4,5},{6,7},{8,9},{10,11},{12,13},{14,15},{16,17},{18,19},{..., dimensions={0}, use_global_device_ids=true | all-gather | bytes 786432 | tf_op jit(solution)/shard_map/all_gather | solution.py:419
  60.8 2.2 %all-gather.3 = f32[1024,128]{1,0:T(8,128)S(1)} all-gather(f32[512,128]{1,0:T(8,128)S(1)} %get-tuple-element.51), channel_id=5, replica_groups={{0,1},{2,3},{4,5},{6,7},{8,9},{10,11},{12,13},{14,15},{16,17},{18,19},{..., dimensions={0}, use_global_device_ids=true | all-gather | bytes 786432 | tf_op jit(solution)/shard_map/all_gather | solution.py:419
  63.6 3.0 %collective-permute-start.4 = (f32[2,256,128]{2,1,0:T(8,128)S(1)}, f32[2,256,128]{2,1,0:T(8,128)S(1)}, u32[]{:S(2)}, u32[]{:S(2)}) collective-permute-start(f32[2,256,128]{2,1,0:T(8,128)S(1)} %get-tuple-element.53), channel_id=1, source_target_pairs={{0,16},{16,0},{32,48},{48,32},{64,80},{80,64},{96,112},{112,96},{1... | collective-permute-start | bytes 786440 | tf_op jit(solution)/shard_map/ppermute | solution.py:414
  66.6 2.1 %collective-permute-start.5 = (f32[2,256,128]{2,1,0:T(8,128)S(1)}, f32[2,256,128]{2,1,0:T(8,128)S(1)}, u32[]{:S(2)}, u32[]{:S(2)}) collective-permute-start(f32[2,256,128]{2,1,0:T(8,128)S(1)} %get-tuple-element.54), channel_id=1, source_target_pairs={{16,32},{32,16},{48,64},{64,48},{80,96},{96,80},{17,33},{33,17},{4... | collective-permute-start | bytes 786440 | tf_op jit(solution)/shard_map/ppermute | solution.py:414
  69.4 5.5 %collective-permute-start.9 = (f32[2,512,128]{2,1,0:T(8,128)S(1)}, f32[2,512,128]{2,1,0:T(8,128)S(1)}, u32[]{:S(2)}, u32[]{:S(2)}) collective-permute-start(f32[2,512,128]{2,1,0:T(8,128)S(1)} %shard_map.125.ext_b), channel_id=1, source_target_pairs={{1,2},{2,1},{3,4},{4,3},{5,6},{6,5},{7,8},{8,7},{9,10},{10,9},{11,... | collective-permute-start | bytes 1572872 | tf_op jit(solution)/shard_map/ppermute | solution.py:414
  74.9 4.1 %collective-permute-done.5.halo_b = f32[2,256,128]{2,1,0:T(8,128)S(1)} collective-permute-done((f32[2,256,128]{2,1,0:T(8,128)S(1)}, f32[2,256,128]{2,1,0:T(8,128)S(1)}, u32[]{:S(2)}, u32[]{:S(2)}) %collective-permute-start.5) | collective-permute-done | bytes 262176 | tf_op jit(solution)/shard_map/ppermute | solution.py:414
  79.7 2.2 %all-gather.4 = f32[1024,128]{1,0:T(8,128)S(1)} all-gather(f32[512,128]{1,0:T(8,128)S(1)} %get-tuple-element.55.ext_r), channel_id=6, replica_groups={{0,1},{2,3},{4,5},{6,7},{8,9},{10,11},{12,13},{14,15},{16,17},{18,19},{..., dimensions={0}, use_global_device_ids=true | all-gather | bytes 786432 | tf_op jit(solution)/shard_map/all_gather | solution.py:419
  81.8 2.2 %all-gather.5 = f32[1024,128]{1,0:T(8,128)S(1)} all-gather(f32[512,128]{1,0:T(8,128)S(1)} %get-tuple-element.56.ext_i), channel_id=7, replica_groups={{0,1},{2,3},{4,5},{6,7},{8,9},{10,11},{12,13},{14,15},{16,17},{18,19},{..., dimensions={0}, use_global_device_ids=true | all-gather | bytes 786432 | tf_op jit(solution)/shard_map/all_gather | solution.py:419
  84.0 4.3 %collective-permute-done.9.refs_2_ = f32[2,512,128]{2,1,0:T(8,128)S(1)} collective-permute-done((f32[2,512,128]{2,1,0:T(8,128)S(1)}, f32[2,512,128]{2,1,0:T(8,128)S(1)}, u32[]{:S(2)}, u32[]{:S(2)}) %collective-permute-start.9) | collective-permute-done | bytes 524320 | tf_op jit(solution)/shard_map/ppermute | solution.py:414
  88.3 5.7 %shard_map.126 = (f32[512,128]{1,0:T(8,128)S(1)}, f32[512,128]{1,0:T(8,128)S(1)}, f32[2,512,128]{2,1,0:T(8,128)S(1)}, f32[4,2,512,128]{3,2,1,0:T(8,128)S(1)}) custom-call(s32[4]{0:T(128)S(1)} %pad_add_fusion.info, s32[6,2]{1,0:T(8,128)S(1)} %copy.17.positions, s32[1,1]{1,0:T(1,128)S(6)} %copy.19.counts, f32[512,128]{1,0:T(8,128)S(1)} %get-tuple-element.55.ext_r, ...), custom_call_target="tpu_custom_call" | custom-call | flops 4831838208 | bytes 8388608 | tf_op jit(solution)/shard_map/pallas_call | solution.py:49
  94.0 4.8 %collective-permute-start.10 = (f32[2,512,128]{2,1,0:T(8,128)S(1)}, f32[2,512,128]{2,1,0:T(8,128)S(1)}, u32[]{:S(2)}, u32[]{:S(2)}) collective-permute-start(f32[2,512,128]{2,1,0:T(8,128)S(1)} %get-tuple-element.65), channel_id=1, source_target_pairs={{1,2},{2,1},{3,4},{4,3},{5,6},{6,5},{7,8},{8,7},{9,10},{10,9},{11,... | collective-permute-start | bytes 1572872 | tf_op jit(solution)/shard_map/ppermute | solution.py:414
  98.8 2.2 %all-gather.6 = f32[1024,128]{1,0:T(8,128)S(1)} all-gather(f32[512,128]{1,0:T(8,128)S(1)} %get-tuple-element.62), channel_id=8, replica_groups={{0,1},{2,3},{4,5},{6,7},{8,9},{10,11},{12,13},{14,15},{16,17},{18,19},{..., dimensions={0}, use_global_device_ids=true | all-gather | bytes 786432 | tf_op jit(solution)/shard_map/all_gather | solution.py:419
  101.0 2.2 %all-gather.7 = f32[1024,128]{1,0:T(8,128)S(1)} all-gather(f32[512,128]{1,0:T(8,128)S(1)} %get-tuple-element.63), channel_id=9, replica_groups={{0,1},{2,3},{4,5},{6,7},{8,9},{10,11},{12,13},{14,15},{16,17},{18,19},{..., dimensions={0}, use_global_device_ids=true | all-gather | bytes 786432 | tf_op jit(solution)/shard_map/all_gather | solution.py:419
  103.9 2.6 %collective-permute-start.12 = (f32[2,128,128]{2,1,0:T(8,128)S(1)}, f32[2,128,128]{2,1,0:T(8,128)S(1)}, u32[]{:S(2)}, u32[]{:S(2)}) collective-permute-start(f32[2,128,128]{2,1,0:T(8,128)S(1)} %get-tuple-element.68), channel_id=1, source_target_pairs={{16,32},{32,16},{48,64},{64,48},{80,96},{96,80},{17,33},{33,17},{4... | collective-permute-start | bytes 393224 | tf_op jit(solution)/shard_map/ppermute | solution.py:414
  107.3 2.8 %collective-permute-start.13 = (f32[2,128,128]{2,1,0:T(8,128)S(1)}, f32[2,128,128]{2,1,0:T(8,128)S(1)}, u32[]{:S(2)}, u32[]{:S(2)}) collective-permute-start(f32[2,128,128]{2,1,0:T(8,128)S(1)} %get-tuple-element.69), channel_id=1, source_target_pairs={{0,16},{16,0},{32,48},{48,32},{64,80},{80,64},{96,112},{112,96},{1... | collective-permute-start | bytes 393224 | tf_op jit(solution)/shard_map/ppermute | solution.py:414
  110.0 2.8 %collective-permute-start.14 = (f32[2,128,128]{2,1,0:T(8,128)S(1)}, f32[2,128,128]{2,1,0:T(8,128)S(1)}, u32[]{:S(2)}, u32[]{:S(2)}) collective-permute-start(f32[2,128,128]{2,1,0:T(8,128)S(1)} %get-tuple-element.70), channel_id=1, source_target_pairs={{16,32},{32,16},{48,64},{64,48},{80,96},{96,80},{17,33},{33,17},{4... | collective-permute-start | bytes 393224 | tf_op jit(solution)/shard_map/ppermute | solution.py:414
  112.9 1.6 %collective-permute-done.12.near_b = f32[2,128,128]{2,1,0:T(8,128)S(1)} collective-permute-done((f32[2,128,128]{2,1,0:T(8,128)S(1)}, f32[2,128,128]{2,1,0:T(8,128)S(1)}, u32[]{:S(2)}, u32[]{:S(2)}) %collective-permute-start.12) | collective-permute-done | bytes 131104 | tf_op jit(solution)/shard_map/ppermute | solution.py:414
  114.5 2.0 %collective-permute-done.13.far_a = f32[2,128,128]{2,1,0:T(8,128)S(1)} collective-permute-done((f32[2,128,128]{2,1,0:T(8,128)S(1)}, f32[2,128,128]{2,1,0:T(8,128)S(1)}, u32[]{:S(2)}, u32[]{:S(2)}) %collective-permute-start.13) | collective-permute-done | bytes 131104 | tf_op jit(solution)/shard_map/ppermute | solution.py:414
  116.5 2.8 %collective-permute-done.14.far_b = f32[2,128,128]{2,1,0:T(8,128)S(1)} collective-permute-done((f32[2,128,128]{2,1,0:T(8,128)S(1)}, f32[2,128,128]{2,1,0:T(8,128)S(1)}, u32[]{:S(2)}, u32[]{:S(2)}) %collective-permute-start.14) | collective-permute-done | bytes 131104 | tf_op jit(solution)/shard_map/ppermute | solution.py:414
  (42 shorter events, 10.6 us)
Async XLA Ops:
  0.0 23.8 %copy-start.10 = (s32[1,1,6,2]{2,3,1,0:T(2,128)S(1)}, s32[1,1,6,2]{2,3,1,0:T(2,128)}, u32[]{:S(2)}) copy-start(s32[1,1,6,2]{2,3,1,0:T(2,128)} %param.14) | copy-start | bytes 148
  0.1 1.0 copy-start
  1.1 22.8 %copy-start.1 = (s32[1,1,6,256,256]{4,3,2,1,0:T(8,128)S(1)}, s32[1,1,6,256,256]{4,3,2,1,0:T(8,128)}, u32[]{:S(2)}) copy-start(s32[1,1,6,256,256]{4,3,2,1,0:T(8,128)} %param.16) | copy-start | bytes 4718596
  1.1 22.8 %copy-start.8 = (bf16[256,256]{1,0:T(8,128)(2,1)S(1)}, bf16[256,256]{1,0:T(8,128)(2,1)}, u32[]{:S(2)}) copy-start(bf16[256,256]{1,0:T(8,128)(2,1)} %constant.53.order) | copy-start | bytes 393220
  2.4 12.3 %collective-permute-start = (f32[2,128,256]{2,1,0:T(8,128)S(1)}, f32[2,128,256]{2,1,0:T(8,128)S(1)}, u32[]{:S(2)}, u32[]{:S(2)}) collective-permute-start(f32[2,128,256]{2,1,0:T(8,128)S(1)} %get-tuple-element.38), channel_id=1, source_target_pairs={{0,16},{16,0},{32,48},{48,32},{64,80},{80,64},{96,112},{112,96},{1... | collective-permute-start | bytes 786440 | tf_op jit(solution)/shard_map/ppermute | solution.py:414
  4.6 12.9 %collective-permute-start.1 = (f32[2,128,256]{2,1,0:T(8,128)S(1)}, f32[2,128,256]{2,1,0:T(8,128)S(1)}, u32[]{:S(2)}, u32[]{:S(2)}) collective-permute-start(f32[2,128,256]{2,1,0:T(8,128)S(1)} %get-tuple-element.39), channel_id=1, source_target_pairs={{16,32},{32,16},{48,64},{64,48},{80,96},{96,80},{17,33},{33,17},{4... | collective-permute-start | bytes 786440 | tf_op jit(solution)/shard_map/ppermute | solution.py:414
  7.8 23.2 %collective-permute-start.2 = (f32[2,256,128]{2,1,0:T(8,128)}, f32[2,256,128]{2,1,0:T(8,128)}, u32[]{:S(2)}, u32[]{:S(2)}) collective-permute-start(f32[2,256,128]{2,1,0:T(8,128)} %get-tuple-element.45), channel_id=1, source_target_pairs={{1,2},{2,1},{3,4},{4,3},{5,6},{6,5},{7,8},{8,7},{9,10},{10,9},{11,... | collective-permute-start | bytes 786440 | tf_op jit(solution)/shard_map/ppermute | solution.py:414
  18.9 12.1 %copy-start.9 = (f32[2,1,128]{2,1,0:T(1,128)S(1)}, f32[2,1,128]{2,1,0:T(1,128)}, u32[]{:S(2)}) copy-start(f32[2,1,128]{2,1,0:T(1,128)} %constant.47.clone.refs_10_.refs_9_) | copy-start | bytes 3076
  18.9 12.1 %collective-permute-start.3 = (f32[2,2,128,128]{3,2,1,0:T(8,128)}, f32[2,2,128,128]{3,2,1,0:T(8,128)}, u32[]{:S(2)}, u32[]{:S(2)}) collective-permute-start(f32[2,2,128,128]{3,2,1,0:T(8,128)} %get-tuple-element.46), channel_id=1, source_target_pairs={{1,2},{2,1},{3,4},{4,3},{5,6},{6,5},{7,8},{8,7},{9,10},{10,9},{11,... | collective-permute-start | bytes 786440 | tf_op jit(solution)/shard_map/ppermute | solution.py:414
  23.9 1.0 copy-start.2
  25.0 6.0 %copy-start.3 = (bf16[768,256]{1,0:T(8,128)(2,1)S(1)}, bf16[768,256]{1,0:T(8,128)(2,1)}, u32[]{:S(2)}) copy-start(bf16[768,256]{1,0:T(8,128)(2,1)} %constant.46.clone.refs_9_.refs_8_) | copy-start | bytes 1179652
  25.0 6.0 %copy-start.4 = (bf16[256,768]{1,0:T(8,128)(2,1)S(1)}, bf16[256,768]{1,0:T(8,128)(2,1)}, u32[]{:S(2)}) copy-start(bf16[256,768]{1,0:T(8,128)(2,1)} %constant.45.clone.refs_7_.refs_6_) | copy-start | bytes 1179652
  25.0 6.0 %copy-start.5 = (bf16[256,768]{1,0:T(8,128)(2,1)S(1)}, bf16[256,768]{1,0:T(8,128)(2,1)}, u32[]{:S(2)}) copy-start(bf16[256,768]{1,0:T(8,128)(2,1)} %constant.44.clone.refs_8_.refs_7_) | copy-start | bytes 1179652
  25.0 6.0 %copy-start.6 = (bf16[768,256]{1,0:T(8,128)(2,1)S(1)}, bf16[768,256]{1,0:T(8,128)(2,1)}, u32[]{:S(2)}) copy-start(bf16[768,256]{1,0:T(8,128)(2,1)} %constant.43.clone.refs_6_.refs_5_) | copy-start | bytes 1179652
  25.0 6.0 %copy-start.7 = (f32[2,128,256]{2,1,0:T(8,128)S(1)}, f32[2,128,256]{2,1,0:T(8,128)}, u32[]{:S(2)}) copy-start(f32[2,128,256]{2,1,0:T(8,128)} %constant.48.clone.refs_11_.refs_10_) | copy-start | bytes 786436
  37.2 14.1 %collective-permute-start.6 = (f32[2,512,128]{2,1,0:T(8,128)S(1)}, f32[2,512,128]{2,1,0:T(8,128)S(1)}, u32[]{:S(2)}, u32[]{:S(2)}) collective-permute-start(f32[2,512,128]{2,1,0:T(8,128)S(1)} %get-tuple-element.57), channel_id=1, source_target_pairs={{1,2},{2,1},{3,4},{4,3},{5,6},{6,5},{7,8},{8,7},{9,10},{10,9},{11,... | collective-permute-start | bytes 1572872 | tf_op jit(solution)/shard_map/ppermute | solution.py:414
  52.0 16.7 %collective-permute-start.7 = (f32[2,256,128]{2,1,0:T(8,128)S(1)}, f32[2,256,128]{2,1,0:T(8,128)S(1)}, u32[]{:S(2)}, u32[]{:S(2)}) collective-permute-start(f32[2,256,128]{2,1,0:T(8,128)S(1)} %get-tuple-element.59), channel_id=1, source_target_pairs={{0,16},{16,0},{32,48},{48,32},{64,80},{80,64},{96,112},{112,96},{1... | collective-permute-start | bytes 786440 | tf_op jit(solution)/shard_map/ppermute | solution.py:414
  55.3 13.4 %collective-permute-start.8 = (f32[2,256,128]{2,1,0:T(8,128)S(1)}, f32[2,256,128]{2,1,0:T(8,128)S(1)}, u32[]{:S(2)}, u32[]{:S(2)}) collective-permute-start(f32[2,256,128]{2,1,0:T(8,128)S(1)} %get-tuple-element.60), channel_id=1, source_target_pairs={{16,32},{32,16},{48,64},{64,48},{80,96},{96,80},{17,33},{33,17},{4... | collective-permute-start | bytes 786440 | tf_op jit(solution)/shard_map/ppermute | solution.py:414
  63.6 11.3 %collective-permute-start.4 = (f32[2,256,128]{2,1,0:T(8,128)S(1)}, f32[2,256,128]{2,1,0:T(8,128)S(1)}, u32[]{:S(2)}, u32[]{:S(2)}) collective-permute-start(f32[2,256,128]{2,1,0:T(8,128)S(1)} %get-tuple-element.53), channel_id=1, source_target_pairs={{0,16},{16,0},{32,48},{48,32},{64,80},{80,64},{96,112},{112,96},{1... | collective-permute-start | bytes 786440 | tf_op jit(solution)/shard_map/ppermute | solution.py:414
  66.6 12.4 %collective-permute-start.5 = (f32[2,256,128]{2,1,0:T(8,128)S(1)}, f32[2,256,128]{2,1,0:T(8,128)S(1)}, u32[]{:S(2)}, u32[]{:S(2)}) collective-permute-start(f32[2,256,128]{2,1,0:T(8,128)S(1)} %get-tuple-element.54), channel_id=1, source_target_pairs={{16,32},{32,16},{48,64},{64,48},{80,96},{96,80},{17,33},{33,17},{4... | collective-permute-start | bytes 786440 | tf_op jit(solution)/shard_map/ppermute | solution.py:414
  69.4 18.9 %collective-permute-start.9 = (f32[2,512,128]{2,1,0:T(8,128)S(1)}, f32[2,512,128]{2,1,0:T(8,128)S(1)}, u32[]{:S(2)}, u32[]{:S(2)}) collective-permute-start(f32[2,512,128]{2,1,0:T(8,128)S(1)} %shard_map.125.ext_b), channel_id=1, source_target_pairs={{1,2},{2,1},{3,4},{4,3},{5,6},{6,5},{7,8},{8,7},{9,10},{10,9},{11,... | collective-permute-start | bytes 1572872 | tf_op jit(solution)/shard_map/ppermute | solution.py:414
  94.0 12.6 %collective-permute-start.10 = (f32[2,512,128]{2,1,0:T(8,128)S(1)}, f32[2,512,128]{2,1,0:T(8,128)S(1)}, u32[]{:S(2)}, u32[]{:S(2)}) collective-permute-start(f32[2,512,128]{2,1,0:T(8,128)S(1)} %get-tuple-element.65), channel_id=1, source_target_pairs={{1,2},{2,1},{3,4},{4,3},{5,6},{6,5},{7,8},{8,7},{9,10},{10,9},{11,... | collective-permute-start | bytes 1572872 | tf_op jit(solution)/shard_map/ppermute | solution.py:414
  103.8 9.1 %collective-permute-start.11 = (f32[2,128,128]{2,1,0:T(8,128)S(1)}, f32[2,128,128]{2,1,0:T(8,128)S(1)}, u32[]{:S(2)}, u32[]{:S(2)}) collective-permute-start(f32[2,128,128]{2,1,0:T(8,128)S(1)} %get-tuple-element.67), channel_id=1, source_target_pairs={{0,16},{16,0},{32,48},{48,32},{64,80},{80,64},{96,112},{112,96},{1... | collective-permute-start | bytes 393224 | tf_op jit(solution)/shard_map/ppermute | solution.py:414
  103.9 10.6 %collective-permute-start.12 = (f32[2,128,128]{2,1,0:T(8,128)S(1)}, f32[2,128,128]{2,1,0:T(8,128)S(1)}, u32[]{:S(2)}, u32[]{:S(2)}) collective-permute-start(f32[2,128,128]{2,1,0:T(8,128)S(1)} %get-tuple-element.68), channel_id=1, source_target_pairs={{16,32},{32,16},{48,64},{64,48},{80,96},{96,80},{17,33},{33,17},{4... | collective-permute-start | bytes 393224 | tf_op jit(solution)/shard_map/ppermute | solution.py:414
  107.3 9.3 %collective-permute-start.13 = (f32[2,128,128]{2,1,0:T(8,128)S(1)}, f32[2,128,128]{2,1,0:T(8,128)S(1)}, u32[]{:S(2)}, u32[]{:S(2)}) collective-permute-start(f32[2,128,128]{2,1,0:T(8,128)S(1)} %get-tuple-element.69), channel_id=1, source_target_pairs={{0,16},{16,0},{32,48},{48,32},{64,80},{80,64},{96,112},{112,96},{1... | collective-permute-start | bytes 393224 | tf_op jit(solution)/shard_map/ppermute | solution.py:414
  110.0 9.3 %collective-permute-start.14 = (f32[2,128,128]{2,1,0:T(8,128)S(1)}, f32[2,128,128]{2,1,0:T(8,128)S(1)}, u32[]{:S(2)}, u32[]{:S(2)}) collective-permute-start(f32[2,128,128]{2,1,0:T(8,128)S(1)} %get-tuple-element.70), channel_id=1, source_target_pairs={{16,32},{32,16},{48,64},{64,48},{80,96},{96,80},{17,33},{33,17},{4... | collective-permute-start | bytes 393224 | tf_op jit(solution)/shard_map/ppermute | solution.py:414

commit v2 on v0

--- a/solution.py
+++ b/solution.py
@@ -30,12 +30,6 @@
     return mixed, twiddle
 
 
-def split_order(length):
-    half = length // 2
-    order = np.concatenate([np.arange(half) * 2, np.arange(half) * 2 + 1])
-    return (np.arange(length)[:, None] == order[None, :]).astype(np.float32)
-
-
 VMEM = pl.BlockSpec(memory_space=pltpu.VMEM)
 SMEM = pl.BlockSpec(memory_space=pltpu.SMEM)
 ANY = pl.BlockSpec(memory_space=pl.ANY)
@@ -45,7 +39,7 @@
     return jax.ShapeDtypeStruct(dims, jnp.float32)
 
 
-def whole(body, outs, scalars, arrays, scratch=(), limit=40 << 20, flops=1 << 20, unread=()):
+def whole(body, outs, scalars, arrays, scratch=(), limit=16 << 20, flops=1 << 20, unread=()):
     return pl.pallas_call(
         body,
         out_shape=outs,
@@ -74,25 +68,33 @@
         side_b[...] = tile[:, :, left]
 
 
-def prepare_body(positions, intensity, probe, order, earlier, measured, rolled, held, arrived):
+def prepare_body(
+    positions, intensity, probe, measured, rolled, held, wave, arrived
+):
     slots, size = intensity.shape[0], probe.shape[1]
     half = size // 2
-    moves = [order[:half], order[half:]]
-    copies = [
-        pltpu.make_async_copy(intensity.at[:, :, pl.ds(half * block, half)], held.at[block], arrived.at[block])
-        for block in range(2)
-    ]
+    copies = [pltpu.make_async_copy(probe, wave, arrived.at[0])]
+    for block in range(2):
+        columns = intensity.at[:, :, pl.ds(half * block, half)]
+        copies.append(pltpu.make_async_copy(columns, held.at[block], arrived.at[1 + block]))
     for copy in copies:
         copy.start()
+    copies[0].wait()
 
     def turn(slot, carry):
-        shift = lax.rem(positions[slot, 1], size)
+        shift = lax.rem(positions[0, 0, slot, 1], size)
         for part in range(2):
-            rolled[slot, part] = pltpu.roll(probe[part], shift, 1)
+            rolled[slot, part] = pltpu.roll(wave[part], shift, 1)
         return carry
 
     lax.fori_loop(0, slots, turn, 0)
-    for copy in copies:
+    source = lax.broadcasted_iota(jnp.int32, (half, size), 0)
+    target = lax.broadcasted_iota(jnp.int32, (half, size), 1)
+    wanted = jnp.where(target < half, 2 * target, 2 * (target - half) + 1)
+    moves = [
+        jnp.where(source + half * block == wanted, 1.0, 0.0).astype(jnp.bfloat16) for block in range(2)
+    ]
+    for copy in copies[1:]:
         copy.wait()
 
     def reorder(slot, carry):
@@ -111,18 +113,23 @@
     lax.fori_loop(0, slots, reorder, 0)
 
 
-def prepare(positions, intensity, probe, order, earlier):
+def prepare(positions, intensity, probe):
     slots, size = intensity.shape[0], probe.shape[1]
     half = size // 2
+    hbm = pl.BlockSpec(memory_space=pltpu.HBM)
     return pl.pallas_call(
         prepare_body,
         out_shape=(shaped(slots, 2, half, size), shaped(slots, 2, size, size)),
-        in_specs=[SMEM, ANY, VMEM, VMEM, ANY],
+        in_specs=[SMEM, hbm, hbm],
         out_specs=(VMEM, VMEM),
-        scratch_shapes=[pltpu.VMEM((2, slots, size, half), jnp.int32), pltpu.SemaphoreType.DMA((2,))],
-        compiler_params=pltpu.CompilerParams(vmem_limit_bytes=24 << 20),
+        scratch_shapes=[
+            pltpu.VMEM((2, slots, size, half), jnp.int32),
+            pltpu.VMEM((2, size, size), jnp.float32),
+            pltpu.SemaphoreType.DMA((3,)),
+        ],
+        compiler_params=pltpu.CompilerParams(vmem_limit_bytes=16 << 20),
         cost_estimate=pl.CostEstimate(flops=slots * 2**27, bytes_accessed=8 << 20, transcendentals=0),
-    )(positions, intensity, probe, order, earlier)
+    )(positions, intensity, probe)
 
 
 def halves(value):
@@ -180,7 +187,7 @@
         field[near_at, :, middle] = near_edge[other]
         field[near_at, :, upper] = near_corner[other, 0]
         field[near_at, :, lower] = near_corner[other, 1]
-        field[far_at, :, middle] = jnp.where(info[4] == 1, 0.0, far_edge[odd_col])
+        field[far_at, :, middle] = far_edge[...]
         field[far_at, :, upper] = far_corner[0]
         field[far_at, :, lower] = far_corner[1]
     else:
@@ -191,10 +198,10 @@
     row_r, row_i = twist_row[0], twist_row[1]
 
     def enter(slot):
-        rows = pl.ds(positions[slot, 0], size)
+        rows = pl.ds(positions[0, 0, slot, 0], size)
         waves = []
         for block in range(2):
-            near = lanes + half * block >= positions[slot, 1]
+            near = lanes + half * block >= positions[0, 0, slot, 1]
             cut = slice(half * block, half * (block + 1))
             p_r, p_i = rolled[slot, 0, :, cut], rolled[slot, 1, :, cut]
             o_r = jnp.where(near, field[block, 0, rows, :], field[block + 2, 0, rows, :])
@@ -241,7 +248,7 @@
         ]
 
     def leave(slot, pair, keep):
-        rows = pl.ds(positions[slot, 0], size)
+        rows = pl.ds(positions[0, 0, slot, 0], size)
         even, odd = pair
         e_r, e_i = even[:, :half], even[:, half:]
         o_r, o_i = odd[:, :half], odd[:, half:]
@@ -250,8 +257,8 @@
         outs = [(e_r + t_r, e_i + t_i), (e_r - t_r, e_i - t_i)]
         for block, (b_r, b_i) in enumerate(outs):
             place = lanes + half * block
-            near = place >= positions[slot, 1]
-            far = place < positions[slot, 1]
+            near = place >= positions[0, 0, slot, 1]
+            far = place < positions[0, 0, slot, 1]
             if keep is not None:
                 near, far = near & keep, far & keep
             cut = slice(half * block, half * (block + 1))
@@ -297,7 +304,7 @@
     )
 
 
-def extend_body(info, tile, halo_a, halo_b, near, far, ext_r, ext_i, ext_b, corner_a, corner_b):
+def extend_body(info, tile, halo_a, halo_b, ready, ext_r, ext_i, ext_b, corner_a, corner_b):
     size = tile.shape[1]
     odd_row, odd_col = info[0], info[1]
 
@@ -415,9 +422,8 @@
     return lax.ppermute(value, axis, route)
 
 
-def paired(value, first=0):
-    count = lax.axis_size("cols")
-    groups = [[i, (i + 1) % count] for i in range(first, count, 2)]
+def paired(value):
+    groups = [[i, i + 1] for i in range(0, lax.axis_size("cols"), 2)]
     return lax.all_gather(value, "cols", axis_index_groups=groups)
 
 
@@ -442,28 +448,25 @@
     tile = object_field.shape[1]
     extent = tile + 2 * MARGIN
     row, col = lax.axis_index("rows"), lax.axis_index("cols")
-    last, end = lax.axis_size("rows") - 1, lax.axis_size("cols") - 1
-    info = jnp.stack(
-        [row % 2, col % 2, row == 0, row == last, (col == 0) | (col == end)]
-    ).astype(jnp.int32)
+    last = lax.axis_size("rows") - 1
+    info = jnp.stack([row % 2, col % 2, row == 0, row == last]).astype(jnp.int32)
     tables = constants(size)
-    order = jnp.asarray(split_order(size)).astype(jnp.bfloat16)
-    positions, intensity = positions[0, 0], intensity[0, 0]
+    intensity = intensity[0, 0]
     plane, strip = shaped(extent, HALF), shaped(2, extent, HALF)
     corner = shaped(2, 2, MARGIN, HALF)
 
     edge, side = shaped(2, MARGIN, tile), shaped(2, tile, MARGIN)
     edge_a, edge_b, side_a, side_b = whole(cut_body, (edge, edge, side, side), (info,), (object_field,))
     halos = both_rows(edge_a, edge_b)
-    far_edge, near_edge = paired(side_b, 1), paired(side_a)
+    far_edge, near_edge = swapped(side_b, "cols", 1), paired(side_a)
+    measured, rolled = prepare(positions, intensity, probe)
     *ext, corner_a, corner_b = whole(
         extend_body,
         (plane, plane, strip, corner, corner),
         (info,),
         (object_field, *halos),
-        unread=(near_edge, far_edge),
+        unread=(measured,),
     )
-    measured, rolled = prepare(positions, intensity, probe, order, corner_a)
     far_corner = swapped(corner_b, "cols", 1)
     sides = near_edge, paired(corner_a), far_edge, far_corner
     parts = gradient(True, info, positions, counts, ext, sides, measured, rolled, tables)

time: 124 us -> 120 us (0.968)
  blocking collectives: 31.4 us -> 17.4 us
  starting transfers between devices: 37.6 us -> 50.8 us
  Pallas kernels: 26.8 us -> 21.9 us
  local copies, waits for them, and re-layouts: 2.67 us -> 4.31 us
    all_gather x9 -> x8, blocking collectives: 31.4 us -> 17.4 us  [paired(): return lax.all_gather(value, 'cols', axis_index_groups=groups)]
    ppermute x14 -> x15, starting transfers between devices: 37.6 us -> 50.8 us  [swapped(): return lax.ppermute(value, axis, route)]
    pallas_call x11, Pallas kernels: 23.1 us -> 18.2 us  [whole(): pl.pallas_call(body, out_shape=outs, in_specs=[SMEM] * len(scalars) + [VM...]
    unnamed x22 -> x21, local copies, waits for them, and re-layouts: 2.49 us -> 4.31 us
    ppermute x14 -> x15, waiting for transfers between devices: 26.2 us -> 25.2 us  [swapped(): return lax.ppermute(value, axis, route)]
  transfers between devices with their start and end apart: 14 -> 15, of which waited for: 7 -> 7; matrix products, arithmetic and copies ran while one was open for 0% -> 1% of each run, Pallas kernels for 6% -> 6%
where the time goes in v2:
time: 120 us; the launch traced here: 121 us
  starting transfers between devices  50.8 us (42%)
  waiting for transfers between devices  25.2 us (21%)
  Pallas kernels  21.9 us (18%)
  blocking collectives  17.4 us (14%)
  local copies, waits for them, and re-layouts  4.31 us (4%)
    ppermute x15, starting transfers between devices, swapped(): return lax.ppermute(value, axis, route)  50.8 us
    ppermute x15, waiting for transfers between devices, swapped(): return lax.ppermute(value, axis, route)  25.2 us
    pallas_call x11, Pallas kernels, whole(): pl.pallas_call(body, out_shape=outs, in_specs=[SMEM] * len(scalars) + [VM...  18.2 us
    all_gather x8, blocking collectives, paired(): return lax.all_gather(value, 'cols', axis_index_groups=groups)  17.4 us
    unnamed x21, local copies, waits for them, and re-layouts  4.31 us
    pallas_call x1, Pallas kernels, prepare(): pl.pallas_call(prepare_body, out_shape=(shaped(slots, 2, half, size), sha...  3.79 us
  transfers between devices with their start and end apart: 15, of which 7 were waited for; matrix products, arithmetic and copies ran while one was open for 1% of the time, Pallas kernels for 6%

profile of v2, /device:TPU:10, one launch (start us, length us, event | category | flops | bytes accessed | tf_op | source)
XLA Modules:
  0.0 120.7 jit_solution(6268959176274049234)
XLA Ops:
  1.8 2.2 %collective-permute-start = (f32[2,128,256]{2,1,0:T(8,128)S(1)}, f32[2,128,256]{2,1,0:T(8,128)S(1)}, u32[]{:S(2)}, u32[]{:S(2)}) collective-permute-start(f32[2,128,256]{2,1,0:T(8,128)S(1)} %get-tuple-element.40), channel_id=1, source_target_pairs={{0,16},{16,0},{32,48},{48,32},{64,80},{80,64},{96,112},{112,96},{1... | collective-permute-start | bytes 786440 | tf_op jit(solution)/shard_map/ppermute | solution.py:422
  4.0 3.2 %collective-permute-start.1 = (f32[2,128,256]{2,1,0:T(8,128)S(1)}, f32[2,128,256]{2,1,0:T(8,128)S(1)}, u32[]{:S(2)}, u32[]{:S(2)}) collective-permute-start(f32[2,128,256]{2,1,0:T(8,128)S(1)} %get-tuple-element.41), channel_id=1, source_target_pairs={{16,32},{32,16},{48,64},{64,48},{80,96},{96,80},{17,33},{33,17},{4... | collective-permute-start | bytes 786440 | tf_op jit(solution)/shard_map/ppermute | solution.py:422
  7.2 4.8 %collective-permute-start.2 = (f32[2,256,128]{2,1,0:T(8,128)S(1)}, f32[2,256,128]{2,1,0:T(8,128)S(1)}, u32[]{:S(2)}, u32[]{:S(2)}) collective-permute-start(f32[2,256,128]{2,1,0:T(8,128)S(1)} %get-tuple-element.48), channel_id=1, source_target_pairs={{1,2},{2,1},{3,4},{4,3},{5,6},{6,5},{7,8},{8,7},{9,10},{10,9},{11,... | collective-permute-start | bytes 786440 | tf_op jit(solution)/shard_map/ppermute | solution.py:422
  15.8 3.8 %shard_map.110 = (f32[6,2,128,256]{3,2,1,0:T(8,128)S(1)}, f32[6,2,256,256]{3,2,1,0:T(8,128)S(1)}) custom-call(s32[1,1,6,2]{3,2,1,0:T(8,128)S(1)} %copy.15.positions, s32[6,256,256]{2,1,0:T(8,128)S(1)} %bitcast.21, f32[2,256,256]{2,1,0:T(8,128)S(1)} %copy-done.3), custom_call_target="tpu_custom_call" | custom-call | flops 805306368 | bytes 8388608 | tf_op jit(solution)/shard_map/pallas_call | solution.py:120
  20.4 2.9 %collective-permute-start.3 = (f32[2,2,128,128]{3,2,1,0:T(8,128)S(1)}, f32[2,2,128,128]{3,2,1,0:T(8,128)S(1)}, u32[]{:S(2)}, u32[]{:S(2)}) collective-permute-start(f32[2,2,128,128]{3,2,1,0:T(8,128)S(1)} %get-tuple-element.49), channel_id=1, source_target_pairs={{1,2},{2,1},{3,4},{4,3},{5,6},{6,5},{7,8},{8,7},{9,10},{10,9},{11,... | collective-permute-start | bytes 786440 | tf_op jit(solution)/shard_map/ppermute | solution.py:422
  23.3 2.2 %all-gather = f32[4,256,128]{2,1,0:T(8,128)S(1)} all-gather(f32[2,256,128]{2,1,0:T(8,128)S(1)} %get-tuple-element.46), channel_id=2, replica_groups={{0,1},{2,3},{4,5},{6,7},{8,9},{10,11},{12,13},{14,15},{16,17},{18,19},{..., dimensions={0}, use_global_device_ids=true | all-gather | bytes 786432 | tf_op jit(solution)/shard_map/all_gather | solution.py:427
  25.5 2.2 %all-gather.1 = f32[4,2,128,128]{3,2,1,0:T(8,128)S(1)} all-gather(f32[2,2,128,128]{3,2,1,0:T(8,128)S(1)} %get-tuple-element.47), channel_id=3, replica_groups={{0,1},{2,3},{4,5},{6,7},{8,9},{10,11},{12,13},{14,15},{16,17},{18,19},{..., dimensions={0}, use_global_device_ids=true | all-gather | bytes 786432 | tf_op jit(solution)/shard_map/all_gather | solution.py:427
  27.6 2.6 %collective-permute-done.3.refs_3_ = f32[2,2,128,128]{3,2,1,0:T(8,128)S(1)} collective-permute-done((f32[2,2,128,128]{3,2,1,0:T(8,128)S(1)}, f32[2,2,128,128]{3,2,1,0:T(8,128)S(1)}, u32[]{:S(2)}, u32[]{:S(2)}) %collective-permute-start.3) | collective-permute-done | bytes 262176 | tf_op jit(solution)/shard_map/ppermute | solution.py:422
  30.2 5.8 %shard_map.112 = (f32[512,128]{1,0:T(8,128)S(1)}, f32[512,128]{1,0:T(8,128)S(1)}, f32[2,512,128]{2,1,0:T(8,128)S(1)}, f32[2,512,128]{2,1,0:T(8,128)S(1)}, f32[2,512,128]{2,1,0:T(8,128)S(1)}) custom-call(s32[4]{0:T(128)S(1)} %pad_add_fusion.info, s32[1,1,6,2]{3,2,1,0:T(8,128)S(1)} %copy.15.positions, s32[1,1]{1,0:T(1,128)S(6)} %copy.18.counts, ...), custom_call_target="tpu_custom_call" | custom-call | flops 4831838208 | bytes 8388608 | tf_op jit(solution)/shard_map/pallas_call | solution.py:43
  36.1 1.9 %collective-permute-start.6 = (f32[2,512,128]{2,1,0:T(8,128)S(1)}, f32[2,512,128]{2,1,0:T(8,128)S(1)}, u32[]{:S(2)}, u32[]{:S(2)}) collective-permute-start(f32[2,512,128]{2,1,0:T(8,128)S(1)} %get-tuple-element.60), channel_id=1, source_target_pairs={{1,2},{2,1},{3,4},{4,3},{5,6},{6,5},{7,8},{8,7},{9,10},{10,9},{11,... | collective-permute-start | bytes 1572872 | tf_op jit(solution)/shard_map/ppermute | solution.py:422
  38.0 10.7 %collective-permute-done.6.strip = f32[2,512,128]{2,1,0:T(8,128)S(1)} collective-permute-done((f32[2,512,128]{2,1,0:T(8,128)S(1)}, f32[2,512,128]{2,1,0:T(8,128)S(1)}, u32[]{:S(2)}, u32[]{:S(2)}) %collective-permute-start.6) | collective-permute-done | bytes 524320 | tf_op jit(solution)/shard_map/ppermute | solution.py:422
  49.3 5.1 %collective-permute-start.7 = (f32[2,256,128]{2,1,0:T(8,128)S(1)}, f32[2,256,128]{2,1,0:T(8,128)S(1)}, u32[]{:S(2)}, u32[]{:S(2)}) collective-permute-start(f32[2,256,128]{2,1,0:T(8,128)S(1)} %get-tuple-element.62), channel_id=1, source_target_pairs={{0,16},{16,0},{32,48},{48,32},{64,80},{80,64},{96,112},{112,96},{1... | collective-permute-start | bytes 786440 | tf_op jit(solution)/shard_map/ppermute | solution.py:422
  54.4 1.9 %collective-permute-start.8 = (f32[2,256,128]{2,1,0:T(8,128)S(1)}, f32[2,256,128]{2,1,0:T(8,128)S(1)}, u32[]{:S(2)}, u32[]{:S(2)}) collective-permute-start(f32[2,256,128]{2,1,0:T(8,128)S(1)} %get-tuple-element.63), channel_id=1, source_target_pairs={{16,32},{32,16},{48,64},{64,48},{80,96},{96,80},{17,33},{33,17},{4... | collective-permute-start | bytes 786440 | tf_op jit(solution)/shard_map/ppermute | solution.py:422
  56.3 2.2 %all-gather.2 = f32[1024,128]{1,0:T(8,128)S(1)} all-gather(f32[512,128]{1,0:T(8,128)S(1)} %get-tuple-element.52), channel_id=4, replica_groups={{0,1},{2,3},{4,5},{6,7},{8,9},{10,11},{12,13},{14,15},{16,17},{18,19},{..., dimensions={0}, use_global_device_ids=true | all-gather | bytes 786432 | tf_op jit(solution)/shard_map/all_gather | solution.py:427
  58.5 2.2 %all-gather.3 = f32[1024,128]{1,0:T(8,128)S(1)} all-gather(f32[512,128]{1,0:T(8,128)S(1)} %get-tuple-element.53), channel_id=5, replica_groups={{0,1},{2,3},{4,5},{6,7},{8,9},{10,11},{12,13},{14,15},{16,17},{18,19},{..., dimensions={0}, use_global_device_ids=true | all-gather | bytes 786432 | tf_op jit(solution)/shard_map/all_gather | solution.py:427
  61.3 6.2 %collective-permute-start.4 = (f32[2,256,128]{2,1,0:T(8,128)S(1)}, f32[2,256,128]{2,1,0:T(8,128)S(1)}, u32[]{:S(2)}, u32[]{:S(2)}) collective-permute-start(f32[2,256,128]{2,1,0:T(8,128)S(1)} %get-tuple-element.55), channel_id=1, source_target_pairs={{0,16},{16,0},{32,48},{48,32},{64,80},{80,64},{96,112},{112,96},{1... | collective-permute-start | bytes 786440 | tf_op jit(solution)/shard_map/ppermute | solution.py:422
  67.5 1.9 %collective-permute-start.5 = (f32[2,256,128]{2,1,0:T(8,128)S(1)}, f32[2,256,128]{2,1,0:T(8,128)S(1)}, u32[]{:S(2)}, u32[]{:S(2)}) collective-permute-start(f32[2,256,128]{2,1,0:T(8,128)S(1)} %get-tuple-element.56), channel_id=1, source_target_pairs={{16,32},{32,16},{48,64},{64,48},{80,96},{96,80},{17,33},{33,17},{4... | collective-permute-start | bytes 786440 | tf_op jit(solution)/shard_map/ppermute | solution.py:422
  70.1 4.0 %collective-permute-start.9 = (f32[2,512,128]{2,1,0:T(8,128)S(1)}, f32[2,512,128]{2,1,0:T(8,128)S(1)}, u32[]{:S(2)}, u32[]{:S(2)}) collective-permute-start(f32[2,512,128]{2,1,0:T(8,128)S(1)} %shard_map.116.ext_b), channel_id=1, source_target_pairs={{1,2},{2,1},{3,4},{4,3},{5,6},{6,5},{7,8},{8,7},{9,10},{10,9},{11,... | collective-permute-start | bytes 1572872 | tf_op jit(solution)/shard_map/ppermute | solution.py:422
  74.6 5.3 %collective-permute-done.5.halo_b = f32[2,256,128]{2,1,0:T(8,128)S(1)} collective-permute-done((f32[2,256,128]{2,1,0:T(8,128)S(1)}, f32[2,256,128]{2,1,0:T(8,128)S(1)}, u32[]{:S(2)}, u32[]{:S(2)}) %collective-permute-start.5) | collective-permute-done | bytes 262176 | tf_op jit(solution)/shard_map/ppermute | solution.py:422
  80.6 2.2 %all-gather.4 = f32[1024,128]{1,0:T(8,128)S(1)} all-gather(f32[512,128]{1,0:T(8,128)S(1)} %get-tuple-element.57.ext_r), channel_id=6, replica_groups={{0,1},{2,3},{4,5},{6,7},{8,9},{10,11},{12,13},{14,15},{16,17},{18,19},{..., dimensions={0}, use_global_device_ids=true | all-gather | bytes 786432 | tf_op jit(solution)/shard_map/all_gather | solution.py:427
  82.7 2.2 %all-gather.5 = f32[1024,128]{1,0:T(8,128)S(1)} all-gather(f32[512,128]{1,0:T(8,128)S(1)} %get-tuple-element.58.ext_i), channel_id=7, replica_groups={{0,1},{2,3},{4,5},{6,7},{8,9},{10,11},{12,13},{14,15},{16,17},{18,19},{..., dimensions={0}, use_global_device_ids=true | all-gather | bytes 786432 | tf_op jit(solution)/shard_map/all_gather | solution.py:427
  84.9 5.8 %shard_map.117 = (f32[512,128]{1,0:T(8,128)S(1)}, f32[512,128]{1,0:T(8,128)S(1)}, f32[2,512,128]{2,1,0:T(8,128)S(1)}, f32[2,512,128]{2,1,0:T(8,128)S(1)}, f32[2,512,128]{2,1,0:T(8,128)S(1)}) custom-call(s32[4]{0:T(128)S(1)} %pad_add_fusion.info, s32[1,1,6,2]{3,2,1,0:T(8,128)S(1)} %copy.15.positions, s32[1,1]{1,0:T(1,128)S(6)} %copy.18.counts, ...), custom_call_target="tpu_custom_call" | custom-call | flops 4831838208 | bytes 8388608 | tf_op jit(solution)/shard_map/pallas_call | solution.py:43
  90.7 3.3 %collective-permute-start.10 = (f32[2,512,128]{2,1,0:T(8,128)S(1)}, f32[2,512,128]{2,1,0:T(8,128)S(1)}, u32[]{:S(2)}, u32[]{:S(2)}) collective-permute-start(f32[2,512,128]{2,1,0:T(8,128)S(1)} %get-tuple-element.69), channel_id=1, source_target_pairs={{1,2},{2,1},{3,4},{4,3},{5,6},{6,5},{7,8},{8,7},{9,10},{10,9},{11,... | collective-permute-start | bytes 1572872 | tf_op jit(solution)/shard_map/ppermute | solution.py:422
  94.0 2.2 %all-gather.6 = f32[1024,128]{1,0:T(8,128)S(1)} all-gather(f32[512,128]{1,0:T(8,128)S(1)} %get-tuple-element.65), channel_id=8, replica_groups={{0,1},{2,3},{4,5},{6,7},{8,9},{10,11},{12,13},{14,15},{16,17},{18,19},{..., dimensions={0}, use_global_device_ids=true | all-gather | bytes 786432 | tf_op jit(solution)/shard_map/all_gather | solution.py:427
  96.2 2.2 %all-gather.7 = f32[1024,128]{1,0:T(8,128)S(1)} all-gather(f32[512,128]{1,0:T(8,128)S(1)} %get-tuple-element.66), channel_id=9, replica_groups={{0,1},{2,3},{4,5},{6,7},{8,9},{10,11},{12,13},{14,15},{16,17},{18,19},{..., dimensions={0}, use_global_device_ids=true | all-gather | bytes 786432 | tf_op jit(solution)/shard_map/all_gather | solution.py:427
  99.0 5.1 %collective-permute-start.11 = (f32[2,128,128]{2,1,0:T(8,128)S(1)}, f32[2,128,128]{2,1,0:T(8,128)S(1)}, u32[]{:S(2)}, u32[]{:S(2)}) collective-permute-start(f32[2,128,128]{2,1,0:T(8,128)S(1)} %get-tuple-element.71), channel_id=1, source_target_pairs={{0,16},{16,0},{32,48},{48,32},{64,80},{80,64},{96,112},{112,96},{1... | collective-permute-start | bytes 393224 | tf_op jit(solution)/shard_map/ppermute | solution.py:422
  104.1 2.0 %collective-permute-start.12 = (f32[2,128,128]{2,1,0:T(8,128)S(1)}, f32[2,128,128]{2,1,0:T(8,128)S(1)}, u32[]{:S(2)}, u32[]{:S(2)}) collective-permute-start(f32[2,128,128]{2,1,0:T(8,128)S(1)} %get-tuple-element.72), channel_id=1, source_target_pairs={{16,32},{32,16},{48,64},{64,48},{80,96},{96,80},{17,33},{33,17},{4... | collective-permute-start | bytes 393224 | tf_op jit(solution)/shard_map/ppermute | solution.py:422
  106.8 2.8 %collective-permute-start.13 = (f32[2,128,128]{2,1,0:T(8,128)S(1)}, f32[2,128,128]{2,1,0:T(8,128)S(1)}, u32[]{:S(2)}, u32[]{:S(2)}) collective-permute-start(f32[2,128,128]{2,1,0:T(8,128)S(1)} %get-tuple-element.73), channel_id=1, source_target_pairs={{0,16},{16,0},{32,48},{48,32},{64,80},{80,64},{96,112},{112,96},{1... | collective-permute-start | bytes 393224 | tf_op jit(solution)/shard_map/ppermute | solution.py:422
  109.5 3.6 %collective-permute-start.14 = (f32[2,128,128]{2,1,0:T(8,128)S(1)}, f32[2,128,128]{2,1,0:T(8,128)S(1)}, u32[]{:S(2)}, u32[]{:S(2)}) collective-permute-start(f32[2,128,128]{2,1,0:T(8,128)S(1)} %get-tuple-element.74), channel_id=1, source_target_pairs={{16,32},{32,16},{48,64},{64,48},{80,96},{96,80},{17,33},{33,17},{4... | collective-permute-start | bytes 393224 | tf_op jit(solution)/shard_map/ppermute | solution.py:422
  113.1 1.7 %collective-permute-done.12.near_b = f32[2,128,128]{2,1,0:T(8,128)S(1)} collective-permute-done((f32[2,128,128]{2,1,0:T(8,128)S(1)}, f32[2,128,128]{2,1,0:T(8,128)S(1)}, u32[]{:S(2)}, u32[]{:S(2)}) %collective-permute-start.12) | collective-permute-done | bytes 131104 | tf_op jit(solution)/shard_map/ppermute | solution.py:422
  115.1 4.2 %collective-permute-done.14.far_b = f32[2,128,128]{2,1,0:T(8,128)S(1)} collective-permute-done((f32[2,128,128]{2,1,0:T(8,128)S(1)}, f32[2,128,128]{2,1,0:T(8,128)S(1)}, u32[]{:S(2)}, u32[]{:S(2)}) %collective-permute-start.14) | collective-permute-done | bytes 131104 | tf_op jit(solution)/shard_map/ppermute | solution.py:422
  119.3 1.5 %shard_map.120 = f32[2,256,256]{2,1,0:T(8,128)} custom-call(s32[4]{0:T(128)S(1)} %pad_add_fusion.info, f32[512,128]{1,0:T(8,128)S(1)} %get-tuple-element.57.ext_r, f32[512,128]{1,0:T(8,128)S(1)} %get-tuple-element.58.ext_i, f32[2,512,128]{2,1,0:T(8,128)S(1)} %shard_map.116.ext_b, f32[2,512,128]{2,1,0:T(8,128)S(1)} %get-tuple-element.67.total_a, ...), custom_call_target="tpu_custom_call" | custom-call | flops 1048576 | bytes 8388608 | tf_op jit(solution)/shard_map/pallas_call | solution.py:43
  (40 shorter events, 10.4 us)
Async XLA Ops:
  0.1 1.0 copy-start
  1.7 17.9 %copy-start.1 = (f32[2,256,256]{2,1,0:T(8,128)S(1)}, f32[2,256,256]{2,1,0:T(8,128)}, u32[]{:S(2)}) copy-start(f32[2,256,256]{2,1,0:T(8,128)} %tile.3) | copy-start | bytes 1572868
  1.8 17.9 %collective-permute-start = (f32[2,128,256]{2,1,0:T(8,128)S(1)}, f32[2,128,256]{2,1,0:T(8,128)S(1)}, u32[]{:S(2)}, u32[]{:S(2)}) collective-permute-start(f32[2,128,256]{2,1,0:T(8,128)S(1)} %get-tuple-element.40), channel_id=1, source_target_pairs={{0,16},{16,0},{32,48},{48,32},{64,80},{80,64},{96,112},{112,96},{1... | collective-permute-start | bytes 786440 | tf_op jit(solution)/shard_map/ppermute | solution.py:422
  4.0 15.7 %collective-permute-start.1 = (f32[2,128,256]{2,1,0:T(8,128)S(1)}, f32[2,128,256]{2,1,0:T(8,128)S(1)}, u32[]{:S(2)}, u32[]{:S(2)}) collective-permute-start(f32[2,128,256]{2,1,0:T(8,128)S(1)} %get-tuple-element.41), channel_id=1, source_target_pairs={{16,32},{32,16},{48,64},{64,48},{80,96},{96,80},{17,33},{33,17},{4... | collective-permute-start | bytes 786440 | tf_op jit(solution)/shard_map/ppermute | solution.py:422
  7.2 20.5 %collective-permute-start.2 = (f32[2,256,128]{2,1,0:T(8,128)S(1)}, f32[2,256,128]{2,1,0:T(8,128)S(1)}, u32[]{:S(2)}, u32[]{:S(2)}) collective-permute-start(f32[2,256,128]{2,1,0:T(8,128)S(1)} %get-tuple-element.48), channel_id=1, source_target_pairs={{1,2},{2,1},{3,4},{4,3},{5,6},{6,5},{7,8},{8,7},{9,10},{10,9},{11,... | collective-permute-start | bytes 786440 | tf_op jit(solution)/shard_map/ppermute | solution.py:422
  13.4 1.4 %copy-start.2 = (s32[1,1,6,256,256]{4,3,2,1,0:T(8,128)S(1)}, s32[1,1,6,256,256]{4,3,2,1,0:T(8,128)}, u32[]{:S(2)}) copy-start(s32[1,1,6,256,256]{4,3,2,1,0:T(8,128)} %param.15) | copy-start | bytes 4718596
  14.8 1.0 copy-start.3
  19.7 10.5 %copy-start.4 = (bf16[768,256]{1,0:T(8,128)(2,1)S(1)}, bf16[768,256]{1,0:T(8,128)(2,1)}, u32[]{:S(2)}) copy-start(bf16[768,256]{1,0:T(8,128)(2,1)} %constant.44.clone.refs_9_.refs_8_) | copy-start | bytes 1179652
  19.7 10.5 %copy-start.5 = (bf16[256,768]{1,0:T(8,128)(2,1)S(1)}, bf16[256,768]{1,0:T(8,128)(2,1)}, u32[]{:S(2)}) copy-start(bf16[256,768]{1,0:T(8,128)(2,1)} %constant.43.clone.refs_7_.refs_6_) | copy-start | bytes 1179652
  19.7 10.5 %copy-start.6 = (bf16[256,768]{1,0:T(8,128)(2,1)S(1)}, bf16[256,768]{1,0:T(8,128)(2,1)}, u32[]{:S(2)}) copy-start(bf16[256,768]{1,0:T(8,128)(2,1)} %constant.42.clone.refs_8_.refs_7_) | copy-start | bytes 1179652
  19.7 10.5 %copy-start.7 = (bf16[768,256]{1,0:T(8,128)(2,1)S(1)}, bf16[768,256]{1,0:T(8,128)(2,1)}, u32[]{:S(2)}) copy-start(bf16[768,256]{1,0:T(8,128)(2,1)} %constant.41.clone.refs_6_.refs_5_) | copy-start | bytes 1179652
  19.7 10.5 %copy-start.8 = (f32[2,128,256]{2,1,0:T(8,128)S(1)}, f32[2,128,256]{2,1,0:T(8,128)}, u32[]{:S(2)}) copy-start(f32[2,128,256]{2,1,0:T(8,128)} %constant.46.clone.refs_11_.refs_10_) | copy-start | bytes 786436
  19.7 10.5 %copy-start.9 = (f32[2,1,128]{2,1,0:T(1,128)S(1)}, f32[2,1,128]{2,1,0:T(1,128)}, u32[]{:S(2)}) copy-start(f32[2,1,128]{2,1,0:T(1,128)} %constant.45.clone.refs_10_.refs_9_) | copy-start | bytes 3076
  20.4 9.8 %collective-permute-start.3 = (f32[2,2,128,128]{3,2,1,0:T(8,128)S(1)}, f32[2,2,128,128]{3,2,1,0:T(8,128)S(1)}, u32[]{:S(2)}, u32[]{:S(2)}) collective-permute-start(f32[2,2,128,128]{3,2,1,0:T(8,128)S(1)} %get-tuple-element.49), channel_id=1, source_target_pairs={{1,2},{2,1},{3,4},{4,3},{5,6},{6,5},{7,8},{8,7},{9,10},{10,9},{11,... | collective-permute-start | bytes 786440 | tf_op jit(solution)/shard_map/ppermute | solution.py:422
  36.1 12.6 %collective-permute-start.6 = (f32[2,512,128]{2,1,0:T(8,128)S(1)}, f32[2,512,128]{2,1,0:T(8,128)S(1)}, u32[]{:S(2)}, u32[]{:S(2)}) collective-permute-start(f32[2,512,128]{2,1,0:T(8,128)S(1)} %get-tuple-element.60), channel_id=1, source_target_pairs={{1,2},{2,1},{3,4},{4,3},{5,6},{6,5},{7,8},{8,7},{9,10},{10,9},{11,... | collective-permute-start | bytes 1572872 | tf_op jit(solution)/shard_map/ppermute | solution.py:422
  49.3 20.2 %collective-permute-start.7 = (f32[2,256,128]{2,1,0:T(8,128)S(1)}, f32[2,256,128]{2,1,0:T(8,128)S(1)}, u32[]{:S(2)}, u32[]{:S(2)}) collective-permute-start(f32[2,256,128]{2,1,0:T(8,128)S(1)} %get-tuple-element.62), channel_id=1, source_target_pairs={{0,16},{16,0},{32,48},{48,32},{64,80},{80,64},{96,112},{112,96},{1... | collective-permute-start | bytes 786440 | tf_op jit(solution)/shard_map/ppermute | solution.py:422
  54.4 15.1 %collective-permute-start.8 = (f32[2,256,128]{2,1,0:T(8,128)S(1)}, f32[2,256,128]{2,1,0:T(8,128)S(1)}, u32[]{:S(2)}, u32[]{:S(2)}) collective-permute-start(f32[2,256,128]{2,1,0:T(8,128)S(1)} %get-tuple-element.63), channel_id=1, source_target_pairs={{16,32},{32,16},{48,64},{64,48},{80,96},{96,80},{17,33},{33,17},{4... | collective-permute-start | bytes 786440 | tf_op jit(solution)/shard_map/ppermute | solution.py:422
  61.3 13.3 %collective-permute-start.4 = (f32[2,256,128]{2,1,0:T(8,128)S(1)}, f32[2,256,128]{2,1,0:T(8,128)S(1)}, u32[]{:S(2)}, u32[]{:S(2)}) collective-permute-start(f32[2,256,128]{2,1,0:T(8,128)S(1)} %get-tuple-element.55), channel_id=1, source_target_pairs={{0,16},{16,0},{32,48},{48,32},{64,80},{80,64},{96,112},{112,96},{1... | collective-permute-start | bytes 786440 | tf_op jit(solution)/shard_map/ppermute | solution.py:422
  67.5 12.4 %collective-permute-start.5 = (f32[2,256,128]{2,1,0:T(8,128)S(1)}, f32[2,256,128]{2,1,0:T(8,128)S(1)}, u32[]{:S(2)}, u32[]{:S(2)}) collective-permute-start(f32[2,256,128]{2,1,0:T(8,128)S(1)} %get-tuple-element.56), channel_id=1, source_target_pairs={{16,32},{32,16},{48,64},{64,48},{80,96},{96,80},{17,33},{33,17},{4... | collective-permute-start | bytes 786440 | tf_op jit(solution)/shard_map/ppermute | solution.py:422
  70.1 14.8 %collective-permute-start.9 = (f32[2,512,128]{2,1,0:T(8,128)S(1)}, f32[2,512,128]{2,1,0:T(8,128)S(1)}, u32[]{:S(2)}, u32[]{:S(2)}) collective-permute-start(f32[2,512,128]{2,1,0:T(8,128)S(1)} %shard_map.116.ext_b), channel_id=1, source_target_pairs={{1,2},{2,1},{3,4},{4,3},{5,6},{6,5},{7,8},{8,7},{9,10},{10,9},{11,... | collective-permute-start | bytes 1572872 | tf_op jit(solution)/shard_map/ppermute | solution.py:422
  90.7 15.4 %collective-permute-start.10 = (f32[2,512,128]{2,1,0:T(8,128)S(1)}, f32[2,512,128]{2,1,0:T(8,128)S(1)}, u32[]{:S(2)}, u32[]{:S(2)}) collective-permute-start(f32[2,512,128]{2,1,0:T(8,128)S(1)} %get-tuple-element.69), channel_id=1, source_target_pairs={{1,2},{2,1},{3,4},{4,3},{5,6},{6,5},{7,8},{8,7},{9,10},{10,9},{11,... | collective-permute-start | bytes 1572872 | tf_op jit(solution)/shard_map/ppermute | solution.py:422
  99.0 14.1 %collective-permute-start.11 = (f32[2,128,128]{2,1,0:T(8,128)S(1)}, f32[2,128,128]{2,1,0:T(8,128)S(1)}, u32[]{:S(2)}, u32[]{:S(2)}) collective-permute-start(f32[2,128,128]{2,1,0:T(8,128)S(1)} %get-tuple-element.71), channel_id=1, source_target_pairs={{0,16},{16,0},{32,48},{48,32},{64,80},{80,64},{96,112},{112,96},{1... | collective-permute-start | bytes 393224 | tf_op jit(solution)/shard_map/ppermute | solution.py:422
  104.1 10.7 %collective-permute-start.12 = (f32[2,128,128]{2,1,0:T(8,128)S(1)}, f32[2,128,128]{2,1,0:T(8,128)S(1)}, u32[]{:S(2)}, u32[]{:S(2)}) collective-permute-start(f32[2,128,128]{2,1,0:T(8,128)S(1)} %get-tuple-element.72), channel_id=1, source_target_pairs={{16,32},{32,16},{48,64},{64,48},{80,96},{96,80},{17,33},{33,17},{4... | collective-permute-start | bytes 393224 | tf_op jit(solution)/shard_map/ppermute | solution.py:422
  106.8 8.3 %collective-permute-start.13 = (f32[2,128,128]{2,1,0:T(8,128)S(1)}, f32[2,128,128]{2,1,0:T(8,128)S(1)}, u32[]{:S(2)}, u32[]{:S(2)}) collective-permute-start(f32[2,128,128]{2,1,0:T(8,128)S(1)} %get-tuple-element.73), channel_id=1, source_target_pairs={{0,16},{16,0},{32,48},{48,32},{64,80},{80,64},{96,112},{112,96},{1... | collective-permute-start | bytes 393224 | tf_op jit(solution)/shard_map/ppermute | solution.py:422
  109.5 9.8 %collective-permute-start.14 = (f32[2,128,128]{2,1,0:T(8,128)S(1)}, f32[2,128,128]{2,1,0:T(8,128)S(1)}, u32[]{:S(2)}, u32[]{:S(2)}) collective-permute-start(f32[2,128,128]{2,1,0:T(8,128)S(1)} %get-tuple-element.74), channel_id=1, source_target_pairs={{16,32},{32,16},{48,64},{64,48},{80,96},{96,80},{17,33},{33,17},{4... | collective-permute-start | bytes 393224 | tf_op jit(solution)/shard_map/ppermute | solution.py:422

commit v3 on v2

--- a/solution.py
+++ b/solution.py
@@ -88,26 +88,25 @@
         return carry
 
     lax.fori_loop(0, slots, turn, 0)
-    source = lax.broadcasted_iota(jnp.int32, (half, size), 0)
-    target = lax.broadcasted_iota(jnp.int32, (half, size), 1)
+    source = lax.broadcasted_iota(jnp.int32, (size, size), 0)
+    target = lax.broadcasted_iota(jnp.int32, (size, size), 1)
     wanted = jnp.where(target < half, 2 * target, 2 * (target - half) + 1)
-    moves = [
-        jnp.where(source + half * block == wanted, 1.0, 0.0).astype(jnp.bfloat16) for block in range(2)
-    ]
+    moves = jnp.where(source == wanted, 1.0, 0.0).astype(jnp.bfloat16)
     for copy in copies[1:]:
         copy.wait()
 
     def reorder(slot, carry):
-        for parity in range(2):
-            moved = jnp.zeros((half, size), jnp.float32)
-            for block in range(2):
-                counts = held[block, slot, pl.ds(parity, half, stride=2), :]
-                upper = lax.shift_right_logical(counts, 8).astype(jnp.float32).astype(jnp.bfloat16)
-                lower = lax.bitwise_and(counts, 255).astype(jnp.float32).astype(jnp.bfloat16)
-                high = jnp.dot(upper, moves[block], preferred_element_type=jnp.float32)
-                low = jnp.dot(lower, moves[block], preferred_element_type=jnp.float32)
-                moved = moved + (256.0 * high + low)
-            measured[slot, parity] = moved * photon_unit
+        rows = [
+            wide(*[held[block, slot, pl.ds(parity, half, stride=2), :] for block in range(2)])
+            for parity in range(2)
+        ]
+        counts = tall(*rows)
+        upper = lax.shift_right_logical(counts, 8).astype(jnp.float32).astype(jnp.bfloat16)
+        lower = lax.bitwise_and(counts, 255).astype(jnp.float32).astype(jnp.bfloat16)
+        moved = jnp.dot(tall(upper, lower), moves, preferred_element_type=jnp.float32)
+        moved = (256.0 * moved[:size] + moved[size:]) * photon_unit
+        measured[slot, 0] = moved[:half]
+        measured[slot, 1] = moved[half:]
         return carry
 
     lax.fori_loop(0, slots, reorder, 0)
@@ -198,7 +197,7 @@
     row_r, row_i = twist_row[0], twist_row[1]
 
     def enter(slot):
-        rows = pl.ds(positions[0, 0, slot, 0], size)
+        rows = pl.ds(jnp.clip(positions[0, 0, slot, 0], 0, size), size)
         waves = []
         for block in range(2):
             near = lanes + half * block >= positions[0, 0, slot, 1]
@@ -248,7 +247,7 @@
         ]
 
     def leave(slot, pair, keep):
-        rows = pl.ds(positions[0, 0, slot, 0], size)
+        rows = pl.ds(jnp.clip(positions[0, 0, slot, 0], 0, size), size)
         even, odd = pair
         e_r, e_i = even[:, :half], even[:, half:]
         o_r, o_i = odd[:, :half], odd[:, half:]
@@ -373,31 +372,51 @@
         out[part] = updated(info, part, ext_b.at[part], total, halo_a, halo_b)
 
 
-def finish_body(info, ext_r, ext_i, ext_b, total_a, total_b, near_a, near_b, far_a, far_b, out):
-    size = out.shape[1]
+def finish_body(
+    info, ext_r, ext_i, ext_b, total_a, total_b, near_a, near_b, far_a, far_b, out, ready, sent
+):
+    size = ready.shape[1]
     half = size // 2
     upper, lower = slice(MARGIN, MARGIN + half), slice(MARGIN + half, MARGIN + size)
-
-    def settle(cut, ext, total, halo_a, halo_b):
-        for part in range(2):
-            above = total[part, upper] + jnp.where(info[0] == 1, halo_a[part], halo_b[part])
-            below = total[part, lower] + jnp.where(info[0] == 1, halo_b[part], halo_a[part])
-            out[part, :half, cut] = ext[part][upper] - step_rate * above
-            out[part, half:, cut] = ext[part][lower] - step_rate * below
-
-    def place(cut_a, cut_b):
-        settle(cut_a, [ext_r, ext_i], total_a, near_a, near_b)
-        settle(cut_b, [ext_b.at[0], ext_b.at[1]], total_b, far_a, far_b)
+    copies = [pltpu.make_async_copy(ready.at[part], out.at[part], sent.at[part]) for part in range(2)]
+
+    def settle(part, cut, ext, total, halo_a, halo_b):
+        above = total[part, upper] + jnp.where(info[0] == 1, halo_a[part], halo_b[part])
+        below = total[part, lower] + jnp.where(info[0] == 1, halo_b[part], halo_a[part])
+        ready[part, :half, cut] = ext[upper] - step_rate * above
+        ready[part, half:, cut] = ext[lower] - step_rate * below
+
+    def place(part, cut_a, cut_b):
+        settle(part, cut_a, [ext_r, ext_i][part], total_a, near_a, near_b)
+        settle(part, cut_b, ext_b.at[part], total_b, far_a, far_b)
 
     left, right = slice(0, HALF), slice(HALF, 2 * HALF)
-
-    @pl.when(info[1] == 1)
-    def _():
-        place(left, right)
-
-    @pl.when(info[1] == 0)
-    def _():
-        place(right, left)
+    for part in range(2):
+
+        @pl.when(info[1] == 1)
+        def _():
+            place(part, left, right)
+
+        @pl.when(info[1] == 0)
+        def _():
+            place(part, right, left)
+
+        copies[part].start()
+    for copy in copies:
+        copy.wait()
+
+
+def finished(info, tile, arrays):
+    whole_tile = shaped(2, tile, tile)
+    return pl.pallas_call(
+        finish_body,
+        out_shape=whole_tile,
+        in_specs=[SMEM] + [VMEM] * len(arrays),
+        out_specs=ANY,
+        scratch_shapes=[pltpu.VMEM(whole_tile.shape, jnp.float32), pltpu.SemaphoreType.DMA((2,))],
+        compiler_params=pltpu.CompilerParams(vmem_limit_bytes=16 << 20),
+        cost_estimate=pl.CostEstimate(flops=1 << 20, bytes_accessed=4 << 20, transcendentals=0),
+    )(info, *arrays)
 
 
 def constants(size):
@@ -477,9 +496,7 @@
     sides = paired(ext[0]), paired(ext[1]), swapped(ext[2], "cols", 1)
     parts = gradient(False, info, positions, counts, ext, sides, measured, rolled, tables)
     total_a, halos_a, total_b, halos_b = summed(info, MARGIN, *parts)
-    return whole(
-        finish_body, (shaped(2, tile, tile),), (info,), (*ext, total_a, total_b, *halos_a, *halos_b)
-    )[0]
+    return finished(info, tile, (*ext, total_a, total_b, *halos_a, *halos_b))
 
 
 def solution(mesh):

time: 120 us -> 120 us (level); the launches traced: 121 us -> 118 us
  starting transfers between devices: 50.8 us -> 41.1 us
  Pallas kernels: 21.9 us -> 26.5 us
  waiting for transfers between devices: 25.2 us -> 27.5 us
    ppermute x15, starting transfers between devices: 50.8 us -> 41.1 us  [swapped(): return lax.ppermute(value, axis, route)]
    pallas_call x11 -> x10, Pallas kernels: 18.2 us -> 21.6 us  [whole(): pl.pallas_call(body, out_shape=outs, in_specs=[SMEM] * len(scalars) + [VM...]
    ppermute x15, waiting for transfers between devices: 25.2 us -> 27.5 us  [swapped(): return lax.ppermute(value, axis, route)]
    pallas_call x0 -> x1, Pallas kernels: none -> 1.42 us  [finished(): pl.pallas_call(finish_body, out_shape=whole_tile, in_specs=[SMEM] + [VMEM...]
where the time goes in v3:
time: 120 us; the launch traced here: 118 us
  starting transfers between devices  41.1 us (34%)
  waiting for transfers between devices  27.5 us (23%)
  Pallas kernels  26.5 us (22%)
  blocking collectives  17.4 us (14%)
  local copies, waits for them, and re-layouts  4.31 us (4%)
    ppermute x15, starting transfers between devices, swapped(): return lax.ppermute(value, axis, route)  41.1 us
    ppermute x15, waiting for transfers between devices, swapped(): return lax.ppermute(value, axis, route)  27.5 us
    pallas_call x10, Pallas kernels, whole(): pl.pallas_call(body, out_shape=outs, in_specs=[SMEM] * len(scalars) + [VM...  21.6 us
    all_gather x8, blocking collectives, paired(): return lax.all_gather(value, 'cols', axis_index_groups=groups)  17.4 us
    unnamed x21, local copies, waits for them, and re-layouts  4.31 us
    pallas_call x1, Pallas kernels, prepare(): pl.pallas_call(prepare_body, out_shape=(shaped(slots, 2, half, size), sha...  3.52 us
  transfers between devices with their start and end apart: 15, of which 7 were waited for; matrix products, arithmetic and copies ran while one was open for 1% of the time, Pallas kernels for 6%

profile of v3, /device:TPU:10, one launch (start us, length us, event | category | flops | bytes accessed | tf_op | source)
XLA Modules:
  0.0 117.8 jit_solution(9539512257736128982)
XLA Ops:
  1.8 2.2 %collective-permute-start = (f32[2,128,256]{2,1,0:T(8,128)S(1)}, f32[2,128,256]{2,1,0:T(8,128)S(1)}, u32[]{:S(2)}, u32[]{:S(2)}) collective-permute-start(f32[2,128,256]{2,1,0:T(8,128)S(1)} %get-tuple-element.40), channel_id=1, source_target_pairs={{0,16},{16,0},{32,48},{48,32},{64,80},{80,64},{96,112},{112,96},{1... | collective-permute-start | bytes 786440 | tf_op jit(solution)/shard_map/ppermute | solution.py:441
  4.0 3.2 %collective-permute-start.1 = (f32[2,128,256]{2,1,0:T(8,128)S(1)}, f32[2,128,256]{2,1,0:T(8,128)S(1)}, u32[]{:S(2)}, u32[]{:S(2)}) collective-permute-start(f32[2,128,256]{2,1,0:T(8,128)S(1)} %get-tuple-element.41), channel_id=1, source_target_pairs={{16,32},{32,16},{48,64},{64,48},{80,96},{96,80},{17,33},{33,17},{4... | collective-permute-start | bytes 786440 | tf_op jit(solution)/shard_map/ppermute | solution.py:441
  7.2 4.8 %collective-permute-start.2 = (f32[2,256,128]{2,1,0:T(8,128)S(1)}, f32[2,256,128]{2,1,0:T(8,128)S(1)}, u32[]{:S(2)}, u32[]{:S(2)}) collective-permute-start(f32[2,256,128]{2,1,0:T(8,128)S(1)} %get-tuple-element.48), channel_id=1, source_target_pairs={{1,2},{2,1},{3,4},{4,3},{5,6},{6,5},{7,8},{8,7},{9,10},{10,9},{11,... | collective-permute-start | bytes 786440 | tf_op jit(solution)/shard_map/ppermute | solution.py:441
  13.4 1.4 %copy-done.2 = s32[1,1,6,256,256]{4,3,2,1,0:T(8,128)S(1)} copy-done((s32[1,1,6,256,256]{4,3,2,1,0:T(8,128)S(1)}, s32[1,1,6,256,256]{4,3,2,1,0:T(8,128)}, u32[]{:S(2)}) %copy-start.2) | copy-done | bytes 1572888
  15.8 3.5 %shard_map.110 = (f32[6,2,128,256]{3,2,1,0:T(8,128)S(1)}, f32[6,2,256,256]{3,2,1,0:T(8,128)S(1)}) custom-call(s32[1,1,6,2]{3,2,1,0:T(8,128)S(1)} %copy.15.positions, s32[6,256,256]{2,1,0:T(8,128)S(1)} %bitcast.21, f32[2,256,256]{2,1,0:T(8,128)S(1)} %copy-done.3), custom_call_target="tpu_custom_call" | custom-call | flops 805306368 | bytes 8388608 | tf_op jit(solution)/shard_map/pallas_call | solution.py:119
  20.1 2.8 %collective-permute-start.3 = (f32[2,2,128,128]{3,2,1,0:T(8,128)S(1)}, f32[2,2,128,128]{3,2,1,0:T(8,128)S(1)}, u32[]{:S(2)}, u32[]{:S(2)}) collective-permute-start(f32[2,2,128,128]{3,2,1,0:T(8,128)S(1)} %get-tuple-element.49), channel_id=1, source_target_pairs={{1,2},{2,1},{3,4},{4,3},{5,6},{6,5},{7,8},{8,7},{9,10},{10,9},{11,... | collective-permute-start | bytes 786440 | tf_op jit(solution)/shard_map/ppermute | solution.py:441
  23.0 2.2 %all-gather = f32[4,256,128]{2,1,0:T(8,128)S(1)} all-gather(f32[2,256,128]{2,1,0:T(8,128)S(1)} %get-tuple-element.46), channel_id=2, replica_groups={{0,1},{2,3},{4,5},{6,7},{8,9},{10,11},{12,13},{14,15},{16,17},{18,19},{..., dimensions={0}, use_global_device_ids=true | all-gather | bytes 786432 | tf_op jit(solution)/shard_map/all_gather | solution.py:446
  25.2 2.2 %all-gather.1 = f32[4,2,128,128]{3,2,1,0:T(8,128)S(1)} all-gather(f32[2,2,128,128]{3,2,1,0:T(8,128)S(1)} %get-tuple-element.47), channel_id=3, replica_groups={{0,1},{2,3},{4,5},{6,7},{8,9},{10,11},{12,13},{14,15},{16,17},{18,19},{..., dimensions={0}, use_global_device_ids=true | all-gather | bytes 786432 | tf_op jit(solution)/shard_map/all_gather | solution.py:446
  27.3 2.6 %collective-permute-done.3.refs_3_ = f32[2,2,128,128]{3,2,1,0:T(8,128)S(1)} collective-permute-done((f32[2,2,128,128]{3,2,1,0:T(8,128)S(1)}, f32[2,2,128,128]{3,2,1,0:T(8,128)S(1)}, u32[]{:S(2)}, u32[]{:S(2)}) %collective-permute-start.3) | collective-permute-done | bytes 262176 | tf_op jit(solution)/shard_map/ppermute | solution.py:441
  30.0 8.3 %shard_map.112 = (f32[512,128]{1,0:T(8,128)S(1)}, f32[512,128]{1,0:T(8,128)S(1)}, f32[2,512,128]{2,1,0:T(8,128)S(1)}, f32[2,512,128]{2,1,0:T(8,128)S(1)}, f32[2,512,128]{2,1,0:T(8,128)S(1)}) custom-call(s32[4]{0:T(128)S(1)} %pad_add_fusion.info, s32[1,1,6,2]{3,2,1,0:T(8,128)S(1)} %copy.15.positions, s32[1,1]{1,0:T(1,128)S(6)} %copy.18.counts, ...), custom_call_target="tpu_custom_call" | custom-call | flops 4831838208 | bytes 8388608 | tf_op jit(solution)/shard_map/pallas_call | solution.py:43
  38.2 1.9 %collective-permute-start.6 = (f32[2,512,128]{2,1,0:T(8,128)S(1)}, f32[2,512,128]{2,1,0:T(8,128)S(1)}, u32[]{:S(2)}, u32[]{:S(2)}) collective-permute-start(f32[2,512,128]{2,1,0:T(8,128)S(1)} %get-tuple-element.60), channel_id=1, source_target_pairs={{1,2},{2,1},{3,4},{4,3},{5,6},{6,5},{7,8},{8,7},{9,10},{10,9},{11,... | collective-permute-start | bytes 1572872 | tf_op jit(solution)/shard_map/ppermute | solution.py:441
  40.2 10.7 %collective-permute-done.6.strip = f32[2,512,128]{2,1,0:T(8,128)S(1)} collective-permute-done((f32[2,512,128]{2,1,0:T(8,128)S(1)}, f32[2,512,128]{2,1,0:T(8,128)S(1)}, u32[]{:S(2)}, u32[]{:S(2)}) %collective-permute-start.6) | collective-permute-done | bytes 524320 | tf_op jit(solution)/shard_map/ppermute | solution.py:441
  51.5 3.6 %collective-permute-start.7 = (f32[2,256,128]{2,1,0:T(8,128)S(1)}, f32[2,256,128]{2,1,0:T(8,128)S(1)}, u32[]{:S(2)}, u32[]{:S(2)}) collective-permute-start(f32[2,256,128]{2,1,0:T(8,128)S(1)} %get-tuple-element.62), channel_id=1, source_target_pairs={{0,16},{16,0},{32,48},{48,32},{64,80},{80,64},{96,112},{112,96},{1... | collective-permute-start | bytes 786440 | tf_op jit(solution)/shard_map/ppermute | solution.py:441
  55.1 2.5 %collective-permute-start.8 = (f32[2,256,128]{2,1,0:T(8,128)S(1)}, f32[2,256,128]{2,1,0:T(8,128)S(1)}, u32[]{:S(2)}, u32[]{:S(2)}) collective-permute-start(f32[2,256,128]{2,1,0:T(8,128)S(1)} %get-tuple-element.63), channel_id=1, source_target_pairs={{16,32},{32,16},{48,64},{64,48},{80,96},{96,80},{17,33},{33,17},{4... | collective-permute-start | bytes 786440 | tf_op jit(solution)/shard_map/ppermute | solution.py:441
  57.5 2.2 %all-gather.2 = f32[1024,128]{1,0:T(8,128)S(1)} all-gather(f32[512,128]{1,0:T(8,128)S(1)} %get-tuple-element.52), channel_id=4, replica_groups={{0,1},{2,3},{4,5},{6,7},{8,9},{10,11},{12,13},{14,15},{16,17},{18,19},{..., dimensions={0}, use_global_device_ids=true | all-gather | bytes 786432 | tf_op jit(solution)/shard_map/all_gather | solution.py:446
  59.7 2.2 %all-gather.3 = f32[1024,128]{1,0:T(8,128)S(1)} all-gather(f32[512,128]{1,0:T(8,128)S(1)} %get-tuple-element.53), channel_id=5, replica_groups={{0,1},{2,3},{4,5},{6,7},{8,9},{10,11},{12,13},{14,15},{16,17},{18,19},{..., dimensions={0}, use_global_device_ids=true | all-gather | bytes 786432 | tf_op jit(solution)/shard_map/all_gather | solution.py:446
  63.9 4.5 %collective-permute-start.5 = (f32[2,256,128]{2,1,0:T(8,128)S(1)}, f32[2,256,128]{2,1,0:T(8,128)S(1)}, u32[]{:S(2)}, u32[]{:S(2)}) collective-permute-start(f32[2,256,128]{2,1,0:T(8,128)S(1)} %get-tuple-element.56), channel_id=1, source_target_pairs={{16,32},{32,16},{48,64},{64,48},{80,96},{96,80},{17,33},{33,17},{4... | collective-permute-start | bytes 786440 | tf_op jit(solution)/shard_map/ppermute | solution.py:441
  69.1 1.9 %collective-permute-start.9 = (f32[2,512,128]{2,1,0:T(8,128)S(1)}, f32[2,512,128]{2,1,0:T(8,128)S(1)}, u32[]{:S(2)}, u32[]{:S(2)}) collective-permute-start(f32[2,512,128]{2,1,0:T(8,128)S(1)} %shard_map.116.ext_b), channel_id=1, source_target_pairs={{1,2},{2,1},{3,4},{4,3},{5,6},{6,5},{7,8},{8,7},{9,10},{10,9},{11,... | collective-permute-start | bytes 1572872 | tf_op jit(solution)/shard_map/ppermute | solution.py:441
  71.0 2.3 %collective-permute-done.4.halo_a = f32[2,256,128]{2,1,0:T(8,128)S(1)} collective-permute-done((f32[2,256,128]{2,1,0:T(8,128)S(1)}, f32[2,256,128]{2,1,0:T(8,128)S(1)}, u32[]{:S(2)}, u32[]{:S(2)}) %collective-permute-start.4) | collective-permute-done | bytes 262176 | tf_op jit(solution)/shard_map/ppermute | solution.py:441
  73.3 5.4 %collective-permute-done.5.halo_b = f32[2,256,128]{2,1,0:T(8,128)S(1)} collective-permute-done((f32[2,256,128]{2,1,0:T(8,128)S(1)}, f32[2,256,128]{2,1,0:T(8,128)S(1)}, u32[]{:S(2)}, u32[]{:S(2)}) %collective-permute-start.5) | collective-permute-done | bytes 262176 | tf_op jit(solution)/shard_map/ppermute | solution.py:441
  79.4 2.2 %all-gather.4 = f32[1024,128]{1,0:T(8,128)S(1)} all-gather(f32[512,128]{1,0:T(8,128)S(1)} %get-tuple-element.57.ext_r), channel_id=6, replica_groups={{0,1},{2,3},{4,5},{6,7},{8,9},{10,11},{12,13},{14,15},{16,17},{18,19},{..., dimensions={0}, use_global_device_ids=true | all-gather | bytes 786432 | tf_op jit(solution)/shard_map/all_gather | solution.py:446
  81.5 2.2 %all-gather.5 = f32[1024,128]{1,0:T(8,128)S(1)} all-gather(f32[512,128]{1,0:T(8,128)S(1)} %get-tuple-element.58.ext_i), channel_id=7, replica_groups={{0,1},{2,3},{4,5},{6,7},{8,9},{10,11},{12,13},{14,15},{16,17},{18,19},{..., dimensions={0}, use_global_device_ids=true | all-gather | bytes 786432 | tf_op jit(solution)/shard_map/all_gather | solution.py:446
  83.7 8.2 %shard_map.117 = (f32[512,128]{1,0:T(8,128)S(1)}, f32[512,128]{1,0:T(8,128)S(1)}, f32[2,512,128]{2,1,0:T(8,128)S(1)}, f32[2,512,128]{2,1,0:T(8,128)S(1)}, f32[2,512,128]{2,1,0:T(8,128)S(1)}) custom-call(s32[4]{0:T(128)S(1)} %pad_add_fusion.info, s32[1,1,6,2]{3,2,1,0:T(8,128)S(1)} %copy.15.positions, s32[1,1]{1,0:T(1,128)S(6)} %copy.18.counts, ...), custom_call_target="tpu_custom_call" | custom-call | flops 4831838208 | bytes 8388608 | tf_op jit(solution)/shard_map/pallas_call | solution.py:43
  92.0 1.9 %collective-permute-start.10 = (f32[2,512,128]{2,1,0:T(8,128)S(1)}, f32[2,512,128]{2,1,0:T(8,128)S(1)}, u32[]{:S(2)}, u32[]{:S(2)}) collective-permute-start(f32[2,512,128]{2,1,0:T(8,128)S(1)} %get-tuple-element.69), channel_id=1, source_target_pairs={{1,2},{2,1},{3,4},{4,3},{5,6},{6,5},{7,8},{8,7},{9,10},{10,9},{11,... | collective-permute-start | bytes 1572872 | tf_op jit(solution)/shard_map/ppermute | solution.py:441
  93.9 2.2 %all-gather.6 = f32[1024,128]{1,0:T(8,128)S(1)} all-gather(f32[512,128]{1,0:T(8,128)S(1)} %get-tuple-element.65), channel_id=8, replica_groups={{0,1},{2,3},{4,5},{6,7},{8,9},{10,11},{12,13},{14,15},{16,17},{18,19},{..., dimensions={0}, use_global_device_ids=true | all-gather | bytes 786432 | tf_op jit(solution)/shard_map/all_gather | solution.py:446
  96.1 2.2 %all-gather.7 = f32[1024,128]{1,0:T(8,128)S(1)} all-gather(f32[512,128]{1,0:T(8,128)S(1)} %get-tuple-element.66), channel_id=9, replica_groups={{0,1},{2,3},{4,5},{6,7},{8,9},{10,11},{12,13},{14,15},{16,17},{18,19},{..., dimensions={0}, use_global_device_ids=true | all-gather | bytes 786432 | tf_op jit(solution)/shard_map/all_gather | solution.py:446
  99.0 6.0 %collective-permute-start.12 = (f32[2,128,128]{2,1,0:T(8,128)S(1)}, f32[2,128,128]{2,1,0:T(8,128)S(1)}, u32[]{:S(2)}, u32[]{:S(2)}) collective-permute-start(f32[2,128,128]{2,1,0:T(8,128)S(1)} %get-tuple-element.72), channel_id=1, source_target_pairs={{16,32},{32,16},{48,64},{64,48},{80,96},{96,80},{17,33},{33,17},{4... | collective-permute-start | bytes 393224 | tf_op jit(solution)/shard_map/ppermute | solution.py:441
  106.3 3.6 %collective-permute-start.14 = (f32[2,128,128]{2,1,0:T(8,128)S(1)}, f32[2,128,128]{2,1,0:T(8,128)S(1)}, u32[]{:S(2)}, u32[]{:S(2)}) collective-permute-start(f32[2,128,128]{2,1,0:T(8,128)S(1)} %get-tuple-element.74), channel_id=1, source_target_pairs={{16,32},{32,16},{48,64},{64,48},{80,96},{96,80},{17,33},{33,17},{4... | collective-permute-start | bytes 393224 | tf_op jit(solution)/shard_map/ppermute | solution.py:441
  109.9 1.9 %collective-permute-done.12.near_b = f32[2,128,128]{2,1,0:T(8,128)S(1)} collective-permute-done((f32[2,128,128]{2,1,0:T(8,128)S(1)}, f32[2,128,128]{2,1,0:T(8,128)S(1)}, u32[]{:S(2)}, u32[]{:S(2)}) %collective-permute-start.12) | collective-permute-done | bytes 131104 | tf_op jit(solution)/shard_map/ppermute | solution.py:441
  111.8 1.4 %collective-permute-done.13.far_a = f32[2,128,128]{2,1,0:T(8,128)S(1)} collective-permute-done((f32[2,128,128]{2,1,0:T(8,128)S(1)}, f32[2,128,128]{2,1,0:T(8,128)S(1)}, u32[]{:S(2)}, u32[]{:S(2)}) %collective-permute-start.13) | collective-permute-done | bytes 131104 | tf_op jit(solution)/shard_map/ppermute | solution.py:441
  113.2 3.2 %collective-permute-done.14.far_b = f32[2,128,128]{2,1,0:T(8,128)S(1)} collective-permute-done((f32[2,128,128]{2,1,0:T(8,128)S(1)}, f32[2,128,128]{2,1,0:T(8,128)S(1)}, u32[]{:S(2)}, u32[]{:S(2)}) %collective-permute-start.14) | collective-permute-done | bytes 131104 | tf_op jit(solution)/shard_map/ppermute | solution.py:441
  116.4 1.4 %shard_map.120 = f32[2,256,256]{2,1,0:T(8,128)} custom-call(s32[4]{0:T(128)S(1)} %pad_add_fusion.info, f32[512,128]{1,0:T(8,128)S(1)} %get-tuple-element.57.ext_r, f32[512,128]{1,0:T(8,128)S(1)} %get-tuple-element.58.ext_i, f32[2,512,128]{2,1,0:T(8,128)S(1)} %shard_map.116.ext_b, f32[2,512,128]{2,1,0:T(8,128)S(1)} %get-tuple-element.67.total_a, ...), custom_call_target="tpu_custom_call" | custom-call | flops 1048576 | bytes 4194304 | tf_op jit(solution)/shard_map/pallas_call | solution.py:411
  (40 shorter events, 10.2 us)
Async XLA Ops:
  0.1 1.0 copy-start
  1.7 17.6 %copy-start.1 = (f32[2,256,256]{2,1,0:T(8,128)S(1)}, f32[2,256,256]{2,1,0:T(8,128)}, u32[]{:S(2)}) copy-start(f32[2,256,256]{2,1,0:T(8,128)} %tile.3) | copy-start | bytes 1572868
  1.8 17.6 %collective-permute-start = (f32[2,128,256]{2,1,0:T(8,128)S(1)}, f32[2,128,256]{2,1,0:T(8,128)S(1)}, u32[]{:S(2)}, u32[]{:S(2)}) collective-permute-start(f32[2,128,256]{2,1,0:T(8,128)S(1)} %get-tuple-element.40), channel_id=1, source_target_pairs={{0,16},{16,0},{32,48},{48,32},{64,80},{80,64},{96,112},{112,96},{1... | collective-permute-start | bytes 786440 | tf_op jit(solution)/shard_map/ppermute | solution.py:441
  4.0 15.4 %collective-permute-start.1 = (f32[2,128,256]{2,1,0:T(8,128)S(1)}, f32[2,128,256]{2,1,0:T(8,128)S(1)}, u32[]{:S(2)}, u32[]{:S(2)}) collective-permute-start(f32[2,128,256]{2,1,0:T(8,128)S(1)} %get-tuple-element.41), channel_id=1, source_target_pairs={{16,32},{32,16},{48,64},{64,48},{80,96},{96,80},{17,33},{33,17},{4... | collective-permute-start | bytes 786440 | tf_op jit(solution)/shard_map/ppermute | solution.py:441
  7.2 20.2 %collective-permute-start.2 = (f32[2,256,128]{2,1,0:T(8,128)S(1)}, f32[2,256,128]{2,1,0:T(8,128)S(1)}, u32[]{:S(2)}, u32[]{:S(2)}) collective-permute-start(f32[2,256,128]{2,1,0:T(8,128)S(1)} %get-tuple-element.48), channel_id=1, source_target_pairs={{1,2},{2,1},{3,4},{4,3},{5,6},{6,5},{7,8},{8,7},{9,10},{10,9},{11,... | collective-permute-start | bytes 786440 | tf_op jit(solution)/shard_map/ppermute | solution.py:441
  13.4 1.4 %copy-start.2 = (s32[1,1,6,256,256]{4,3,2,1,0:T(8,128)S(1)}, s32[1,1,6,256,256]{4,3,2,1,0:T(8,128)}, u32[]{:S(2)}) copy-start(s32[1,1,6,256,256]{4,3,2,1,0:T(8,128)} %param.15) | copy-start | bytes 4718596
  14.8 1.0 copy-start.3
  19.4 10.5 %copy-start.4 = (bf16[768,256]{1,0:T(8,128)(2,1)S(1)}, bf16[768,256]{1,0:T(8,128)(2,1)}, u32[]{:S(2)}) copy-start(bf16[768,256]{1,0:T(8,128)(2,1)} %constant.44.clone.refs_9_.refs_8_) | copy-start | bytes 1179652
  19.4 10.5 %copy-start.5 = (bf16[256,768]{1,0:T(8,128)(2,1)S(1)}, bf16[256,768]{1,0:T(8,128)(2,1)}, u32[]{:S(2)}) copy-start(bf16[256,768]{1,0:T(8,128)(2,1)} %constant.43.clone.refs_7_.refs_6_) | copy-start | bytes 1179652
  19.4 10.5 %copy-start.6 = (bf16[256,768]{1,0:T(8,128)(2,1)S(1)}, bf16[256,768]{1,0:T(8,128)(2,1)}, u32[]{:S(2)}) copy-start(bf16[256,768]{1,0:T(8,128)(2,1)} %constant.42.clone.refs_8_.refs_7_) | copy-start | bytes 1179652
  19.4 10.5 %copy-start.7 = (bf16[768,256]{1,0:T(8,128)(2,1)S(1)}, bf16[768,256]{1,0:T(8,128)(2,1)}, u32[]{:S(2)}) copy-start(bf16[768,256]{1,0:T(8,128)(2,1)} %constant.41.clone.refs_6_.refs_5_) | copy-start | bytes 1179652
  19.4 10.5 %copy-start.8 = (f32[2,128,256]{2,1,0:T(8,128)S(1)}, f32[2,128,256]{2,1,0:T(8,128)}, u32[]{:S(2)}) copy-start(f32[2,128,256]{2,1,0:T(8,128)} %constant.46.clone.refs_11_.refs_10_) | copy-start | bytes 786436
  19.5 10.5 %copy-start.9 = (f32[2,1,128]{2,1,0:T(1,128)S(1)}, f32[2,1,128]{2,1,0:T(1,128)}, u32[]{:S(2)}) copy-start(f32[2,1,128]{2,1,0:T(1,128)} %constant.45.clone.refs_10_.refs_9_) | copy-start | bytes 3076
  20.1 9.8 %collective-permute-start.3 = (f32[2,2,128,128]{3,2,1,0:T(8,128)S(1)}, f32[2,2,128,128]{3,2,1,0:T(8,128)S(1)}, u32[]{:S(2)}, u32[]{:S(2)}) collective-permute-start(f32[2,2,128,128]{3,2,1,0:T(8,128)S(1)} %get-tuple-element.49), channel_id=1, source_target_pairs={{1,2},{2,1},{3,4},{4,3},{5,6},{6,5},{7,8},{8,7},{9,10},{10,9},{11,... | collective-permute-start | bytes 786440 | tf_op jit(solution)/shard_map/ppermute | solution.py:441
  38.2 12.6 %collective-permute-start.6 = (f32[2,512,128]{2,1,0:T(8,128)S(1)}, f32[2,512,128]{2,1,0:T(8,128)S(1)}, u32[]{:S(2)}, u32[]{:S(2)}) collective-permute-start(f32[2,512,128]{2,1,0:T(8,128)S(1)} %get-tuple-element.60), channel_id=1, source_target_pairs={{1,2},{2,1},{3,4},{4,3},{5,6},{6,5},{7,8},{8,7},{9,10},{10,9},{11,... | collective-permute-start | bytes 1572872 | tf_op jit(solution)/shard_map/ppermute | solution.py:441
  51.5 16.9 %collective-permute-start.7 = (f32[2,256,128]{2,1,0:T(8,128)S(1)}, f32[2,256,128]{2,1,0:T(8,128)S(1)}, u32[]{:S(2)}, u32[]{:S(2)}) collective-permute-start(f32[2,256,128]{2,1,0:T(8,128)S(1)} %get-tuple-element.62), channel_id=1, source_target_pairs={{0,16},{16,0},{32,48},{48,32},{64,80},{80,64},{96,112},{112,96},{1... | collective-permute-start | bytes 786440 | tf_op jit(solution)/shard_map/ppermute | solution.py:441
  55.1 13.3 %collective-permute-start.8 = (f32[2,256,128]{2,1,0:T(8,128)S(1)}, f32[2,256,128]{2,1,0:T(8,128)S(1)}, u32[]{:S(2)}, u32[]{:S(2)}) collective-permute-start(f32[2,256,128]{2,1,0:T(8,128)S(1)} %get-tuple-element.63), channel_id=1, source_target_pairs={{16,32},{32,16},{48,64},{64,48},{80,96},{96,80},{17,33},{33,17},{4... | collective-permute-start | bytes 786440 | tf_op jit(solution)/shard_map/ppermute | solution.py:441
  62.5 10.7 %collective-permute-start.4 = (f32[2,256,128]{2,1,0:T(8,128)S(1)}, f32[2,256,128]{2,1,0:T(8,128)S(1)}, u32[]{:S(2)}, u32[]{:S(2)}) collective-permute-start(f32[2,256,128]{2,1,0:T(8,128)S(1)} %get-tuple-element.55), channel_id=1, source_target_pairs={{0,16},{16,0},{32,48},{48,32},{64,80},{80,64},{96,112},{112,96},{1... | collective-permute-start | bytes 786440 | tf_op jit(solution)/shard_map/ppermute | solution.py:441
  63.9 14.8 %collective-permute-start.5 = (f32[2,256,128]{2,1,0:T(8,128)S(1)}, f32[2,256,128]{2,1,0:T(8,128)S(1)}, u32[]{:S(2)}, u32[]{:S(2)}) collective-permute-start(f32[2,256,128]{2,1,0:T(8,128)S(1)} %get-tuple-element.56), channel_id=1, source_target_pairs={{16,32},{32,16},{48,64},{64,48},{80,96},{96,80},{17,33},{33,17},{4... | collective-permute-start | bytes 786440 | tf_op jit(solution)/shard_map/ppermute | solution.py:441
  69.1 14.6 %collective-permute-start.9 = (f32[2,512,128]{2,1,0:T(8,128)S(1)}, f32[2,512,128]{2,1,0:T(8,128)S(1)}, u32[]{:S(2)}, u32[]{:S(2)}) collective-permute-start(f32[2,512,128]{2,1,0:T(8,128)S(1)} %shard_map.116.ext_b), channel_id=1, source_target_pairs={{1,2},{2,1},{3,4},{4,3},{5,6},{6,5},{7,8},{8,7},{9,10},{10,9},{11,... | collective-permute-start | bytes 1572872 | tf_op jit(solution)/shard_map/ppermute | solution.py:441
  92.0 13.1 %collective-permute-start.10 = (f32[2,512,128]{2,1,0:T(8,128)S(1)}, f32[2,512,128]{2,1,0:T(8,128)S(1)}, u32[]{:S(2)}, u32[]{:S(2)}) collective-permute-start(f32[2,512,128]{2,1,0:T(8,128)S(1)} %get-tuple-element.69), channel_id=1, source_target_pairs={{1,2},{2,1},{3,4},{4,3},{5,6},{6,5},{7,8},{8,7},{9,10},{10,9},{11,... | collective-permute-start | bytes 1572872 | tf_op jit(solution)/shard_map/ppermute | solution.py:441
  98.9 11.1 %collective-permute-start.11 = (f32[2,128,128]{2,1,0:T(8,128)S(1)}, f32[2,128,128]{2,1,0:T(8,128)S(1)}, u32[]{:S(2)}, u32[]{:S(2)}) collective-permute-start(f32[2,128,128]{2,1,0:T(8,128)S(1)} %get-tuple-element.71), channel_id=1, source_target_pairs={{0,16},{16,0},{32,48},{48,32},{64,80},{80,64},{96,112},{112,96},{1... | collective-permute-start | bytes 393224 | tf_op jit(solution)/shard_map/ppermute | solution.py:441
  99.0 12.8 %collective-permute-start.12 = (f32[2,128,128]{2,1,0:T(8,128)S(1)}, f32[2,128,128]{2,1,0:T(8,128)S(1)}, u32[]{:S(2)}, u32[]{:S(2)}) collective-permute-start(f32[2,128,128]{2,1,0:T(8,128)S(1)} %get-tuple-element.72), channel_id=1, source_target_pairs={{16,32},{32,16},{48,64},{64,48},{80,96},{96,80},{17,33},{33,17},{4... | collective-permute-start | bytes 393224 | tf_op jit(solution)/shard_map/ppermute | solution.py:441
  105.7 7.5 %collective-permute-start.13 = (f32[2,128,128]{2,1,0:T(8,128)S(1)}, f32[2,128,128]{2,1,0:T(8,128)S(1)}, u32[]{:S(2)}, u32[]{:S(2)}) collective-permute-start(f32[2,128,128]{2,1,0:T(8,128)S(1)} %get-tuple-element.73), channel_id=1, source_target_pairs={{0,16},{16,0},{32,48},{48,32},{64,80},{80,64},{96,112},{112,96},{1... | collective-permute-start | bytes 393224 | tf_op jit(solution)/shard_map/ppermute | solution.py:441
  106.3 10.1 %collective-permute-start.14 = (f32[2,128,128]{2,1,0:T(8,128)S(1)}, f32[2,128,128]{2,1,0:T(8,128)S(1)}, u32[]{:S(2)}, u32[]{:S(2)}) collective-permute-start(f32[2,128,128]{2,1,0:T(8,128)S(1)} %get-tuple-element.74), channel_id=1, source_target_pairs={{16,32},{32,16},{48,64},{64,48},{80,96},{96,80},{17,33},{33,17},{4... | collective-permute-start | bytes 393224 | tf_op jit(solution)/shard_map/ppermute | solution.py:441

commit v4 on v3

--- a/solution.py
+++ b/solution.py
@@ -347,7 +347,7 @@
     outgoing(info[0], total, width, out_a, out_b)
 
 
-def join_far_body(width, info, inner, strip, total, out_a, out_b):
+def join_far_body(width, info, inner, strip, earlier, total, out_a, out_b):
     total[...] = inner[...] + strip[...]
     outgoing(info[0], total, width, out_a, out_b)
 
@@ -457,7 +457,13 @@
     near = paired(out_r), paired(out_i)
     total_a, *edges = whole(functools.partial(join_near_body, width), (strip, piece, piece), (info,), (in_a, *near))
     halos_a = both_rows(*edges)
-    total_b, *edges = whole(functools.partial(join_far_body, width), (strip, piece, piece), (info,), (in_b, far))
+    total_b, *edges = whole(
+        functools.partial(join_far_body, width),
+        (strip, piece, piece),
+        (info,),
+        (in_b, far),
+        unread=edges[:1],
+    )
     halos_b = both_rows(*edges)
     return total_a, halos_a, total_b, halos_b
 

time: 120 us -> 119 us (level); the launches traced: 118 us -> 119 us
  transfers between devices with their start and end apart: 15 -> 15, of which waited for: 7 -> 9; matrix products, arithmetic and copies ran while one was open for 1% -> 1% of each run, Pallas kernels for 6% -> 6%
where the time goes in v4:
time: 119 us
  starting transfers between devices  40.7 us (34%)
  waiting for transfers between devices  28.6 us (24%)
  Pallas kernels  26.5 us (22%)
  blocking collectives  17.4 us (15%)
  local copies, waits for them, and re-layouts  4.31 us (4%)
    ppermute x15, starting transfers between devices, swapped(): return lax.ppermute(value, axis, route)  40.7 us
    ppermute x15, waiting for transfers between devices, swapped(): return lax.ppermute(value, axis, route)  28.6 us
    pallas_call x10, Pallas kernels, whole(): pl.pallas_call(body, out_shape=outs, in_specs=[SMEM] * len(scalars) + [VM...  21.5 us
    all_gather x8, blocking collectives, paired(): return lax.all_gather(value, 'cols', axis_index_groups=groups)  17.4 us
    unnamed x21, local copies, waits for them, and re-layouts  4.31 us
    pallas_call x1, Pallas kernels, prepare(): pl.pallas_call(prepare_body, out_shape=(shaped(slots, 2, half, size), sha...  3.52 us
  transfers between devices with their start and end apart: 15, of which 9 were waited for; matrix products, arithmetic and copies ran while one was open for 1% of the time, Pallas kernels for 6%

profile of v4, /device:TPU:10, one launch (start us, length us, event | category | flops | bytes accessed | tf_op | source)
XLA Modules:
  0.0 118.6 jit_solution(8987052287069397516)
XLA Ops:
  1.8 2.2 %collective-permute-start = (f32[2,128,256]{2,1,0:T(8,128)S(1)}, f32[2,128,256]{2,1,0:T(8,128)S(1)}, u32[]{:S(2)}, u32[]{:S(2)}) collective-permute-start(f32[2,128,256]{2,1,0:T(8,128)S(1)} %get-tuple-element.40), channel_id=1, source_target_pairs={{0,16},{16,0},{32,48},{48,32},{64,80},{80,64},{96,112},{112,96},{1... | collective-permute-start | bytes 786440 | tf_op jit(solution)/shard_map/ppermute | solution.py:441
  4.0 3.2 %collective-permute-start.1 = (f32[2,128,256]{2,1,0:T(8,128)S(1)}, f32[2,128,256]{2,1,0:T(8,128)S(1)}, u32[]{:S(2)}, u32[]{:S(2)}) collective-permute-start(f32[2,128,256]{2,1,0:T(8,128)S(1)} %get-tuple-element.41), channel_id=1, source_target_pairs={{16,32},{32,16},{48,64},{64,48},{80,96},{96,80},{17,33},{33,17},{4... | collective-permute-start | bytes 786440 | tf_op jit(solution)/shard_map/ppermute | solution.py:441
  7.2 4.8 %collective-permute-start.2 = (f32[2,256,128]{2,1,0:T(8,128)S(1)}, f32[2,256,128]{2,1,0:T(8,128)S(1)}, u32[]{:S(2)}, u32[]{:S(2)}) collective-permute-start(f32[2,256,128]{2,1,0:T(8,128)S(1)} %get-tuple-element.48), channel_id=1, source_target_pairs={{1,2},{2,1},{3,4},{4,3},{5,6},{6,5},{7,8},{8,7},{9,10},{10,9},{11,... | collective-permute-start | bytes 786440 | tf_op jit(solution)/shard_map/ppermute | solution.py:441
  15.8 3.5 %shard_map.110 = (f32[6,2,128,256]{3,2,1,0:T(8,128)S(1)}, f32[6,2,256,256]{3,2,1,0:T(8,128)S(1)}) custom-call(s32[1,1,6,2]{3,2,1,0:T(8,128)S(1)} %copy.15.positions, s32[6,256,256]{2,1,0:T(8,128)S(1)} %bitcast.21, f32[2,256,256]{2,1,0:T(8,128)S(1)} %copy-done.3), custom_call_target="tpu_custom_call" | custom-call | flops 805306368 | bytes 8388608 | tf_op jit(solution)/shard_map/pallas_call | solution.py:119
  20.1 2.8 %collective-permute-start.3 = (f32[2,2,128,128]{3,2,1,0:T(8,128)S(1)}, f32[2,2,128,128]{3,2,1,0:T(8,128)S(1)}, u32[]{:S(2)}, u32[]{:S(2)}) collective-permute-start(f32[2,2,128,128]{3,2,1,0:T(8,128)S(1)} %get-tuple-element.49), channel_id=1, source_target_pairs={{1,2},{2,1},{3,4},{4,3},{5,6},{6,5},{7,8},{8,7},{9,10},{10,9},{11,... | collective-permute-start | bytes 786440 | tf_op jit(solution)/shard_map/ppermute | solution.py:441
  23.0 2.2 %all-gather = f32[4,256,128]{2,1,0:T(8,128)S(1)} all-gather(f32[2,256,128]{2,1,0:T(8,128)S(1)} %get-tuple-element.46), channel_id=2, replica_groups={{0,1},{2,3},{4,5},{6,7},{8,9},{10,11},{12,13},{14,15},{16,17},{18,19},{..., dimensions={0}, use_global_device_ids=true | all-gather | bytes 786432 | tf_op jit(solution)/shard_map/all_gather | solution.py:446
  25.2 2.2 %all-gather.1 = f32[4,2,128,128]{3,2,1,0:T(8,128)S(1)} all-gather(f32[2,2,128,128]{3,2,1,0:T(8,128)S(1)} %get-tuple-element.47), channel_id=3, replica_groups={{0,1},{2,3},{4,5},{6,7},{8,9},{10,11},{12,13},{14,15},{16,17},{18,19},{..., dimensions={0}, use_global_device_ids=true | all-gather | bytes 786432 | tf_op jit(solution)/shard_map/all_gather | solution.py:446
  27.3 2.6 %collective-permute-done.3.refs_3_ = f32[2,2,128,128]{3,2,1,0:T(8,128)S(1)} collective-permute-done((f32[2,2,128,128]{3,2,1,0:T(8,128)S(1)}, f32[2,2,128,128]{3,2,1,0:T(8,128)S(1)}, u32[]{:S(2)}, u32[]{:S(2)}) %collective-permute-start.3) | collective-permute-done | bytes 262176 | tf_op jit(solution)/shard_map/ppermute | solution.py:441
  30.0 8.2 %shard_map.112 = (f32[512,128]{1,0:T(8,128)S(1)}, f32[512,128]{1,0:T(8,128)S(1)}, f32[2,512,128]{2,1,0:T(8,128)S(1)}, f32[2,512,128]{2,1,0:T(8,128)S(1)}, f32[2,512,128]{2,1,0:T(8,128)S(1)}) custom-call(s32[4]{0:T(128)S(1)} %pad_add_fusion.info, s32[1,1,6,2]{3,2,1,0:T(8,128)S(1)} %copy.15.positions, s32[1,1]{1,0:T(1,128)S(6)} %copy.18.counts, ...), custom_call_target="tpu_custom_call" | custom-call | flops 4831838208 | bytes 8388608 | tf_op jit(solution)/shard_map/pallas_call | solution.py:43
  38.2 1.9 %collective-permute-start.6 = (f32[2,512,128]{2,1,0:T(8,128)S(1)}, f32[2,512,128]{2,1,0:T(8,128)S(1)}, u32[]{:S(2)}, u32[]{:S(2)}) collective-permute-start(f32[2,512,128]{2,1,0:T(8,128)S(1)} %get-tuple-element.60), channel_id=1, source_target_pairs={{1,2},{2,1},{3,4},{4,3},{5,6},{6,5},{7,8},{8,7},{9,10},{10,9},{11,... | collective-permute-start | bytes 1572872 | tf_op jit(solution)/shard_map/ppermute | solution.py:441
  40.1 2.2 %all-gather.2 = f32[1024,128]{1,0:T(8,128)S(1)} all-gather(f32[512,128]{1,0:T(8,128)S(1)} %get-tuple-element.52), channel_id=4, replica_groups={{0,1},{2,3},{4,5},{6,7},{8,9},{10,11},{12,13},{14,15},{16,17},{18,19},{..., dimensions={0}, use_global_device_ids=true | all-gather | bytes 786432 | tf_op jit(solution)/shard_map/all_gather | solution.py:446
  42.3 2.2 %all-gather.3 = f32[1024,128]{1,0:T(8,128)S(1)} all-gather(f32[512,128]{1,0:T(8,128)S(1)} %get-tuple-element.53), channel_id=5, replica_groups={{0,1},{2,3},{4,5},{6,7},{8,9},{10,11},{12,13},{14,15},{16,17},{18,19},{..., dimensions={0}, use_global_device_ids=true | all-gather | bytes 786432 | tf_op jit(solution)/shard_map/all_gather | solution.py:446
  45.1 5.7 %collective-permute-done.6.strip = f32[2,512,128]{2,1,0:T(8,128)S(1)} collective-permute-done((f32[2,512,128]{2,1,0:T(8,128)S(1)}, f32[2,512,128]{2,1,0:T(8,128)S(1)}, u32[]{:S(2)}, u32[]{:S(2)}) %collective-permute-start.6) | collective-permute-done | bytes 524320 | tf_op jit(solution)/shard_map/ppermute | solution.py:441
  51.5 3.5 %collective-permute-start.7 = (f32[2,256,128]{2,1,0:T(8,128)S(1)}, f32[2,256,128]{2,1,0:T(8,128)S(1)}, u32[]{:S(2)}, u32[]{:S(2)}) collective-permute-start(f32[2,256,128]{2,1,0:T(8,128)S(1)} %get-tuple-element.62), channel_id=1, source_target_pairs={{0,16},{16,0},{32,48},{48,32},{64,80},{80,64},{96,112},{112,96},{1... | collective-permute-start | bytes 786440 | tf_op jit(solution)/shard_map/ppermute | solution.py:441
  55.0 1.9 %collective-permute-start.8 = (f32[2,256,128]{2,1,0:T(8,128)S(1)}, f32[2,256,128]{2,1,0:T(8,128)S(1)}, u32[]{:S(2)}, u32[]{:S(2)}) collective-permute-start(f32[2,256,128]{2,1,0:T(8,128)S(1)} %get-tuple-element.63), channel_id=1, source_target_pairs={{16,32},{32,16},{48,64},{64,48},{80,96},{96,80},{17,33},{33,17},{4... | collective-permute-start | bytes 786440 | tf_op jit(solution)/shard_map/ppermute | solution.py:441
  56.9 6.3 %collective-permute-start.5 = (f32[2,256,128]{2,1,0:T(8,128)S(1)}, f32[2,256,128]{2,1,0:T(8,128)S(1)}, u32[]{:S(2)}, u32[]{:S(2)}) collective-permute-start(f32[2,256,128]{2,1,0:T(8,128)S(1)} %get-tuple-element.56), channel_id=1, source_target_pairs={{16,32},{32,16},{48,64},{64,48},{80,96},{96,80},{17,33},{33,17},{4... | collective-permute-start | bytes 786440 | tf_op jit(solution)/shard_map/ppermute | solution.py:441
  63.4 5.1 %collective-permute-done.8.halo_b = f32[2,256,128]{2,1,0:T(8,128)S(1)} collective-permute-done((f32[2,256,128]{2,1,0:T(8,128)S(1)}, f32[2,256,128]{2,1,0:T(8,128)S(1)}, u32[]{:S(2)}, u32[]{:S(2)}) %collective-permute-start.8) | collective-permute-done | bytes 262176 | tf_op jit(solution)/shard_map/ppermute | solution.py:441
  69.2 1.9 %collective-permute-start.9 = (f32[2,512,128]{2,1,0:T(8,128)S(1)}, f32[2,512,128]{2,1,0:T(8,128)S(1)}, u32[]{:S(2)}, u32[]{:S(2)}) collective-permute-start(f32[2,512,128]{2,1,0:T(8,128)S(1)} %shard_map.116.ext_b), channel_id=1, source_target_pairs={{1,2},{2,1},{3,4},{4,3},{5,6},{6,5},{7,8},{8,7},{9,10},{10,9},{11,... | collective-permute-start | bytes 1572872 | tf_op jit(solution)/shard_map/ppermute | solution.py:441
  71.1 1.8 %collective-permute-done.5.halo_b = f32[2,256,128]{2,1,0:T(8,128)S(1)} collective-permute-done((f32[2,256,128]{2,1,0:T(8,128)S(1)}, f32[2,256,128]{2,1,0:T(8,128)S(1)}, u32[]{:S(2)}, u32[]{:S(2)}) %collective-permute-start.5) | collective-permute-done | bytes 262176 | tf_op jit(solution)/shard_map/ppermute | solution.py:441
  72.9 2.1 %collective-permute-done.4.halo_a = f32[2,256,128]{2,1,0:T(8,128)S(1)} collective-permute-done((f32[2,256,128]{2,1,0:T(8,128)S(1)}, f32[2,256,128]{2,1,0:T(8,128)S(1)}, u32[]{:S(2)}, u32[]{:S(2)}) %collective-permute-start.4) | collective-permute-done | bytes 262176 | tf_op jit(solution)/shard_map/ppermute | solution.py:441
  75.7 2.2 %all-gather.4 = f32[1024,128]{1,0:T(8,128)S(1)} all-gather(f32[512,128]{1,0:T(8,128)S(1)} %get-tuple-element.57.ext_r), channel_id=6, replica_groups={{0,1},{2,3},{4,5},{6,7},{8,9},{10,11},{12,13},{14,15},{16,17},{18,19},{..., dimensions={0}, use_global_device_ids=true | all-gather | bytes 786432 | tf_op jit(solution)/shard_map/all_gather | solution.py:446
  77.9 2.2 %all-gather.5 = f32[1024,128]{1,0:T(8,128)S(1)} all-gather(f32[512,128]{1,0:T(8,128)S(1)} %get-tuple-element.58.ext_i), channel_id=7, replica_groups={{0,1},{2,3},{4,5},{6,7},{8,9},{10,11},{12,13},{14,15},{16,17},{18,19},{..., dimensions={0}, use_global_device_ids=true | all-gather | bytes 786432 | tf_op jit(solution)/shard_map/all_gather | solution.py:446
  80.0 3.7 %collective-permute-done.9.refs_2_ = f32[2,512,128]{2,1,0:T(8,128)S(1)} collective-permute-done((f32[2,512,128]{2,1,0:T(8,128)S(1)}, f32[2,512,128]{2,1,0:T(8,128)S(1)}, u32[]{:S(2)}, u32[]{:S(2)}) %collective-permute-start.9) | collective-permute-done | bytes 524320 | tf_op jit(solution)/shard_map/ppermute | solution.py:441
  83.8 8.2 %shard_map.117 = (f32[512,128]{1,0:T(8,128)S(1)}, f32[512,128]{1,0:T(8,128)S(1)}, f32[2,512,128]{2,1,0:T(8,128)S(1)}, f32[2,512,128]{2,1,0:T(8,128)S(1)}, f32[2,512,128]{2,1,0:T(8,128)S(1)}) custom-call(s32[4]{0:T(128)S(1)} %pad_add_fusion.info, s32[1,1,6,2]{3,2,1,0:T(8,128)S(1)} %copy.15.positions, s32[1,1]{1,0:T(1,128)S(6)} %copy.18.counts, ...), custom_call_target="tpu_custom_call" | custom-call | flops 4831838208 | bytes 8388608 | tf_op jit(solution)/shard_map/pallas_call | solution.py:43
  92.0 1.9 %collective-permute-start.10 = (f32[2,512,128]{2,1,0:T(8,128)S(1)}, f32[2,512,128]{2,1,0:T(8,128)S(1)}, u32[]{:S(2)}, u32[]{:S(2)}) collective-permute-start(f32[2,512,128]{2,1,0:T(8,128)S(1)} %get-tuple-element.69), channel_id=1, source_target_pairs={{1,2},{2,1},{3,4},{4,3},{5,6},{6,5},{7,8},{8,7},{9,10},{10,9},{11,... | collective-permute-start | bytes 1572872 | tf_op jit(solution)/shard_map/ppermute | solution.py:441
  93.9 2.2 %all-gather.6 = f32[1024,128]{1,0:T(8,128)S(1)} all-gather(f32[512,128]{1,0:T(8,128)S(1)} %get-tuple-element.65), channel_id=8, replica_groups={{0,1},{2,3},{4,5},{6,7},{8,9},{10,11},{12,13},{14,15},{16,17},{18,19},{..., dimensions={0}, use_global_device_ids=true | all-gather | bytes 786432 | tf_op jit(solution)/shard_map/all_gather | solution.py:446
  96.1 2.2 %all-gather.7 = f32[1024,128]{1,0:T(8,128)S(1)} all-gather(f32[512,128]{1,0:T(8,128)S(1)} %get-tuple-element.66), channel_id=9, replica_groups={{0,1},{2,3},{4,5},{6,7},{8,9},{10,11},{12,13},{14,15},{16,17},{18,19},{..., dimensions={0}, use_global_device_ids=true | all-gather | bytes 786432 | tf_op jit(solution)/shard_map/all_gather | solution.py:446
  98.9 3.0 %collective-permute-start.12 = (f32[2,128,128]{2,1,0:T(8,128)S(1)}, f32[2,128,128]{2,1,0:T(8,128)S(1)}, u32[]{:S(2)}, u32[]{:S(2)}) collective-permute-start(f32[2,128,128]{2,1,0:T(8,128)S(1)} %get-tuple-element.72), channel_id=1, source_target_pairs={{16,32},{32,16},{48,64},{64,48},{80,96},{96,80},{17,33},{33,17},{4... | collective-permute-start | bytes 393224 | tf_op jit(solution)/shard_map/ppermute | solution.py:441
  102.7 1.9 %collective-permute-done.10.strip = f32[2,512,128]{2,1,0:T(8,128)S(1)} collective-permute-done((f32[2,512,128]{2,1,0:T(8,128)S(1)}, f32[2,512,128]{2,1,0:T(8,128)S(1)}, u32[]{:S(2)}, u32[]{:S(2)}) %collective-permute-start.10) | collective-permute-done | bytes 524320 | tf_op jit(solution)/shard_map/ppermute | solution.py:441
  106.2 5.2 %collective-permute-start.14 = (f32[2,128,128]{2,1,0:T(8,128)S(1)}, f32[2,128,128]{2,1,0:T(8,128)S(1)}, u32[]{:S(2)}, u32[]{:S(2)}) collective-permute-start(f32[2,128,128]{2,1,0:T(8,128)S(1)} %get-tuple-element.74), channel_id=1, source_target_pairs={{16,32},{32,16},{48,64},{64,48},{80,96},{96,80},{17,33},{33,17},{4... | collective-permute-start | bytes 393224 | tf_op jit(solution)/shard_map/ppermute | solution.py:441
  111.5 1.4 %collective-permute-done.13.far_a = f32[2,128,128]{2,1,0:T(8,128)S(1)} collective-permute-done((f32[2,128,128]{2,1,0:T(8,128)S(1)}, f32[2,128,128]{2,1,0:T(8,128)S(1)}, u32[]{:S(2)}, u32[]{:S(2)}) %collective-permute-start.13) | collective-permute-done | bytes 131104 | tf_op jit(solution)/shard_map/ppermute | solution.py:441
  112.9 4.3 %collective-permute-done.14.far_b = f32[2,128,128]{2,1,0:T(8,128)S(1)} collective-permute-done((f32[2,128,128]{2,1,0:T(8,128)S(1)}, f32[2,128,128]{2,1,0:T(8,128)S(1)}, u32[]{:S(2)}, u32[]{:S(2)}) %collective-permute-start.14) | collective-permute-done | bytes 131104 | tf_op jit(solution)/shard_map/ppermute | solution.py:441
  (40 shorter events, 12.9 us)
Async XLA Ops:
  0.1 1.0 copy-start
  1.7 17.6 %copy-start.1 = (f32[2,256,256]{2,1,0:T(8,128)S(1)}, f32[2,256,256]{2,1,0:T(8,128)}, u32[]{:S(2)}) copy-start(f32[2,256,256]{2,1,0:T(8,128)} %tile.3) | copy-start | bytes 1572868
  1.8 17.6 %collective-permute-start = (f32[2,128,256]{2,1,0:T(8,128)S(1)}, f32[2,128,256]{2,1,0:T(8,128)S(1)}, u32[]{:S(2)}, u32[]{:S(2)}) collective-permute-start(f32[2,128,256]{2,1,0:T(8,128)S(1)} %get-tuple-element.40), channel_id=1, source_target_pairs={{0,16},{16,0},{32,48},{48,32},{64,80},{80,64},{96,112},{112,96},{1... | collective-permute-start | bytes 786440 | tf_op jit(solution)/shard_map/ppermute | solution.py:441
  4.0 15.4 %collective-permute-start.1 = (f32[2,128,256]{2,1,0:T(8,128)S(1)}, f32[2,128,256]{2,1,0:T(8,128)S(1)}, u32[]{:S(2)}, u32[]{:S(2)}) collective-permute-start(f32[2,128,256]{2,1,0:T(8,128)S(1)} %get-tuple-element.41), channel_id=1, source_target_pairs={{16,32},{32,16},{48,64},{64,48},{80,96},{96,80},{17,33},{33,17},{4... | collective-permute-start | bytes 786440 | tf_op jit(solution)/shard_map/ppermute | solution.py:441
  7.2 20.2 %collective-permute-start.2 = (f32[2,256,128]{2,1,0:T(8,128)S(1)}, f32[2,256,128]{2,1,0:T(8,128)S(1)}, u32[]{:S(2)}, u32[]{:S(2)}) collective-permute-start(f32[2,256,128]{2,1,0:T(8,128)S(1)} %get-tuple-element.48), channel_id=1, source_target_pairs={{1,2},{2,1},{3,4},{4,3},{5,6},{6,5},{7,8},{8,7},{9,10},{10,9},{11,... | collective-permute-start | bytes 786440 | tf_op jit(solution)/shard_map/ppermute | solution.py:441
  13.4 1.4 %copy-start.2 = (s32[1,1,6,256,256]{4,3,2,1,0:T(8,128)S(1)}, s32[1,1,6,256,256]{4,3,2,1,0:T(8,128)}, u32[]{:S(2)}) copy-start(s32[1,1,6,256,256]{4,3,2,1,0:T(8,128)} %param.15) | copy-start | bytes 4718596
  14.8 1.0 copy-start.3
  19.4 10.5 %copy-start.4 = (bf16[768,256]{1,0:T(8,128)(2,1)S(1)}, bf16[768,256]{1,0:T(8,128)(2,1)}, u32[]{:S(2)}) copy-start(bf16[768,256]{1,0:T(8,128)(2,1)} %constant.44.clone.refs_9_.refs_8_) | copy-start | bytes 1179652
  19.4 10.5 %copy-start.5 = (bf16[256,768]{1,0:T(8,128)(2,1)S(1)}, bf16[256,768]{1,0:T(8,128)(2,1)}, u32[]{:S(2)}) copy-start(bf16[256,768]{1,0:T(8,128)(2,1)} %constant.43.clone.refs_7_.refs_6_) | copy-start | bytes 1179652
  19.4 10.5 %copy-start.6 = (bf16[256,768]{1,0:T(8,128)(2,1)S(1)}, bf16[256,768]{1,0:T(8,128)(2,1)}, u32[]{:S(2)}) copy-start(bf16[256,768]{1,0:T(8,128)(2,1)} %constant.42.clone.refs_8_.refs_7_) | copy-start | bytes 1179652
  19.4 10.5 %copy-start.7 = (bf16[768,256]{1,0:T(8,128)(2,1)S(1)}, bf16[768,256]{1,0:T(8,128)(2,1)}, u32[]{:S(2)}) copy-start(bf16[768,256]{1,0:T(8,128)(2,1)} %constant.41.clone.refs_6_.refs_5_) | copy-start | bytes 1179652
  19.4 10.5 %copy-start.8 = (f32[2,128,256]{2,1,0:T(8,128)S(1)}, f32[2,128,256]{2,1,0:T(8,128)}, u32[]{:S(2)}) copy-start(f32[2,128,256]{2,1,0:T(8,128)} %constant.46.clone.refs_11_.refs_10_) | copy-start | bytes 786436
  19.5 10.5 %copy-start.9 = (f32[2,1,128]{2,1,0:T(1,128)S(1)}, f32[2,1,128]{2,1,0:T(1,128)}, u32[]{:S(2)}) copy-start(f32[2,1,128]{2,1,0:T(1,128)} %constant.45.clone.refs_10_.refs_9_) | copy-start | bytes 3076
  20.1 9.8 %collective-permute-start.3 = (f32[2,2,128,128]{3,2,1,0:T(8,128)S(1)}, f32[2,2,128,128]{3,2,1,0:T(8,128)S(1)}, u32[]{:S(2)}, u32[]{:S(2)}) collective-permute-start(f32[2,2,128,128]{3,2,1,0:T(8,128)S(1)} %get-tuple-element.49), channel_id=1, source_target_pairs={{1,2},{2,1},{3,4},{4,3},{5,6},{6,5},{7,8},{8,7},{9,10},{10,9},{11,... | collective-permute-start | bytes 786440 | tf_op jit(solution)/shard_map/ppermute | solution.py:441
  38.2 12.6 %collective-permute-start.6 = (f32[2,512,128]{2,1,0:T(8,128)S(1)}, f32[2,512,128]{2,1,0:T(8,128)S(1)}, u32[]{:S(2)}, u32[]{:S(2)}) collective-permute-start(f32[2,512,128]{2,1,0:T(8,128)S(1)} %get-tuple-element.60), channel_id=1, source_target_pairs={{1,2},{2,1},{3,4},{4,3},{5,6},{6,5},{7,8},{8,7},{9,10},{10,9},{11,... | collective-permute-start | bytes 1572872 | tf_op jit(solution)/shard_map/ppermute | solution.py:441
  51.5 11.9 %collective-permute-start.7 = (f32[2,256,128]{2,1,0:T(8,128)S(1)}, f32[2,256,128]{2,1,0:T(8,128)S(1)}, u32[]{:S(2)}, u32[]{:S(2)}) collective-permute-start(f32[2,256,128]{2,1,0:T(8,128)S(1)} %get-tuple-element.62), channel_id=1, source_target_pairs={{0,16},{16,0},{32,48},{48,32},{64,80},{80,64},{96,112},{112,96},{1... | collective-permute-start | bytes 786440 | tf_op jit(solution)/shard_map/ppermute | solution.py:441
  55.0 13.5 %collective-permute-start.8 = (f32[2,256,128]{2,1,0:T(8,128)S(1)}, f32[2,256,128]{2,1,0:T(8,128)S(1)}, u32[]{:S(2)}, u32[]{:S(2)}) collective-permute-start(f32[2,256,128]{2,1,0:T(8,128)S(1)} %get-tuple-element.63), channel_id=1, source_target_pairs={{16,32},{32,16},{48,64},{64,48},{80,96},{96,80},{17,33},{33,17},{4... | collective-permute-start | bytes 786440 | tf_op jit(solution)/shard_map/ppermute | solution.py:441
  56.9 16.0 %collective-permute-start.5 = (f32[2,256,128]{2,1,0:T(8,128)S(1)}, f32[2,256,128]{2,1,0:T(8,128)S(1)}, u32[]{:S(2)}, u32[]{:S(2)}) collective-permute-start(f32[2,256,128]{2,1,0:T(8,128)S(1)} %get-tuple-element.56), channel_id=1, source_target_pairs={{16,32},{32,16},{48,64},{64,48},{80,96},{96,80},{17,33},{33,17},{4... | collective-permute-start | bytes 786440 | tf_op jit(solution)/shard_map/ppermute | solution.py:441
  63.2 11.8 %collective-permute-start.4 = (f32[2,256,128]{2,1,0:T(8,128)S(1)}, f32[2,256,128]{2,1,0:T(8,128)S(1)}, u32[]{:S(2)}, u32[]{:S(2)}) collective-permute-start(f32[2,256,128]{2,1,0:T(8,128)S(1)} %get-tuple-element.55.earlier), channel_id=1, source_target_pairs={{0,16},{16,0},{32,48},{48,32},{64,80},{80,64},{96,112},{112,96},{1... | collective-permute-start | bytes 786440 | tf_op jit(solution)/shard_map/ppermute | solution.py:441
  69.2 14.6 %collective-permute-start.9 = (f32[2,512,128]{2,1,0:T(8,128)S(1)}, f32[2,512,128]{2,1,0:T(8,128)S(1)}, u32[]{:S(2)}, u32[]{:S(2)}) collective-permute-start(f32[2,512,128]{2,1,0:T(8,128)S(1)} %shard_map.116.ext_b), channel_id=1, source_target_pairs={{1,2},{2,1},{3,4},{4,3},{5,6},{6,5},{7,8},{8,7},{9,10},{10,9},{11,... | collective-permute-start | bytes 1572872 | tf_op jit(solution)/shard_map/ppermute | solution.py:441
  92.0 12.6 %collective-permute-start.10 = (f32[2,512,128]{2,1,0:T(8,128)S(1)}, f32[2,512,128]{2,1,0:T(8,128)S(1)}, u32[]{:S(2)}, u32[]{:S(2)}) collective-permute-start(f32[2,512,128]{2,1,0:T(8,128)S(1)} %get-tuple-element.69), channel_id=1, source_target_pairs={{1,2},{2,1},{3,4},{4,3},{5,6},{6,5},{7,8},{8,7},{9,10},{10,9},{11,... | collective-permute-start | bytes 1572872 | tf_op jit(solution)/shard_map/ppermute | solution.py:441
  98.9 12.6 %collective-permute-start.12 = (f32[2,128,128]{2,1,0:T(8,128)S(1)}, f32[2,128,128]{2,1,0:T(8,128)S(1)}, u32[]{:S(2)}, u32[]{:S(2)}) collective-permute-start(f32[2,128,128]{2,1,0:T(8,128)S(1)} %get-tuple-element.72), channel_id=1, source_target_pairs={{16,32},{32,16},{48,64},{64,48},{80,96},{96,80},{17,33},{33,17},{4... | collective-permute-start | bytes 393224 | tf_op jit(solution)/shard_map/ppermute | solution.py:441
  101.9 9.5 %collective-permute-start.11 = (f32[2,128,128]{2,1,0:T(8,128)S(1)}, f32[2,128,128]{2,1,0:T(8,128)S(1)}, u32[]{:S(2)}, u32[]{:S(2)}) collective-permute-start(f32[2,128,128]{2,1,0:T(8,128)S(1)} %get-tuple-element.70.earlier), channel_id=1, source_target_pairs={{0,16},{16,0},{32,48},{48,32},{64,80},{80,64},{96,112},{112,96},{1... | collective-permute-start | bytes 393224 | tf_op jit(solution)/shard_map/ppermute | solution.py:441
  105.2 7.7 %collective-permute-start.13 = (f32[2,128,128]{2,1,0:T(8,128)S(1)}, f32[2,128,128]{2,1,0:T(8,128)S(1)}, u32[]{:S(2)}, u32[]{:S(2)}) collective-permute-start(f32[2,128,128]{2,1,0:T(8,128)S(1)} %get-tuple-element.73), channel_id=1, source_target_pairs={{0,16},{16,0},{32,48},{48,32},{64,80},{80,64},{96,112},{112,96},{1... | collective-permute-start | bytes 393224 | tf_op jit(solution)/shard_map/ppermute | solution.py:441
  106.2 10.9 %collective-permute-start.14 = (f32[2,128,128]{2,1,0:T(8,128)S(1)}, f32[2,128,128]{2,1,0:T(8,128)S(1)}, u32[]{:S(2)}, u32[]{:S(2)}) collective-permute-start(f32[2,128,128]{2,1,0:T(8,128)S(1)} %get-tuple-element.74), channel_id=1, source_target_pairs={{16,32},{32,16},{48,64},{64,48},{80,96},{96,80},{17,33},{33,17},{4... | collective-permute-start | bytes 393224 | tf_op jit(solution)/shard_map/ppermute | solution.py:441

commit v5 on v4

--- a/solution.py
+++ b/solution.py
@@ -69,22 +69,21 @@
 
 
 def prepare_body(
-    positions, intensity, probe, measured, rolled, held, wave, arrived
+    positions, intensity, probe, measured, rolled, held, arrived
 ):
     slots, size = intensity.shape[0], probe.shape[1]
     half = size // 2
-    copies = [pltpu.make_async_copy(probe, wave, arrived.at[0])]
+    copies = []
     for block in range(2):
         columns = intensity.at[:, :, pl.ds(half * block, half)]
-        copies.append(pltpu.make_async_copy(columns, held.at[block], arrived.at[1 + block]))
+        copies.append(pltpu.make_async_copy(columns, held.at[block], arrived.at[block]))
     for copy in copies:
         copy.start()
-    copies[0].wait()
 
     def turn(slot, carry):
         shift = lax.rem(positions[0, 0, slot, 1], size)
         for part in range(2):
-            rolled[slot, part] = pltpu.roll(wave[part], shift, 1)
+            rolled[slot, part] = pltpu.roll(probe[part], shift, 1)
         return carry
 
     lax.fori_loop(0, slots, turn, 0)
@@ -92,7 +91,7 @@
     target = lax.broadcasted_iota(jnp.int32, (size, size), 1)
     wanted = jnp.where(target < half, 2 * target, 2 * (target - half) + 1)
     moves = jnp.where(source == wanted, 1.0, 0.0).astype(jnp.bfloat16)
-    for copy in copies[1:]:
+    for copy in copies:
         copy.wait()
 
     def reorder(slot, carry):
@@ -119,12 +118,11 @@
     return pl.pallas_call(
         prepare_body,
         out_shape=(shaped(slots, 2, half, size), shaped(slots, 2, size, size)),
-        in_specs=[SMEM, hbm, hbm],
+        in_specs=[SMEM, hbm, VMEM],
         out_specs=(VMEM, VMEM),
         scratch_shapes=[
             pltpu.VMEM((2, slots, size, half), jnp.int32),
-            pltpu.VMEM((2, size, size), jnp.float32),
-            pltpu.SemaphoreType.DMA((3,)),
+            pltpu.SemaphoreType.DMA((2,)),
         ],
         compiler_params=pltpu.CompilerParams(vmem_limit_bytes=16 << 20),
         cost_estimate=pl.CostEstimate(flops=slots * 2**27, bytes_accessed=8 << 20, transcendentals=0),

time: 119 us -> 119 us (level)
  waiting for transfers between devices: 28.6 us -> 23.3 us
  starting transfers between devices: 40.7 us -> 45.2 us
    ppermute x15, waiting for transfers between devices: 28.6 us -> 23.3 us  [swapped(): return lax.ppermute(value, axis, route)]
    ppermute x15, starting transfers between devices: 40.7 us -> 45.2 us  [swapped(): return lax.ppermute(value, axis, route)]
where the time goes in v5:
time: 119 us; the launch traced here: 118 us
  starting transfers between devices  45.2 us (38%)
  Pallas kernels  26.3 us (22%)
  waiting for transfers between devices  23.3 us (20%)
  blocking collectives  17.4 us (15%)
  local copies, waits for them, and re-layouts  4.31 us (4%)
    ppermute x15, starting transfers between devices, swapped(): return lax.ppermute(value, axis, route)  45.2 us
    ppermute x15, waiting for transfers between devices, swapped(): return lax.ppermute(value, axis, route)  23.3 us
    pallas_call x10, Pallas kernels, whole(): pl.pallas_call(body, out_shape=outs, in_specs=[SMEM] * len(scalars) + [VM...  21.5 us
    all_gather x8, blocking collectives, paired(): return lax.all_gather(value, 'cols', axis_index_groups=groups)  17.4 us
    unnamed x21, local copies, waits for them, and re-layouts  4.31 us
    pallas_call x1, Pallas kernels, prepare(): pl.pallas_call(prepare_body, out_shape=(shaped(slots, 2, half, size), sha...  3.43 us
  transfers between devices with their start and end apart: 15, of which 9 were waited for; matrix products, arithmetic and copies ran while one was open for 1% of the time, Pallas kernels for 6%

profile of v5, /device:TPU:10, one launch (start us, length us, event | category | flops | bytes accessed | tf_op | source)
XLA Modules:
  0.0 117.6 jit_solution(2115273825600433032)
XLA Ops:
  1.8 2.2 %collective-permute-start = (f32[2,128,256]{2,1,0:T(8,128)S(1)}, f32[2,128,256]{2,1,0:T(8,128)S(1)}, u32[]{:S(2)}, u32[]{:S(2)}) collective-permute-start(f32[2,128,256]{2,1,0:T(8,128)S(1)} %get-tuple-element.40), channel_id=1, source_target_pairs={{0,16},{16,0},{32,48},{48,32},{64,80},{80,64},{96,112},{112,96},{1... | collective-permute-start | bytes 786440 | tf_op jit(solution)/shard_map/ppermute | solution.py:439
  4.0 3.2 %collective-permute-start.1 = (f32[2,128,256]{2,1,0:T(8,128)S(1)}, f32[2,128,256]{2,1,0:T(8,128)S(1)}, u32[]{:S(2)}, u32[]{:S(2)}) collective-permute-start(f32[2,128,256]{2,1,0:T(8,128)S(1)} %get-tuple-element.41), channel_id=1, source_target_pairs={{16,32},{32,16},{48,64},{64,48},{80,96},{96,80},{17,33},{33,17},{4... | collective-permute-start | bytes 786440 | tf_op jit(solution)/shard_map/ppermute | solution.py:439
  7.2 4.8 %collective-permute-start.2 = (f32[2,256,128]{2,1,0:T(8,128)S(1)}, f32[2,256,128]{2,1,0:T(8,128)S(1)}, u32[]{:S(2)}, u32[]{:S(2)}) collective-permute-start(f32[2,256,128]{2,1,0:T(8,128)S(1)} %get-tuple-element.48), channel_id=1, source_target_pairs={{1,2},{2,1},{3,4},{4,3},{5,6},{6,5},{7,8},{8,7},{9,10},{10,9},{11,... | collective-permute-start | bytes 786440 | tf_op jit(solution)/shard_map/ppermute | solution.py:439
  15.8 3.4 %shard_map.110 = (f32[6,2,128,256]{3,2,1,0:T(8,128)S(1)}, f32[6,2,256,256]{3,2,1,0:T(8,128)S(1)}) custom-call(s32[1,1,6,2]{3,2,1,0:T(8,128)S(1)} %copy.15.positions, s32[6,256,256]{2,1,0:T(8,128)S(1)} %bitcast.21, f32[2,256,256]{2,1,0:T(8,128)S(1)} %copy-done.3), custom_call_target="tpu_custom_call" | custom-call | flops 805306368 | bytes 8388608 | tf_op jit(solution)/shard_map/pallas_call | solution.py:118
  20.0 2.9 %collective-permute-start.3 = (f32[2,2,128,128]{3,2,1,0:T(8,128)S(1)}, f32[2,2,128,128]{3,2,1,0:T(8,128)S(1)}, u32[]{:S(2)}, u32[]{:S(2)}) collective-permute-start(f32[2,2,128,128]{3,2,1,0:T(8,128)S(1)} %get-tuple-element.49), channel_id=1, source_target_pairs={{1,2},{2,1},{3,4},{4,3},{5,6},{6,5},{7,8},{8,7},{9,10},{10,9},{11,... | collective-permute-start | bytes 786440 | tf_op jit(solution)/shard_map/ppermute | solution.py:439
  22.9 2.2 %all-gather = f32[4,256,128]{2,1,0:T(8,128)S(1)} all-gather(f32[2,256,128]{2,1,0:T(8,128)S(1)} %get-tuple-element.46), channel_id=2, replica_groups={{0,1},{2,3},{4,5},{6,7},{8,9},{10,11},{12,13},{14,15},{16,17},{18,19},{..., dimensions={0}, use_global_device_ids=true | all-gather | bytes 786432 | tf_op jit(solution)/shard_map/all_gather | solution.py:444
  25.1 2.2 %all-gather.1 = f32[4,2,128,128]{3,2,1,0:T(8,128)S(1)} all-gather(f32[2,2,128,128]{3,2,1,0:T(8,128)S(1)} %get-tuple-element.47), channel_id=3, replica_groups={{0,1},{2,3},{4,5},{6,7},{8,9},{10,11},{12,13},{14,15},{16,17},{18,19},{..., dimensions={0}, use_global_device_ids=true | all-gather | bytes 786432 | tf_op jit(solution)/shard_map/all_gather | solution.py:444
  27.3 2.6 %collective-permute-done.3.refs_3_ = f32[2,2,128,128]{3,2,1,0:T(8,128)S(1)} collective-permute-done((f32[2,2,128,128]{3,2,1,0:T(8,128)S(1)}, f32[2,2,128,128]{3,2,1,0:T(8,128)S(1)}, u32[]{:S(2)}, u32[]{:S(2)}) %collective-permute-start.3) | collective-permute-done | bytes 262176 | tf_op jit(solution)/shard_map/ppermute | solution.py:439
  29.9 8.2 %shard_map.112 = (f32[512,128]{1,0:T(8,128)S(1)}, f32[512,128]{1,0:T(8,128)S(1)}, f32[2,512,128]{2,1,0:T(8,128)S(1)}, f32[2,512,128]{2,1,0:T(8,128)S(1)}, f32[2,512,128]{2,1,0:T(8,128)S(1)}) custom-call(s32[4]{0:T(128)S(1)} %pad_add_fusion.info, s32[1,1,6,2]{3,2,1,0:T(8,128)S(1)} %copy.15.positions, s32[1,1]{1,0:T(1,128)S(6)} %copy.18.counts, ...), custom_call_target="tpu_custom_call" | custom-call | flops 4831838208 | bytes 8388608 | tf_op jit(solution)/shard_map/pallas_call | solution.py:43
  38.1 2.9 %collective-permute-start.6 = (f32[2,512,128]{2,1,0:T(8,128)S(1)}, f32[2,512,128]{2,1,0:T(8,128)S(1)}, u32[]{:S(2)}, u32[]{:S(2)}) collective-permute-start(f32[2,512,128]{2,1,0:T(8,128)S(1)} %get-tuple-element.60), channel_id=1, source_target_pairs={{1,2},{2,1},{3,4},{4,3},{5,6},{6,5},{7,8},{8,7},{9,10},{10,9},{11,... | collective-permute-start | bytes 1572872 | tf_op jit(solution)/shard_map/ppermute | solution.py:439
  41.0 2.2 %all-gather.2 = f32[1024,128]{1,0:T(8,128)S(1)} all-gather(f32[512,128]{1,0:T(8,128)S(1)} %get-tuple-element.52), channel_id=4, replica_groups={{0,1},{2,3},{4,5},{6,7},{8,9},{10,11},{12,13},{14,15},{16,17},{18,19},{..., dimensions={0}, use_global_device_ids=true | all-gather | bytes 786432 | tf_op jit(solution)/shard_map/all_gather | solution.py:444
  43.2 2.2 %all-gather.3 = f32[1024,128]{1,0:T(8,128)S(1)} all-gather(f32[512,128]{1,0:T(8,128)S(1)} %get-tuple-element.53), channel_id=5, replica_groups={{0,1},{2,3},{4,5},{6,7},{8,9},{10,11},{12,13},{14,15},{16,17},{18,19},{..., dimensions={0}, use_global_device_ids=true | all-gather | bytes 786432 | tf_op jit(solution)/shard_map/all_gather | solution.py:444
  46.0 4.7 %collective-permute-done.6.strip = f32[2,512,128]{2,1,0:T(8,128)S(1)} collective-permute-done((f32[2,512,128]{2,1,0:T(8,128)S(1)}, f32[2,512,128]{2,1,0:T(8,128)S(1)}, u32[]{:S(2)}, u32[]{:S(2)}) %collective-permute-start.6) | collective-permute-done | bytes 524320 | tf_op jit(solution)/shard_map/ppermute | solution.py:439
  52.6 2.8 %collective-permute-start.8 = (f32[2,256,128]{2,1,0:T(8,128)S(1)}, f32[2,256,128]{2,1,0:T(8,128)S(1)}, u32[]{:S(2)}, u32[]{:S(2)}) collective-permute-start(f32[2,256,128]{2,1,0:T(8,128)S(1)} %get-tuple-element.63), channel_id=1, source_target_pairs={{16,32},{32,16},{48,64},{64,48},{80,96},{96,80},{17,33},{33,17},{4... | collective-permute-start | bytes 786440 | tf_op jit(solution)/shard_map/ppermute | solution.py:439
  55.4 5.4 %collective-permute-start.5 = (f32[2,256,128]{2,1,0:T(8,128)S(1)}, f32[2,256,128]{2,1,0:T(8,128)S(1)}, u32[]{:S(2)}, u32[]{:S(2)}) collective-permute-start(f32[2,256,128]{2,1,0:T(8,128)S(1)} %get-tuple-element.56), channel_id=1, source_target_pairs={{16,32},{32,16},{48,64},{64,48},{80,96},{96,80},{17,33},{33,17},{4... | collective-permute-start | bytes 786440 | tf_op jit(solution)/shard_map/ppermute | solution.py:439
  60.8 2.4 %collective-permute-start.4 = (f32[2,256,128]{2,1,0:T(8,128)S(1)}, f32[2,256,128]{2,1,0:T(8,128)S(1)}, u32[]{:S(2)}, u32[]{:S(2)}) collective-permute-start(f32[2,256,128]{2,1,0:T(8,128)S(1)} %get-tuple-element.55.earlier), channel_id=1, source_target_pairs={{0,16},{16,0},{32,48},{48,32},{64,80},{80,64},{96,112},{112,96},{1... | collective-permute-start | bytes 786440 | tf_op jit(solution)/shard_map/ppermute | solution.py:439
  63.3 2.8 %collective-permute-done.8.halo_b = f32[2,256,128]{2,1,0:T(8,128)S(1)} collective-permute-done((f32[2,256,128]{2,1,0:T(8,128)S(1)}, f32[2,256,128]{2,1,0:T(8,128)S(1)}, u32[]{:S(2)}, u32[]{:S(2)}) %collective-permute-start.8) | collective-permute-done | bytes 262176 | tf_op jit(solution)/shard_map/ppermute | solution.py:439
  66.8 2.1 %collective-permute-start.9 = (f32[2,512,128]{2,1,0:T(8,128)S(1)}, f32[2,512,128]{2,1,0:T(8,128)S(1)}, u32[]{:S(2)}, u32[]{:S(2)}) collective-permute-start(f32[2,512,128]{2,1,0:T(8,128)S(1)} %shard_map.116.ext_b), channel_id=1, source_target_pairs={{1,2},{2,1},{3,4},{4,3},{5,6},{6,5},{7,8},{8,7},{9,10},{10,9},{11,... | collective-permute-start | bytes 1572872 | tf_op jit(solution)/shard_map/ppermute | solution.py:439
  68.8 2.9 %collective-permute-done.5.halo_b = f32[2,256,128]{2,1,0:T(8,128)S(1)} collective-permute-done((f32[2,256,128]{2,1,0:T(8,128)S(1)}, f32[2,256,128]{2,1,0:T(8,128)S(1)}, u32[]{:S(2)}, u32[]{:S(2)}) %collective-permute-start.5) | collective-permute-done | bytes 262176 | tf_op jit(solution)/shard_map/ppermute | solution.py:439
  71.7 3.8 %collective-permute-done.4.halo_a = f32[2,256,128]{2,1,0:T(8,128)S(1)} collective-permute-done((f32[2,256,128]{2,1,0:T(8,128)S(1)}, f32[2,256,128]{2,1,0:T(8,128)S(1)}, u32[]{:S(2)}, u32[]{:S(2)}) %collective-permute-start.4) | collective-permute-done | bytes 262176 | tf_op jit(solution)/shard_map/ppermute | solution.py:439
  76.2 2.2 %all-gather.4 = f32[1024,128]{1,0:T(8,128)S(1)} all-gather(f32[512,128]{1,0:T(8,128)S(1)} %get-tuple-element.57.ext_r), channel_id=6, replica_groups={{0,1},{2,3},{4,5},{6,7},{8,9},{10,11},{12,13},{14,15},{16,17},{18,19},{..., dimensions={0}, use_global_device_ids=true | all-gather | bytes 786432 | tf_op jit(solution)/shard_map/all_gather | solution.py:444
  78.4 2.2 %all-gather.5 = f32[1024,128]{1,0:T(8,128)S(1)} all-gather(f32[512,128]{1,0:T(8,128)S(1)} %get-tuple-element.58.ext_i), channel_id=7, replica_groups={{0,1},{2,3},{4,5},{6,7},{8,9},{10,11},{12,13},{14,15},{16,17},{18,19},{..., dimensions={0}, use_global_device_ids=true | all-gather | bytes 786432 | tf_op jit(solution)/shard_map/all_gather | solution.py:444
  81.3 8.2 %shard_map.117 = (f32[512,128]{1,0:T(8,128)S(1)}, f32[512,128]{1,0:T(8,128)S(1)}, f32[2,512,128]{2,1,0:T(8,128)S(1)}, f32[2,512,128]{2,1,0:T(8,128)S(1)}, f32[2,512,128]{2,1,0:T(8,128)S(1)}) custom-call(s32[4]{0:T(128)S(1)} %pad_add_fusion.info, s32[1,1,6,2]{3,2,1,0:T(8,128)S(1)} %copy.15.positions, s32[1,1]{1,0:T(1,128)S(6)} %copy.18.counts, ...), custom_call_target="tpu_custom_call" | custom-call | flops 4831838208 | bytes 8388608 | tf_op jit(solution)/shard_map/pallas_call | solution.py:43
  89.5 3.4 %collective-permute-start.10 = (f32[2,512,128]{2,1,0:T(8,128)S(1)}, f32[2,512,128]{2,1,0:T(8,128)S(1)}, u32[]{:S(2)}, u32[]{:S(2)}) collective-permute-start(f32[2,512,128]{2,1,0:T(8,128)S(1)} %get-tuple-element.69), channel_id=1, source_target_pairs={{1,2},{2,1},{3,4},{4,3},{5,6},{6,5},{7,8},{8,7},{9,10},{10,9},{11,... | collective-permute-start | bytes 1572872 | tf_op jit(solution)/shard_map/ppermute | solution.py:439
  92.9 2.2 %all-gather.6 = f32[1024,128]{1,0:T(8,128)S(1)} all-gather(f32[512,128]{1,0:T(8,128)S(1)} %get-tuple-element.65), channel_id=8, replica_groups={{0,1},{2,3},{4,5},{6,7},{8,9},{10,11},{12,13},{14,15},{16,17},{18,19},{..., dimensions={0}, use_global_device_ids=true | all-gather | bytes 786432 | tf_op jit(solution)/shard_map/all_gather | solution.py:444
  95.1 2.2 %all-gather.7 = f32[1024,128]{1,0:T(8,128)S(1)} all-gather(f32[512,128]{1,0:T(8,128)S(1)} %get-tuple-element.66), channel_id=9, replica_groups={{0,1},{2,3},{4,5},{6,7},{8,9},{10,11},{12,13},{14,15},{16,17},{18,19},{..., dimensions={0}, use_global_device_ids=true | all-gather | bytes 786432 | tf_op jit(solution)/shard_map/all_gather | solution.py:444
  97.9 1.9 %collective-permute-start.12 = (f32[2,128,128]{2,1,0:T(8,128)S(1)}, f32[2,128,128]{2,1,0:T(8,128)S(1)}, u32[]{:S(2)}, u32[]{:S(2)}) collective-permute-start(f32[2,128,128]{2,1,0:T(8,128)S(1)} %get-tuple-element.72), channel_id=1, source_target_pairs={{16,32},{32,16},{48,64},{64,48},{80,96},{96,80},{17,33},{33,17},{4... | collective-permute-start | bytes 393224 | tf_op jit(solution)/shard_map/ppermute | solution.py:439
  99.8 5.0 %collective-permute-start.11 = (f32[2,128,128]{2,1,0:T(8,128)S(1)}, f32[2,128,128]{2,1,0:T(8,128)S(1)}, u32[]{:S(2)}, u32[]{:S(2)}) collective-permute-start(f32[2,128,128]{2,1,0:T(8,128)S(1)} %get-tuple-element.70.earlier), channel_id=1, source_target_pairs={{0,16},{16,0},{32,48},{48,32},{64,80},{80,64},{96,112},{112,96},{1... | collective-permute-start | bytes 393224 | tf_op jit(solution)/shard_map/ppermute | solution.py:439
  105.5 4.9 %collective-permute-start.14 = (f32[2,128,128]{2,1,0:T(8,128)S(1)}, f32[2,128,128]{2,1,0:T(8,128)S(1)}, u32[]{:S(2)}, u32[]{:S(2)}) collective-permute-start(f32[2,128,128]{2,1,0:T(8,128)S(1)} %get-tuple-element.74), channel_id=1, source_target_pairs={{16,32},{32,16},{48,64},{64,48},{80,96},{96,80},{17,33},{33,17},{4... | collective-permute-start | bytes 393224 | tf_op jit(solution)/shard_map/ppermute | solution.py:439
  111.8 2.8 %collective-permute-done.13.far_a = f32[2,128,128]{2,1,0:T(8,128)S(1)} collective-permute-done((f32[2,128,128]{2,1,0:T(8,128)S(1)}, f32[2,128,128]{2,1,0:T(8,128)S(1)}, u32[]{:S(2)}, u32[]{:S(2)}) %collective-permute-start.13) | collective-permute-done | bytes 131104 | tf_op jit(solution)/shard_map/ppermute | solution.py:439
  114.6 1.5 %collective-permute-done.14.far_b = f32[2,128,128]{2,1,0:T(8,128)S(1)} collective-permute-done((f32[2,128,128]{2,1,0:T(8,128)S(1)}, f32[2,128,128]{2,1,0:T(8,128)S(1)}, u32[]{:S(2)}, u32[]{:S(2)}) %collective-permute-start.14) | collective-permute-done | bytes 131104 | tf_op jit(solution)/shard_map/ppermute | solution.py:439
  116.1 1.4 %shard_map.120 = f32[2,256,256]{2,1,0:T(8,128)} custom-call(s32[4]{0:T(128)S(1)} %pad_add_fusion.info, f32[512,128]{1,0:T(8,128)S(1)} %get-tuple-element.57.ext_r, f32[512,128]{1,0:T(8,128)S(1)} %get-tuple-element.58.ext_i, f32[2,512,128]{2,1,0:T(8,128)S(1)} %shard_map.116.ext_b, f32[2,512,128]{2,1,0:T(8,128)S(1)} %get-tuple-element.67.total_a, ...), custom_call_target="tpu_custom_call" | custom-call | flops 1048576 | bytes 4194304 | tf_op jit(solution)/shard_map/pallas_call | solution.py:409
  (40 shorter events, 13.0 us)
Async XLA Ops:
  0.1 1.0 copy-start
  1.7 17.5 %copy-start.1 = (f32[2,256,256]{2,1,0:T(8,128)S(1)}, f32[2,256,256]{2,1,0:T(8,128)}, u32[]{:S(2)}) copy-start(f32[2,256,256]{2,1,0:T(8,128)} %tile.3) | copy-start | bytes 1572868
  1.8 17.5 %collective-permute-start = (f32[2,128,256]{2,1,0:T(8,128)S(1)}, f32[2,128,256]{2,1,0:T(8,128)S(1)}, u32[]{:S(2)}, u32[]{:S(2)}) collective-permute-start(f32[2,128,256]{2,1,0:T(8,128)S(1)} %get-tuple-element.40), channel_id=1, source_target_pairs={{0,16},{16,0},{32,48},{48,32},{64,80},{80,64},{96,112},{112,96},{1... | collective-permute-start | bytes 786440 | tf_op jit(solution)/shard_map/ppermute | solution.py:439
  4.0 15.3 %collective-permute-start.1 = (f32[2,128,256]{2,1,0:T(8,128)S(1)}, f32[2,128,256]{2,1,0:T(8,128)S(1)}, u32[]{:S(2)}, u32[]{:S(2)}) collective-permute-start(f32[2,128,256]{2,1,0:T(8,128)S(1)} %get-tuple-element.41), channel_id=1, source_target_pairs={{16,32},{32,16},{48,64},{64,48},{80,96},{96,80},{17,33},{33,17},{4... | collective-permute-start | bytes 786440 | tf_op jit(solution)/shard_map/ppermute | solution.py:439
  7.2 20.1 %collective-permute-start.2 = (f32[2,256,128]{2,1,0:T(8,128)S(1)}, f32[2,256,128]{2,1,0:T(8,128)S(1)}, u32[]{:S(2)}, u32[]{:S(2)}) collective-permute-start(f32[2,256,128]{2,1,0:T(8,128)S(1)} %get-tuple-element.48), channel_id=1, source_target_pairs={{1,2},{2,1},{3,4},{4,3},{5,6},{6,5},{7,8},{8,7},{9,10},{10,9},{11,... | collective-permute-start | bytes 786440 | tf_op jit(solution)/shard_map/ppermute | solution.py:439
  13.4 1.4 %copy-start.2 = (s32[1,1,6,256,256]{4,3,2,1,0:T(8,128)S(1)}, s32[1,1,6,256,256]{4,3,2,1,0:T(8,128)}, u32[]{:S(2)}) copy-start(s32[1,1,6,256,256]{4,3,2,1,0:T(8,128)} %param.15) | copy-start | bytes 4718596
  14.8 1.0 copy-start.3
  19.3 10.5 %copy-start.4 = (bf16[768,256]{1,0:T(8,128)(2,1)S(1)}, bf16[768,256]{1,0:T(8,128)(2,1)}, u32[]{:S(2)}) copy-start(bf16[768,256]{1,0:T(8,128)(2,1)} %constant.44.clone.refs_9_.refs_8_) | copy-start | bytes 1179652
  19.3 10.5 %copy-start.5 = (bf16[256,768]{1,0:T(8,128)(2,1)S(1)}, bf16[256,768]{1,0:T(8,128)(2,1)}, u32[]{:S(2)}) copy-start(bf16[256,768]{1,0:T(8,128)(2,1)} %constant.43.clone.refs_7_.refs_6_) | copy-start | bytes 1179652
  19.3 10.5 %copy-start.6 = (bf16[256,768]{1,0:T(8,128)(2,1)S(1)}, bf16[256,768]{1,0:T(8,128)(2,1)}, u32[]{:S(2)}) copy-start(bf16[256,768]{1,0:T(8,128)(2,1)} %constant.42.clone.refs_8_.refs_7_) | copy-start | bytes 1179652
  19.3 10.5 %copy-start.7 = (bf16[768,256]{1,0:T(8,128)(2,1)S(1)}, bf16[768,256]{1,0:T(8,128)(2,1)}, u32[]{:S(2)}) copy-start(bf16[768,256]{1,0:T(8,128)(2,1)} %constant.41.clone.refs_6_.refs_5_) | copy-start | bytes 1179652
  19.4 10.5 %copy-start.8 = (f32[2,128,256]{2,1,0:T(8,128)S(1)}, f32[2,128,256]{2,1,0:T(8,128)}, u32[]{:S(2)}) copy-start(f32[2,128,256]{2,1,0:T(8,128)} %constant.46.clone.refs_11_.refs_10_) | copy-start | bytes 786436
  19.4 10.5 %copy-start.9 = (f32[2,1,128]{2,1,0:T(1,128)S(1)}, f32[2,1,128]{2,1,0:T(1,128)}, u32[]{:S(2)}) copy-start(f32[2,1,128]{2,1,0:T(1,128)} %constant.45.clone.refs_10_.refs_9_) | copy-start | bytes 3076
  20.0 9.8 %collective-permute-start.3 = (f32[2,2,128,128]{3,2,1,0:T(8,128)S(1)}, f32[2,2,128,128]{3,2,1,0:T(8,128)S(1)}, u32[]{:S(2)}, u32[]{:S(2)}) collective-permute-start(f32[2,2,128,128]{3,2,1,0:T(8,128)S(1)} %get-tuple-element.49), channel_id=1, source_target_pairs={{1,2},{2,1},{3,4},{4,3},{5,6},{6,5},{7,8},{8,7},{9,10},{10,9},{11,... | collective-permute-start | bytes 786440 | tf_op jit(solution)/shard_map/ppermute | solution.py:439
  38.1 12.6 %collective-permute-start.6 = (f32[2,512,128]{2,1,0:T(8,128)S(1)}, f32[2,512,128]{2,1,0:T(8,128)S(1)}, u32[]{:S(2)}, u32[]{:S(2)}) collective-permute-start(f32[2,512,128]{2,1,0:T(8,128)S(1)} %get-tuple-element.60), channel_id=1, source_target_pairs={{1,2},{2,1},{3,4},{4,3},{5,6},{6,5},{7,8},{8,7},{9,10},{10,9},{11,... | collective-permute-start | bytes 1572872 | tf_op jit(solution)/shard_map/ppermute | solution.py:439
  51.3 11.9 %collective-permute-start.7 = (f32[2,256,128]{2,1,0:T(8,128)S(1)}, f32[2,256,128]{2,1,0:T(8,128)S(1)}, u32[]{:S(2)}, u32[]{:S(2)}) collective-permute-start(f32[2,256,128]{2,1,0:T(8,128)S(1)} %get-tuple-element.62), channel_id=1, source_target_pairs={{0,16},{16,0},{32,48},{48,32},{64,80},{80,64},{96,112},{112,96},{1... | collective-permute-start | bytes 786440 | tf_op jit(solution)/shard_map/ppermute | solution.py:439
  52.6 13.5 %collective-permute-start.8 = (f32[2,256,128]{2,1,0:T(8,128)S(1)}, f32[2,256,128]{2,1,0:T(8,128)S(1)}, u32[]{:S(2)}, u32[]{:S(2)}) collective-permute-start(f32[2,256,128]{2,1,0:T(8,128)S(1)} %get-tuple-element.63), channel_id=1, source_target_pairs={{16,32},{32,16},{48,64},{64,48},{80,96},{96,80},{17,33},{33,17},{4... | collective-permute-start | bytes 786440 | tf_op jit(solution)/shard_map/ppermute | solution.py:439
  55.4 16.3 %collective-permute-start.5 = (f32[2,256,128]{2,1,0:T(8,128)S(1)}, f32[2,256,128]{2,1,0:T(8,128)S(1)}, u32[]{:S(2)}, u32[]{:S(2)}) collective-permute-start(f32[2,256,128]{2,1,0:T(8,128)S(1)} %get-tuple-element.56), channel_id=1, source_target_pairs={{16,32},{32,16},{48,64},{64,48},{80,96},{96,80},{17,33},{33,17},{4... | collective-permute-start | bytes 786440 | tf_op jit(solution)/shard_map/ppermute | solution.py:439
  60.8 14.7 %collective-permute-start.4 = (f32[2,256,128]{2,1,0:T(8,128)S(1)}, f32[2,256,128]{2,1,0:T(8,128)S(1)}, u32[]{:S(2)}, u32[]{:S(2)}) collective-permute-start(f32[2,256,128]{2,1,0:T(8,128)S(1)} %get-tuple-element.55.earlier), channel_id=1, source_target_pairs={{0,16},{16,0},{32,48},{48,32},{64,80},{80,64},{96,112},{112,96},{1... | collective-permute-start | bytes 786440 | tf_op jit(solution)/shard_map/ppermute | solution.py:439
  66.8 14.6 %collective-permute-start.9 = (f32[2,512,128]{2,1,0:T(8,128)S(1)}, f32[2,512,128]{2,1,0:T(8,128)S(1)}, u32[]{:S(2)}, u32[]{:S(2)}) collective-permute-start(f32[2,512,128]{2,1,0:T(8,128)S(1)} %shard_map.116.ext_b), channel_id=1, source_target_pairs={{1,2},{2,1},{3,4},{4,3},{5,6},{6,5},{7,8},{8,7},{9,10},{10,9},{11,... | collective-permute-start | bytes 1572872 | tf_op jit(solution)/shard_map/ppermute | solution.py:439
  89.5 15.3 %collective-permute-start.10 = (f32[2,512,128]{2,1,0:T(8,128)S(1)}, f32[2,512,128]{2,1,0:T(8,128)S(1)}, u32[]{:S(2)}, u32[]{:S(2)}) collective-permute-start(f32[2,512,128]{2,1,0:T(8,128)S(1)} %get-tuple-element.69), channel_id=1, source_target_pairs={{1,2},{2,1},{3,4},{4,3},{5,6},{6,5},{7,8},{8,7},{9,10},{10,9},{11,... | collective-permute-start | bytes 1572872 | tf_op jit(solution)/shard_map/ppermute | solution.py:439
  97.9 12.6 %collective-permute-start.12 = (f32[2,128,128]{2,1,0:T(8,128)S(1)}, f32[2,128,128]{2,1,0:T(8,128)S(1)}, u32[]{:S(2)}, u32[]{:S(2)}) collective-permute-start(f32[2,128,128]{2,1,0:T(8,128)S(1)} %get-tuple-element.72), channel_id=1, source_target_pairs={{16,32},{32,16},{48,64},{64,48},{80,96},{96,80},{17,33},{33,17},{4... | collective-permute-start | bytes 393224 | tf_op jit(solution)/shard_map/ppermute | solution.py:439
  99.8 12.0 %collective-permute-start.11 = (f32[2,128,128]{2,1,0:T(8,128)S(1)}, f32[2,128,128]{2,1,0:T(8,128)S(1)}, u32[]{:S(2)}, u32[]{:S(2)}) collective-permute-start(f32[2,128,128]{2,1,0:T(8,128)S(1)} %get-tuple-element.70.earlier), channel_id=1, source_target_pairs={{0,16},{16,0},{32,48},{48,32},{64,80},{80,64},{96,112},{112,96},{1... | collective-permute-start | bytes 393224 | tf_op jit(solution)/shard_map/ppermute | solution.py:439
  105.4 9.2 %collective-permute-start.13 = (f32[2,128,128]{2,1,0:T(8,128)S(1)}, f32[2,128,128]{2,1,0:T(8,128)S(1)}, u32[]{:S(2)}, u32[]{:S(2)}) collective-permute-start(f32[2,128,128]{2,1,0:T(8,128)S(1)} %get-tuple-element.73), channel_id=1, source_target_pairs={{0,16},{16,0},{32,48},{48,32},{64,80},{80,64},{96,112},{112,96},{1... | collective-permute-start | bytes 393224 | tf_op jit(solution)/shard_map/ppermute | solution.py:439
  105.5 10.6 %collective-permute-start.14 = (f32[2,128,128]{2,1,0:T(8,128)S(1)}, f32[2,128,128]{2,1,0:T(8,128)S(1)}, u32[]{:S(2)}, u32[]{:S(2)}) collective-permute-start(f32[2,128,128]{2,1,0:T(8,128)S(1)} %get-tuple-element.74), channel_id=1, source_target_pairs={{16,32},{32,16},{48,64},{64,48},{80,96},{96,80},{17,33},{33,17},{4... | collective-permute-start | bytes 393224 | tf_op jit(solution)/shard_map/ppermute | solution.py:439
